TPU v7x, 32 devices: a whole 2x2x4 slice. The times are simulated.
32 devices in a mesh: gx: 4 (over y, x), gz: 8 (over z, core).
Axes of the slice: x: 2, y: 2, z: 4, core: 2. Of those that a mesh axis runs over, the one named last changes fastest.
Arguments:
- constituent_mass: float32 [5, 4, 64, 512], P(None, None, 'gz', 'gx'), may hold values from 0.05 to 0.5
- flow_speeds: float32 [3, 4, 64, 512], P(None, None, 'gz', 'gx'), may hold values from -3 to 4
- thermal_pair: float32 [2, 4, 64, 512], P(None, None, 'gz', 'gx'), may hold values from 0.005 to 0.05
- blowing_indicator: int32 [64, 512], P('gz', 'gx'), may hold values 0 or 1
Outputs:
- tendency: float32 [10, 4, 64, 512], P(None, None, 'gz', 'gx')
- coefficients: float32 [3, 4, 512], P(None, None, 'gx')
All inputs are finite; a program needn't handle non-finite values. No bound on the sum of `blowing_indicator` on one device may be relied on, other than what follows from the above.
Results may differ from a plain program's by a relative error of at most 0.000029.
Values sent between devices are 32-bit elements; how exact they have to be, the bound alone decides.
No kernel may reach another device: no remote copies, remote signals or barrier semaphores. Data moves between devices by JAX's collectives and lax.ppermute only.
A program may use at most 64 MiB of HBM per device.

v0:
```python
import jax
import jax.numpy as jnp
from jax import lax
from jax.sharding import PartitionSpec as P

NSP = 5


SPECIFIC_HEAT = 2.5
SPECIFIC_HEAT_P = 3.5
HEAT_RATIO = 1.4
STEP_STREAM = 1.0
STEP_NORMAL = 0.5
STEP_SPAN = 1.0
FILTER_SQUARE = 0.5 ** (2.0 / 3.0)
TEST_SQUARE = 2.0 ** (2.0 / 3.0)
FORMATION = (0.0, 0.0, 0.1, 0.5, 0.25)
BLOWING = 0.3
RELAX_TIME = 0.5
SMOOTH_FLOOR = 0.01
RATIO_EPSILON = 1e-06


def padded_2(block, sides, width, periodic):
    for axis, dim in sides:
        count = lax.axis_size(axis)
        forward = [(i, i + 1) for i in range(count - 1)]
        if periodic:
            forward.append((count - 1, 0))
        backward = [(target, source) for source, target in forward]
        low = lax.ppermute(
            lax.slice_in_dim(block, block.shape[dim] - width, None, axis=dim), axis, forward
        )
        high = lax.ppermute(lax.slice_in_dim(block, 0, width, axis=dim), axis, backward)
        block = jnp.concatenate([low, block, high], axis=dim)
    return block


def shrink(values, margin):
    return values[..., margin:-margin, margin:-margin]


def window(values, offset, length, dimension):
    return lax.slice_in_dim(values, offset, offset + length, axis=values.ndim + dimension)


def cell_state(flow_variables):
    partial_value = flow_variables[:NSP]
    density = jnp.sum(partial_value, axis=0)
    motion = flow_variables[NSP : NSP + 3]
    thermal = flow_variables[NSP + 3]
    vibration = flow_variables[NSP + 4]
    return (partial_value, density, motion, thermal, vibration)


def conserved_fluxes(flow_variables, component):
    partial_value, density, motion, thermal, vibration = cell_state(flow_variables)
    pressure = density * thermal
    formation_energy = sum((FORMATION[s] * partial_value[s] for s in range(NSP)))
    energy = (
        density * (SPECIFIC_HEAT * thermal + vibration + 0.5 * jnp.sum(motion * motion, axis=0))
        + formation_energy
    )
    momentum = density[None] * motion
    conserved = jnp.concatenate(
        [partial_value, momentum, energy[None], (density * vibration)[None]], axis=0
    )
    speed_along = motion[component]
    direction = jnp.array(
        [1.0 if k == component else 0.0 for k in range(3)], dtype=flow_variables.dtype
    )
    direction = direction.reshape((3,) + (1,) * (flow_variables.ndim - 1))
    fluxes = jnp.concatenate(
        [
            partial_value * speed_along,
            momentum * speed_along + direction * pressure,
            ((energy + pressure) * speed_along)[None],
            (density * vibration * speed_along)[None],
        ],
        axis=0,
    )
    signal = jnp.abs(speed_along) + jnp.sqrt(HEAT_RATIO * thermal)
    return (conserved, fluxes, signal)


def upwind_blend(stencil):
    guesses = (
        (2.0 * stencil[0] - 7.0 * stencil[1] + 11.0 * stencil[2]) / 6.0,
        (-stencil[1] + 5.0 * stencil[2] + 2.0 * stencil[3]) / 6.0,
        (2.0 * stencil[2] + 5.0 * stencil[3] - stencil[4]) / 6.0,
    )
    roughness = (
        13.0 / 12.0 * (stencil[0] - 2.0 * stencil[1] + stencil[2]) ** 2
        + 0.25 * (stencil[0] - 4.0 * stencil[1] + 3.0 * stencil[2]) ** 2,
        13.0 / 12.0 * (stencil[1] - 2.0 * stencil[2] + stencil[3]) ** 2
        + 0.25 * (stencil[1] - stencil[3]) ** 2,
        13.0 / 12.0 * (stencil[2] - 2.0 * stencil[3] + stencil[4]) ** 2
        + 0.25 * (3.0 * stencil[2] - 4.0 * stencil[3] + stencil[4]) ** 2,
    )
    weights = [
        linear_weight / (SMOOTH_FLOOR + smooth) ** 2
        for linear_weight, smooth in zip((0.1, 0.6, 0.3), roughness)
    ]
    return (weights[0] * guesses[0] + weights[1] * guesses[1] + weights[2] * guesses[2]) / (
        weights[0] + weights[1] + weights[2]
    )


def upwind_faces(flow_variables, component, dimension):
    conserved, fluxes, signal = conserved_fluxes(flow_variables, component)
    face_count = flow_variables.shape[dimension] - 5
    face_signal = jnp.maximum(
        window(signal, 2, face_count, dimension), window(signal, 3, face_count, dimension)
    )
    plus_side = [
        0.5
        * (
            window(fluxes, o, face_count, dimension)
            + face_signal * window(conserved, o, face_count, dimension)
        )
        for o in range(5)
    ]
    minus_side = [
        0.5
        * (
            window(fluxes, o, face_count, dimension)
            - face_signal * window(conserved, o, face_count, dimension)
        )
        for o in range(1, 6)
    ]
    return upwind_blend(plus_side) + upwind_blend(minus_side[::-1])


def normal_slope(values):
    bottom_slope = (values[..., 1:2, :, :] - values[..., 0:1, :, :]) / STEP_NORMAL
    middle = (values[..., 2:, :, :] - values[..., :-2, :, :]) / (2.0 * STEP_NORMAL)
    top_slope = (values[..., -1:, :, :] - values[..., -2:-1, :, :]) / STEP_NORMAL
    return jnp.concatenate([bottom_slope, middle, top_slope], axis=-3)


def gradient(values):
    stream_slope = (values[..., 1:-1, 2:] - values[..., 1:-1, :-2]) / (2.0 * STEP_STREAM)
    span_slope = (values[..., 2:, 1:-1] - values[..., :-2, 1:-1]) / (2.0 * STEP_SPAN)
    normal_part = normal_slope(values[..., 1:-1, 1:-1])
    return jnp.stack([stream_slope, normal_part, span_slope])


def strain_parts(gradients):
    strain = 0.5 * (gradients + jnp.swapaxes(gradients, 0, 1))
    third_trace = (strain[0, 0] + strain[1, 1] + strain[2, 2]) / 3.0
    identity = jnp.eye(3, dtype=gradients.dtype).reshape((3, 3) + (1,) * (gradients.ndim - 2))
    deviator = strain - identity * third_trace
    magnitude = jnp.sqrt(2.0 * jnp.sum(deviator * deviator, axis=(0, 1)) + 1e-06)
    return (deviator, magnitude)


def test_filter(values):
    stream_pass = 0.25 * values[..., :-2] + 0.5 * values[..., 1:-1] + 0.25 * values[..., 2:]
    return (
        0.25 * stream_pass[..., :-2, :]
        + 0.5 * stream_pass[..., 1:-1, :]
        + 0.25 * stream_pass[..., 2:, :]
    )


def germano_sums(padded_block, margin):
    partial_value, density, motion, thermal, vibration = cell_state(padded_block)
    fraction = partial_value / density
    deviator, magnitude = strain_parts(gradient(motion))
    density_in = shrink(density, 1)
    motion_in = shrink(motion, 1)
    thermal_in = shrink(thermal, 1)
    eddy_scale = FILTER_SQUARE * density_in * magnitude
    thermal_grad = gradient(thermal)
    fraction_grad = gradient(fraction)
    momentum_in = density_in * motion_in
    hat_density = test_filter(density_in)
    hat_momentum = test_filter(momentum_in)
    hat_product = test_filter(momentum_in[:, None] * motion_in[None])
    hat_stress = test_filter(eddy_scale * deviator)
    hat_thermal = test_filter(density_in * thermal_in)
    hat_thermal_flux = test_filter(momentum_in * thermal_in)
    hat_thermal_grad = test_filter(eddy_scale * thermal_grad)
    hat_partial = test_filter(shrink(partial_value, 1))
    hat_partial_flux = test_filter(momentum_in[:, None] * shrink(fraction, 1)[None])
    hat_partial_grad = test_filter(eddy_scale * fraction_grad)
    favre_motion = hat_momentum / hat_density
    favre_thermal = hat_thermal / hat_density
    favre_fraction = hat_partial / hat_density
    test_deviator, test_magnitude = strain_parts(gradient(favre_motion))
    test_density = shrink(hat_density, 1)
    test_eddy = TEST_SQUARE * test_density * test_magnitude
    outer_momentum = shrink(hat_momentum, 1)
    leonard = shrink(hat_product, 1) - outer_momentum[:, None] * outer_momentum[None] / test_density
    modelled_terms = 2.0 * (shrink(hat_stress, 1) - test_eddy * test_deviator)
    leonard_thermal = (
        shrink(hat_thermal_flux, 1) - outer_momentum * shrink(hat_thermal, 1) / test_density
    )
    modelled_thermal = shrink(hat_thermal_grad, 1) - test_eddy * gradient(favre_thermal)
    leonard_partial = (
        shrink(hat_partial_flux, 1)
        - outer_momentum[:, None] * shrink(hat_partial, 1)[None] / test_density
    )
    modelled_partial = shrink(hat_partial_grad, 1) - test_eddy * gradient(favre_fraction)
    contract = [
        jnp.sum(leonard * modelled_terms, axis=(0, 1)),
        jnp.sum(modelled_terms * modelled_terms, axis=(0, 1)),
        jnp.sum(leonard_thermal * modelled_thermal, axis=0),
        jnp.sum(modelled_thermal * modelled_thermal, axis=0),
        jnp.sum(leonard_partial * modelled_partial, axis=(0, 1)),
        jnp.sum(modelled_partial * modelled_partial, axis=(0, 1)),
    ]
    totals = jnp.stack([jnp.sum(contracted, axis=-2) for contracted in contract])
    grid_rim = margin - 2
    grid_fields = (
        shrink(motion_in, grid_rim),
        shrink(deviator, grid_rim),
        shrink(eddy_scale, grid_rim),
        shrink(thermal_grad, grid_rim),
        shrink(gradient(vibration), grid_rim),
        shrink(fraction_grad, grid_rim),
    )
    return (totals, grid_fields)


def dynamic_ratio(totals, span_count):
    averages = totals / span_count
    return averages[0::2] / (averages[1::2] + RATIO_EPSILON)


def subgrid_flux(grid_fields, coefficient):
    motion, deviator, eddy_scale, thermal_grad, vibration_grad, fraction_grad = grid_fields
    viscous = coefficient[0][:, None, :] * eddy_scale
    conduct = coefficient[1][:, None, :] * eddy_scale
    diffuse = coefficient[2][:, None, :] * eddy_scale
    stress = -2.0 * viscous * deviator
    heat_flux = -SPECIFIC_HEAT_P * conduct * thermal_grad
    vibration_flux = -conduct * vibration_grad
    species_flux = -diffuse * fraction_grad
    stress_work = jnp.sum(motion[:, None] * stress, axis=0)
    formation_energy = sum((FORMATION[s] * species_flux[:, s] for s in range(NSP)))
    energy_flux = stress_work + heat_flux + vibration_flux + formation_energy
    return jnp.concatenate(
        [jnp.swapaxes(species_flux, 0, 1), stress, energy_flux[None], vibration_flux[None]], axis=0
    )


def normal_faces(flow_variables, subgrid, wall_mask):
    conserved, fluxes, signal = conserved_fluxes(flow_variables, 1)
    face_signal = jnp.maximum(signal[:-1], signal[1:])
    inside = (
        0.5 * (fluxes[:, :-1] + fluxes[:, 1:])
        - 0.5 * face_signal * (conserved[:, 1:] - conserved[:, :-1])
        + 0.5 * (subgrid[:, :-1] + subgrid[:, 1:])
    )
    top_flux = fluxes[:, -1:] + subgrid[:, -1:]
    partial_value, density, motion, thermal, vibration = cell_state(flow_variables[:, 0])
    fraction = partial_value / density
    inflow = BLOWING * wall_mask.astype(density.dtype)
    lift_speed = inflow / density
    nothing = jnp.zeros_like(inflow)
    enthalpy = (
        SPECIFIC_HEAT_P * thermal
        + vibration
        + 0.5 * lift_speed * lift_speed
        + sum((FORMATION[s] * fraction[s] for s in range(NSP)))
    )
    wall_flux = jnp.concatenate(
        [
            inflow * fraction,
            jnp.stack(
                [
                    nothing,
                    inflow * lift_speed + density * thermal,
                    nothing,
                    inflow * enthalpy,
                    inflow * vibration,
                ]
            ),
        ],
        axis=0,
    )
    return jnp.concatenate([wall_flux[:, None], inside, top_flux], axis=1)


def tendency_of(padded_block, grid_fields, coefficient, wall_mask):
    subgrid = subgrid_flux(grid_fields, coefficient)
    stream_sub = subgrid[:, 0, :, 1:-1, :]
    span_sub = subgrid[:, 2, :, :, 1:-1]
    normal_sub = subgrid[:, 1, :, 1:-1, 1:-1]
    stream_faces = upwind_faces(padded_block[..., 3:-3, :], 0, -1) + 0.5 * (
        stream_sub[..., :-1] + stream_sub[..., 1:]
    )
    span_faces = upwind_faces(padded_block[..., 3:-3], 2, -2) + 0.5 * (
        span_sub[..., :-1, :] + span_sub[..., 1:, :]
    )
    interior = shrink(padded_block, 3)
    normal_flux = normal_faces(interior, normal_sub, wall_mask)
    change = (
        -(stream_faces[..., 1:] - stream_faces[..., :-1]) / STEP_STREAM
        - (span_faces[..., 1:, :] - span_faces[..., :-1, :]) / STEP_SPAN
        - (normal_flux[:, 1:] - normal_flux[:, :-1]) / STEP_NORMAL
    )
    partial_value, density, motion, thermal, vibration = cell_state(interior)
    relaxation = density * (thermal - vibration) / RELAX_TIME
    return change + jnp.concatenate([jnp.zeros_like(change[:-1]), relaxation[None]], axis=0)


def clamp_ends(padded, margin):
    extent = padded.shape[-1]
    column = lax.broadcasted_iota(jnp.int32, (extent,), 0)
    position = lax.axis_index("gx")
    leading = padded[..., margin : margin + 1]
    trailing = padded[..., extent - margin - 1 : extent - margin]
    padded = jnp.where((column < margin) & (position == 0), leading, padded)
    return jnp.where(
        (column >= extent - margin) & (position == lax.axis_size("gx") - 1), trailing, padded
    )


def body(constituent_mass, flow_speeds, thermal_pair, blowing_indicator):
    flow_variables = jnp.concatenate([constituent_mass, flow_speeds, thermal_pair], axis=0)
    model_rim = 3
    model_block = clamp_ends(
        padded_2(flow_variables, (("gx", 3), ("gz", 2)), model_rim, True), model_rim
    )
    flux_block = clamp_ends(padded_2(flow_variables, (("gx", 3), ("gz", 2)), 3, True), 3)
    totals, grid_fields = germano_sums(model_block, model_rim)
    span_count = flow_variables.shape[2] * lax.axis_size("gz")
    coefficient = dynamic_ratio(lax.psum(totals, "gz"), span_count)
    extended = clamp_ends(padded_2(coefficient, (("gx", 2),), 1, False), 1)
    tendency = tendency_of(flux_block, grid_fields, extended, blowing_indicator)
    return (tendency, coefficient)


def solution(mesh):
    placed = (
        P(None, None, "gz", "gx"),
        P(None, None, "gz", "gx"),
        P(None, None, "gz", "gx"),
        P("gz", "gx"),
    )
    return jax.shard_map(
        body,
        mesh=mesh,
        in_specs=placed,
        out_specs=(P(None, None, "gz", "gx"), P(None, None, "gx")),
        check_vma=False,
    )
```

profile of v0, /device:TPU:0, one launch (start us, length us, event | category | flops | bytes accessed | tf_op | source)
XLA Modules:
  0.0 78.4 jit_solution(1292757808557294554)
XLA Ops:
  0.6 0.9 %constant_dynamic-update-slice_fusion.2 = f32[10,4,8,128]{3,2,1,0:T(8,128)S(1)} fusion(f32[5,4,8,128]{3,2,1,0:T(8,128)} %param.7), kind=kLoop, calls=%fused_computation.330 | loop fusion | bytes 163840
  1.6 0.7 copy-done.3
  2.4 3.9 %collective-permute-start.1 = (f32[10,4,8,3]{3,2,1,0:T(8,128)S(1)}, f32[10,4,8,3]{3,2,1,0:T(8,128)S(1)}, u32[]{:S(2)}, u32[]{:S(2)}) collective-permute-start(f32[10,4,8,3]{3,2,1,0:T(8,128)S(1)} %get-tuple-element.112), channel_id=1, source_target_pairs={{8,0},{16,8},{24,16},{0,24},{9,1},{17,9},{25,17},{1,25},{10,2},{18... | collective-permute-start | bytes 11528 | tf_op jit(solution)/shard_map/ppermute | solution.py:34
  6.4 0.7 copy-done.1
  7.1 3.9 %collective-permute-done.1 = f32[10,4,8,3]{3,2,1,0:T(8,128)S(1)} collective-permute-done((f32[10,4,8,3]{3,2,1,0:T(8,128)S(1)}, f32[10,4,8,3]{3,2,1,0:T(8,128)S(1)}, u32[]{:S(2)}, u32[]{:S(2)}) %collective-permute-start.1) | collective-permute-done | bytes 3872 | tf_op jit(solution)/shard_map/ppermute | solution.py:34
  11.0 3.4 %collective-permute-done = f32[10,4,8,3]{3,2,1,0:T(8,128)S(1)} collective-permute-done((f32[10,4,8,3]{3,2,1,0:T(8,128)S(1)}, f32[10,4,8,3]{3,2,1,0:T(8,128)S(1)}, u32[]{:S(2)}, u32[]{:S(2)}) %collective-permute-start) | collective-permute-done | bytes 3872 | tf_op jit(solution)/shard_map/ppermute | solution.py:31
  14.3 0.2 pad_maximum_fusion.3
  14.6 2.2 %collective-permute-start.3 = (f32[10,4,3,134]{3,2,1,0:T(4,128)S(1)}, f32[10,4,3,134]{3,2,1,0:T(4,128)S(1)}, u32[]{:S(2)}, u32[]{:S(2)}) collective-permute-start(f32[10,4,3,134]{3,2,1,0:T(4,128)S(1)} %get-tuple-element.95), channel_id=1, source_target_pairs={{1,0},{2,1},{3,2},{4,3},{5,4},{6,5},{7,6},{0,7},{9,8},{10,9},{11,1... | collective-permute-start | bytes 192968 | tf_op jit(solution)/shard_map/ppermute | solution.py:34
  16.8 3.5 %collective-permute-done.3 = f32[10,4,3,134]{3,2,1,0:T(4,128)S(1)} collective-permute-done((f32[10,4,3,134]{3,2,1,0:T(4,128)S(1)}, f32[10,4,3,134]{3,2,1,0:T(4,128)S(1)}, u32[]{:S(2)}, u32[]{:S(2)}) %collective-permute-start.3) | collective-permute-done | bytes 64352 | tf_op jit(solution)/shard_map/ppermute | solution.py:34
  20.3 3.0 %collective-permute-done.2 = f32[10,4,3,134]{3,2,1,0:T(4,128)S(1)} collective-permute-done((f32[10,4,3,134]{3,2,1,0:T(4,128)S(1)}, f32[10,4,3,134]{3,2,1,0:T(4,128)S(1)}, u32[]{:S(2)}, u32[]{:S(2)}) %collective-permute-start.2) | collective-permute-done | bytes 64352 | tf_op jit(solution)/shard_map/ppermute | solution.py:31
  23.4 0.3 pad_maximum_fusion.1
  23.7 0.5 slice_reduce_fusion.1
  24.2 0.5 select_select_fusion
  24.8 0.4 fusion.184
  25.2 0.2 fusion.88
  26.1 0.3 broadcast_multiply_fusion.5
  26.4 0.2 fusion.59
  27.4 0.3 fusion.21
  29.6 0.2 multiply_reduce_fusion.1
  30.2 0.2 fusion.51
  30.4 0.2 fusion.49
  30.8 0.4 fusion.6
  31.1 0.2 fusion.182
  31.4 0.4 fusion.4
  31.8 0.2 fusion.183
  32.0 0.2 multiply_reduce_fusion.8
  32.2 0.4 multiply_reduce_fusion.3
  32.8 0.6 fusion.2
  33.4 0.3 fusion.179
  33.7 0.2 pad_maximum_fusion
  33.9 0.6 fusion
  34.5 0.3 fusion.180
  34.8 0.5 multiply_reduce_fusion.2
  35.3 26.6 %psum.7 = f32[6,4,128]{2,1,0:T(4,128)S(1)} all-reduce(f32[6,4,128]{2,1,0:T(4,128)S(1)} %constant_dynamic-update-slice_fusion.3), channel_id=1, replica_groups=mesh['gx'=4,'gz'=8] {'gz'}, use_global_device_ids=true, to_apply=%region_11.12 | all-reduce | flops 3072 | bytes 24576 | tf_op jit(solution)/shard_map/psum | solution.py:330
  62.1 1.3 %collective-permute-start.5 = (f32[3,4,1]{2,1,0:T(4,128)S(1)}, f32[3,4,1]{2,1,0:T(4,128)S(1)}, u32[]{:S(2)}, u32[]{:S(2)}) collective-permute-start(f32[3,4,1]{2,1,0:T(4,128)S(1)} %get-tuple-element.137), channel_id=1, source_target_pairs={{8,0},{16,8},{24,16},{9,1},{17,9},{25,17},{10,2},{18,10},{26,18},{... | collective-permute-start | bytes 152 | tf_op jit(solution)/shard_map/ppermute | solution.py:34
  63.4 4.7 %collective-permute-start.4 = (f32[3,4,1]{2,1,0:T(4,128)S(1)}, f32[3,4,1]{2,1,0:T(4,128)S(1)}, u32[]{:S(2)}, u32[]{:S(2)}) collective-permute-start(f32[3,4,1]{2,1,0:T(4,128)S(1)} %get-tuple-element.138), channel_id=1, source_target_pairs={{0,8},{8,16},{16,24},{1,9},{9,17},{17,25},{2,10},{10,18},{18,26},{... | collective-permute-start | bytes 152 | tf_op jit(solution)/shard_map/ppermute | solution.py:31
  69.1 0.7 copy-done.6
  69.9 0.6 copy-done.5
  70.6 0.6 copy-done.4
  71.8 0.3 slice_multiply_fusion
  72.1 0.2 multiply_reduce_fusion
  72.4 0.2 fusion.42
  72.6 0.7 maximum_bitcast_fusion
  73.3 0.2 maximum_bitcast_fusion.1
  73.5 0.3 fusion.61
  73.8 1.9 %fusion.10 = f32[10,4,9,128]{3,2,1,0:T(8,128)S(1)} fusion(f32[10,4,10,128]{3,2,1,0:T(8,128)S(1)} %maximum_bitcast_fusion, f32[10,4,14,128]{3,2,1,0:T(8,128)S(1)} %pad_maximum_fusion.7, f32[10,4,14,128]{3,2,1,0:T(8,128)S(1)} %pad_maximum_fusion.6, f32[4,9,128]{2,1,0:T(8,128)S(1)} %slice_maximum_fusion), kind=kLoop, calls=%fused_computation.35 | loop fusion | flops 6912000 | bytes 2783232 | tf_op jit(solution)/shard_map/add | solution.py:294
  75.7 1.9 %fusion.14 = f32[10,4,8,129]{3,2,1,0:T(8,128)S(1)} fusion(f32[10,4,8,130]{3,2,1,0:T(8,128)S(1)} %maximum_bitcast_fusion.1, f32[10,4,8,134]{3,2,1,0:T(8,128)S(1)} %pad_maximum_fusion.5, f32[10,4,8,134]{3,2,1,0:T(8,128)S(1)} %pad_maximum_fusion.4, f32[4,8,129]{2,1,0:T(8,128)S(1)} %slice_maximum_fusion.1), kind=kLoop, calls=%fused_computation.47 | loop fusion | flops 6192000 | bytes 2493312 | tf_op jit(solution)/shard_map/add | solution.py:291
  77.6 0.8 %fusion.64 = f32[10,4,8,128]{3,2,1,0:T(8,128)} fusion(f32[10,4,9,128]{3,2,1,0:T(8,128)S(1)} %fusion.10, f32[10,4,8,129]{3,2,1,0:T(8,128)S(1)} %fusion.14, f32[10,1,8,128]{3,2,1,0:T(8,128)S(1)} %slice_add_fusion.7, f32[10,3,8,128]{3,2,1,0:T(8,128)S(1)} %fusion.79, f32[10,1,8,128]{3,2,1,0:T(8,128)S(1)} %bitcast.230, f32[1,4,8,128]{3,2,1,0:T(8,128)S(1)} %get-tuple-element.59), kind=kLoop, calls=%fused_computation.165 | loop fusion | flops 409600 | bytes 1040384 | tf_op jit(solution)/shard_map/add | solution.py:306
  (120 shorter events, 6.1 us)
Async XLA Ops:
  0.6 0.9 %copy-start.2 = (f32[3,4,8,128]{3,2,1,0:T(8,128)S(1)}, f32[3,4,8,128]{3,2,1,0:T(8,128)}, u32[]{:S(2)}) copy-start(f32[3,4,8,128]{3,2,1,0:T(8,128)} %param.8) | copy-start | bytes 147460
  1.5 0.8 copy-start.3
  2.4 8.6 %collective-permute-start.1 = (f32[10,4,8,3]{3,2,1,0:T(8,128)S(1)}, f32[10,4,8,3]{3,2,1,0:T(8,128)S(1)}, u32[]{:S(2)}, u32[]{:S(2)}) collective-permute-start(f32[10,4,8,3]{3,2,1,0:T(8,128)S(1)} %get-tuple-element.112), channel_id=1, source_target_pairs={{8,0},{16,8},{24,16},{0,24},{9,1},{17,9},{25,17},{1,25},{10,2},{18... | collective-permute-start | bytes 11528 | tf_op jit(solution)/shard_map/ppermute | solution.py:34
  6.4 8.0 %collective-permute-start = (f32[10,4,8,3]{3,2,1,0:T(8,128)S(1)}, f32[10,4,8,3]{3,2,1,0:T(8,128)S(1)}, u32[]{:S(2)}, u32[]{:S(2)}) collective-permute-start(f32[10,4,8,3]{3,2,1,0:T(8,128)S(1)} %get-tuple-element.111), channel_id=1, source_target_pairs={{0,8},{8,16},{16,24},{24,0},{1,9},{9,17},{17,25},{25,1},{2,10},{10... | collective-permute-start | bytes 11528 | tf_op jit(solution)/shard_map/ppermute | solution.py:31
  6.4 0.7 copy-start.1
  14.6 5.8 %collective-permute-start.3 = (f32[10,4,3,134]{3,2,1,0:T(4,128)S(1)}, f32[10,4,3,134]{3,2,1,0:T(4,128)S(1)}, u32[]{:S(2)}, u32[]{:S(2)}) collective-permute-start(f32[10,4,3,134]{3,2,1,0:T(4,128)S(1)} %get-tuple-element.95), channel_id=1, source_target_pairs={{1,0},{2,1},{3,2},{4,3},{5,4},{6,5},{7,6},{0,7},{9,8},{10,9},{11,1... | collective-permute-start | bytes 192968 | tf_op jit(solution)/shard_map/ppermute | solution.py:34
  16.8 6.5 %collective-permute-start.2 = (f32[10,4,3,134]{3,2,1,0:T(4,128)S(1)}, f32[10,4,3,134]{3,2,1,0:T(4,128)S(1)}, u32[]{:S(2)}, u32[]{:S(2)}) collective-permute-start(f32[10,4,3,134]{3,2,1,0:T(4,128)S(1)} %get-tuple-element.94), channel_id=1, source_target_pairs={{0,1},{1,2},{2,3},{3,4},{4,5},{5,6},{6,7},{7,0},{8,9},{9,10},{10,1... | collective-permute-start | bytes 192968 | tf_op jit(solution)/shard_map/ppermute | solution.py:31
  61.9 9.7 %copy-start = (f32[3,4,128]{2,1,0:T(4,128)}, f32[3,4,128]{2,1,0:T(4,128)S(1)}, u32[]{:S(2)}) copy-start(f32[3,4,128]{2,1,0:T(4,128)S(1)} %add_divide_fusion) | copy-start | bytes 18436
  62.1 9.5 %collective-permute-start.5 = (f32[3,4,1]{2,1,0:T(4,128)S(1)}, f32[3,4,1]{2,1,0:T(4,128)S(1)}, u32[]{:S(2)}, u32[]{:S(2)}) collective-permute-start(f32[3,4,1]{2,1,0:T(4,128)S(1)} %get-tuple-element.137), channel_id=1, source_target_pairs={{8,0},{16,8},{24,16},{9,1},{17,9},{25,17},{10,2},{18,10},{26,18},{... | collective-permute-start | bytes 152 | tf_op jit(solution)/shard_map/ppermute | solution.py:34
  63.4 8.2 %collective-permute-start.4 = (f32[3,4,1]{2,1,0:T(4,128)S(1)}, f32[3,4,1]{2,1,0:T(4,128)S(1)}, u32[]{:S(2)}, u32[]{:S(2)}) collective-permute-start(f32[3,4,1]{2,1,0:T(4,128)S(1)} %get-tuple-element.138), channel_id=1, source_target_pairs={{0,8},{8,16},{16,24},{1,9},{9,17},{17,25},{2,10},{10,18},{18,26},{... | collective-permute-start | bytes 152 | tf_op jit(solution)/shard_map/ppermute | solution.py:31
  69.1 0.7 copy-start.6
  69.9 0.7 copy-start.5
  70.6 0.7 copy-start.4
where the time goes:
time: 78.7 us; the launch traced here: 78.4 us
  blocking collectives  26.6 us (34%)
  other arithmetic  17.8 us (23%)
  waiting for transfers between devices  13.8 us (18%)
  starting transfers between devices  12.2 us (16%)
  local copies, waits for them, and re-layouts  6.52 us (8%)
  between operations  1.48 us (2%)
    psum x1, blocking collectives, body(): coefficient = dynamic_ratio(lax.psum(totals, 'gz'), span_count)  26.6 us
    ppermute x3, starting transfers between devices, padded_2(): lax.ppermute(lax.slice_in_dim(block, 0, width, axis=dim), axis, backward)  7.47 us
    ppermute x3, waiting for transfers between devices, padded_2(): lax.ppermute(lax.slice_in_dim(block, 0, width, axis=dim), axis, backward)  7.42 us
    ppermute x3, waiting for transfers between devices, padded_2(): lax.ppermute(lax.slice_in_dim(block, block.shape[dim] - width, None, axis...  6.37 us
    ppermute x3, starting transfers between devices, padded_2(): lax.ppermute(lax.slice_in_dim(block, block.shape[dim] - width, None, axis...  4.73 us
    unnamed x23, local copies, waits for them, and re-layouts  4.35 us
    add x10, other arithmetic, test_filter(): 0.25 * values[..., :-2] + 0.5 * values[..., 1:-1] + 0.25 * values[..., 2:]  2.94 us
    add x1, other arithmetic, tendency_of(): upwind_faces(padded_block[..., 3:-3], 2, -2)  1.91 us
  transfers between devices with their start and end apart: 6, of which 4 were waited for; matrix products, arithmetic and copies ran while one was open for 2% of the time, Pallas kernels for 0%

commit v1 on v0

v1 whole, which is shorter than its diff:
```python
import jax
import jax.numpy as jnp
from jax import lax
from jax.experimental import pallas as pl
from jax.experimental.pallas import tpu as pltpu
from jax.sharding import PartitionSpec as P


NSP = 5
NF = 10
ROWS = 4
TILE = 8
LANES = 128
HALO = 3
GROUPS = NF * ROWS
PAIRS = NF // 2
MAIN_ROWS = PAIRS * HALO * TILE
MESSAGE_ROWS = MAIN_ROWS + 2 * TILE

HEAT_RATIO = 1.4
FILTER_SQUARE = 0.5 ** (2.0 / 3.0)
TEST_SQUARE = 2.0 ** (2.0 / 3.0)
FORMATION = (0.0, 0.0, 0.1, 0.5, 0.25)
BLOWING = 0.3
SMOOTH_FLOOR = 0.01
RATIO_EPSILON = 1e-06

VMEM = pl.BlockSpec(memory_space=pltpu.VMEM)
F32 = jnp.float32


def lanes():
    return lax.broadcasted_iota(jnp.int32, (TILE, LANES), 1)


def sublanes():
    return lax.broadcasted_iota(jnp.int32, (TILE, LANES), 0)


def shift_x(tile, step):
    if isinstance(step, int):
        step = step % LANES
        if step == 0:
            return tile
    return pltpu.roll(tile, step, 1)


def shift_s(tile, step):
    return pltpu.roll(tile, step % TILE, 0)


def is_even():
    return (sublanes() & 1) == 0


def level_edges():
    level = sublanes() >> 1
    return level == 0, level == 3


def tile_of(ref, index):
    return ref[pl.ds(index * TILE, TILE), :]


def pack_kernel(mass_ref, speed_ref, heat_ref, own_ref, left_ref, right_ref, up_ref, down_ref):
    lane = lanes()
    even = is_even()
    to_left = jnp.zeros((TILE, LANES), F32)
    to_right = jnp.zeros((TILE, LANES), F32)
    tiles = {}
    for field in range(NF):
        if field < NSP:
            ref, base = mass_ref, field
        elif field < NSP + 3:
            ref, base = speed_ref, field - NSP
        else:
            ref, base = heat_ref, field - NSP - 3
        for zz in range(ROWS):
            group = field * ROWS + zz
            tile = ref[pl.ds(base * 32 + zz, TILE, stride=4), :]
            tiles[field, zz] = tile
            own_ref[pl.ds(group * TILE, TILE), :] = tile
            reached = lane >= 3 * group
            to_left = jnp.where(reached, shift_x(tile, 3 * group), to_left)
            to_right = jnp.where(reached, shift_x(tile, 3 * group + 3), to_right)
        if field % 2:
            pair = field // 2
            for k in range(HALO):
                slot = pl.ds((pair * HALO + k) * TILE, TILE)
                up_ref[slot, :] = jnp.where(
                    even, shift_s(tiles[field - 1, k + 1], -1), tiles[field, k + 1]
                )
                down_ref[slot, :] = jnp.where(
                    even, tiles[field, k], shift_s(tiles[field - 1, k], 1)
                )
    left_ref[...] = to_left
    right_ref[...] = to_right


def edge_kernel(
    position_ref, got_left_ref, got_right_ref, to_left_ref, to_right_ref, up_in, down_in,
    up_ref, down_ref, edge_ref
):
    up_ref[pl.ds(0, MAIN_ROWS), :] = up_in[...]
    down_ref[pl.ds(0, MAIN_ROWS), :] = down_in[...]
    lane = lanes()
    third = lane - 3 * ((lane * 171) >> 9)
    own_left = to_left_ref[...]
    own_right = to_right_ref[...]
    clamp_left = jnp.where(
        third == 0, own_left,
        jnp.where(third == 1, shift_x(own_left, 1), shift_x(own_left, 2)),
    )
    clamp_right = jnp.where(
        third == 2, own_right,
        jnp.where(third == 1, shift_x(own_right, -1), shift_x(own_right, -2)),
    )
    left = jnp.where(position_ref[0] == 1, clamp_left, got_left_ref[...])
    right = jnp.where(position_ref[1] == 1, clamp_right, got_right_ref[...])
    for ref, start in ((up_ref, MAIN_ROWS), (down_ref, MAIN_ROWS), (edge_ref, 0)):
        ref[pl.ds(start, TILE), :] = left
        ref[pl.ds(start + TILE, TILE), :] = right


def row_tile(own_ref, below_ref, above_ref, field, zz):
    if 0 <= zz < ROWS:
        return tile_of(own_ref, field * ROWS + zz)
    pair, second = divmod(field, 2)
    if zz < 0:
        k = zz + ROWS
        halo = tile_of(below_ref, pair * HALO + k - 1)
        if second:
            halo = shift_s(halo, -1)
        return jnp.where(is_even(), halo, shift_s(tile_of(own_ref, field * ROWS + k), 1))
    k = zz - ROWS
    halo = tile_of(above_ref, pair * HALO + k)
    if second:
        halo = shift_s(halo, 1)
    return jnp.where(is_even(), shift_s(tile_of(own_ref, field * ROWS + k), -1), halo)


def halo_packs(edge_ref, below_ref, above_ref):
    even = is_even()
    packs = []
    for side in range(2):
        own = tile_of(edge_ref, side)
        low = below_ref[pl.ds(MAIN_ROWS + side * TILE, TILE), :]
        high = above_ref[pl.ds(MAIN_ROWS + side * TILE, TILE), :]
        packs.append(
            (
                jnp.where(even, shift_s(low, -1), shift_s(own, 1)),
                own,
                jnp.where(even, shift_s(own, -1), shift_s(high, 1)),
            )
        )
    return packs


def spread(left_pack, right_pack, group):
    return jnp.where(
        lanes() < 64,
        shift_x(right_pack, (LANES - 3 * group)),
        shift_x(left_pack, LANES - HALO - 3 * group),
    )


def state_of(fields):
    mass, motion = fields[:NSP], fields[NSP : NSP + 3]
    thermal, vibration = fields[NSP + 3], fields[NSP + 4]
    density = (mass[0] + mass[1]) + (mass[2] + mass[3]) + mass[4]
    formed = FORMATION[2] * mass[2] + FORMATION[3] * mass[3] + FORMATION[4] * mass[4]
    motion_square = motion[0] * motion[0] + motion[1] * motion[1] + motion[2] * motion[2]
    energy = density * (2.5 * thermal + vibration + 0.5 * motion_square) + formed
    conserved = (
        list(mass) + [density * speed for speed in motion] + [energy, density * vibration]
    )
    return density, density * thermal, jnp.sqrt(HEAT_RATIO * thermal), conserved


def flux_of(conserved, pressure, speed, component):
    flux = [value * speed for value in conserved]
    flux[NSP + component] = flux[NSP + component] + pressure
    flux[NSP + 3] = flux[NSP + 3] + pressure * speed
    return flux


def correction(d0, d1, d2, d3):
    floor = 4.0 * SMOOTH_FLOOR * 12.0 / 13.0
    share = 3.0 / 13.0
    e0, e1, e2 = d1 - d0, d2 - d1, d3 - d2
    g0, g1, g2 = e0 + (d1 + d1), d1 + d2, e2 - (d2 + d2)
    b0 = (e0 * e0 + floor) + share * (g0 * g0)
    b1 = (e1 * e1 + floor) + share * (g1 * g1)
    b2 = (e2 * e2 + floor) + share * (g2 * g2)
    p0, p1, p2 = b1 * b2, b0 * b2, b0 * b1
    w0 = p0 * p0
    w1 = 6.0 * (p1 * p1)
    w2 = 3.0 * (p2 * p2)
    r0 = 5.0 * d1 - (d0 + d0)
    r1 = d1 + (d2 + d2)
    r2 = 4.0 * d2 - d3
    return (w0 * r0 + w1 * r1 + w2 * r2) / (w0 + w1 + w2)


def face_flux(here, slopes, jumps, signal):
    waves = [signal * jump for jump in jumps]
    plus = [slopes[k] + waves[k] for k in range(4)]
    minus = [waves[k] - slopes[k] for k in range(1, 5)]
    gain = correction(*plus)
    loss = correction(minus[3], minus[2], minus[1], minus[0])
    return here + 0.5 * (slopes[2] - waves[2]) + (gain + loss) * (1.0 / 12.0)


def stream_kernel(own_ref, edge_ref, blow_ref, out_ref, first_ref, blow_rows):
    lane = lanes()
    bottom, top = level_edges()
    for level in range(4):
        blow_rows[pl.ds(level * TILE, TILE), :] = blow_ref[...].astype(F32)
    left_pack = tile_of(edge_ref, 0)
    right_pack = tile_of(edge_ref, 1)

    fields = []
    for field in range(NF):
        gathered = jnp.zeros((TILE, LANES), F32)
        for zz in range(ROWS):
            group = field * ROWS + zz
            halo = shift_x(left_pack, LANES - 3 - 3 * group)
            tile = jnp.where(lane >= LANES - HALO, halo, tile_of(own_ref, group))
            gathered = jnp.where(lane >= 8 * zz, shift_x(tile, 8 * zz + 3), gathered)
        fields.append(gathered)
    density, pressure, sound, conserved = state_of(fields)
    speed = fields[NSP]
    flux = flux_of(conserved, pressure, speed, 0)
    signal = jnp.abs(speed) + sound
    signal = jnp.maximum(signal, shift_x(signal, -1))
    for field in range(NF):
        slope = shift_x(flux[field], -1) - flux[field]
        jump = shift_x(conserved[field], -1) - conserved[field]
        slopes = [shift_x(slope, -k) for k in range(-2, 3)]
        jumps = [shift_x(jump, -k) for k in range(-2, 3)]
        first_ref[pl.ds(field * TILE, TILE), :] = face_flux(
            flux[field], slopes, jumps, signal
        )

    low = lane < HALO
    high = lane >= LANES - HALO

    def row(zz, carry):
        fields, halos = [], []
        for field in range(NF):
            group = field * ROWS + zz
            start = pl.multiple_of(group * TILE, TILE)
            fields.append(own_ref[pl.ds(start, TILE), :])
            halos.append(
                jnp.where(
                    lane < 64,
                    pltpu.roll(right_pack, (LANES - 3 * group) & (LANES - 1), 1),
                    pltpu.roll(left_pack, LANES - HALO - 3 * group, 1),
                )
            )
        density, pressure, sound, conserved = state_of(fields)
        halo_density, halo_pressure, halo_sound, halo_conserved = state_of(
            [jnp.where(low | high, h, f) for h, f in zip(halos, fields)]
        )
        speed, halo_speed = fields[NSP], jnp.where(low | high, halos[NSP], fields[NSP])
        flux = flux_of(conserved, pressure, speed, 0)
        halo_flux = flux_of(halo_conserved, halo_pressure, halo_speed, 0)
        signal = jnp.abs(speed) + sound
        halo_signal = jnp.abs(halo_speed) + halo_sound
        signal = jnp.maximum(signal, shift_x(jnp.where(lane == 0, halo_signal, signal), -1))

        normal_speed = fields[NSP + 1]
        normal_flux = flux_of(conserved, pressure, normal_speed, 1)
        normal_signal = jnp.abs(normal_speed) + sound
        normal_signal = 0.5 * jnp.maximum(normal_signal, shift_s(normal_signal, -2))
        blown = BLOWING * blow_rows[pl.ds(zz, TILE, stride=4), :]
        lift = blown / density
        enthalpy = 3.5 * fields[NSP + 3] + fields[NSP + 4] + 0.5 * lift * lift
        wall = [lift * fields[s] for s in range(NSP)]
        formed = FORMATION[2] * wall[2] + FORMATION[3] * wall[3] + FORMATION[4] * wall[4]
        zero = jnp.zeros((TILE, LANES), F32)
        wall = wall + [
            zero, blown * lift + pressure, zero, blown * enthalpy + formed, blown * fields[NSP + 4]
        ]

        for field in range(NF):
            def differences(value, halo):
                left, right = jnp.where(high, halo, value), jnp.where(low, halo, value)
                near = shift_x(left, -1) - left
                far = shift_x(right, -1) - right
                here = jnp.where(low, near, far)
                return [
                    shift_x(jnp.where(lane >= LANES - 2, near, here), 2),
                    shift_x(jnp.where(lane >= LANES - 1, near, here), 1),
                    here,
                    shift_x(jnp.where(lane < 1, far, here), -1),
                    shift_x(jnp.where(lane < 2, far, here), -2),
                ]

            slopes = differences(flux[field], halo_flux[field])
            jumps = differences(conserved[field], halo_conserved[field])
            face = face_flux(flux[field], slopes, jumps, signal)
            first = pltpu.roll(
                first_ref[pl.ds(field * TILE, TILE), :], LANES - 2 - 8 * zz, 1
            )
            change = jnp.where(lane == 0, first, shift_x(face, 1)) - face

            value, above = conserved[field], shift_s(conserved[field], -2)
            level_face = 0.5 * (normal_flux[field] + shift_s(normal_flux[field], -2)) - normal_signal * (
                above - value
            )
            level_face = jnp.where(top, normal_flux[field], level_face)
            under = jnp.where(bottom, wall[field], shift_s(level_face, 2))
            change = change + 2.0 * (under - level_face)
            if field == NF - 1:
                change = change + 2.0 * density * (fields[NSP + 3] - fields[NSP + 4])
            start = pl.multiple_of((field * ROWS + zz) * TILE, TILE)
            out_ref[pl.ds(start, TILE), :] = change
        return carry

    lax.fori_loop(0, ROWS, row, 0)


SPAN_TILES = ROWS + 2 * HALO


def span_kernel(own_ref, below_ref, above_ref, part_ref, out_ref, value_ref, flux_ref, signal_ref):
    for zz in range(-HALO, ROWS + HALO):
        fields = [row_tile(own_ref, below_ref, above_ref, field, zz) for field in range(NF)]
        _, pressure, sound, conserved = state_of(fields)
        speed = fields[NSP + 2]
        flux = flux_of(conserved, pressure, speed, 2)
        signal_ref[zz + HALO] = jnp.abs(speed) + sound
        for field in range(NF):
            value_ref[zz + HALO, field] = conserved[field]
            flux_ref[zz + HALO, field] = flux[field]

    def faces_of(place):
        signal = jnp.maximum(signal_ref[place], signal_ref[place + 1])
        faces = []
        for field in range(NF):
            flux = [flux_ref[place + k, field] for k in range(-2, 4)]
            value = [value_ref[place + k, field] for k in range(-2, 4)]
            slopes = [flux[k + 1] - flux[k] for k in range(5)]
            jumps = [value[k + 1] - value[k] for k in range(5)]
            faces.append(face_flux(flux[2], slopes, jumps, signal))
        return tuple(faces)

    def row(zz, before):
        faces = faces_of(zz + HALO)
        for field in range(NF):
            start = pl.multiple_of((field * ROWS + zz) * TILE, TILE)
            out_ref[pl.ds(start, TILE), :] = (
                part_ref[pl.ds(start, TILE), :] + before[field] - faces[field]
            )
        return faces

    lax.fori_loop(0, ROWS, row, faces_of(HALO - 1))


MASS, MOMENTUM, HEAT = 0, 5, 8
SPEED, THERMAL, VIBRATION, FRACTION, DENSITY = 9, 12, 13, 14, 19
STATE_COUNT = 20
SLOPED = 10
STATE_ROWS = 8
GRID_ROWS = 6
PAIR_INDEX = ((0, 0), (1, 1), (0, 1), (0, 2), (1, 2), (2, 2))

PRODUCT, STRESS, HEAT_FLUX, HEAT_SLOPE, MASS_FLUX, MASS_SLOPE = 0, 6, 11, 14, 17, 29
FILTERED = 41

TERMS = 12
TERM_FIELD = (0, 1, 2, 3, 4, 5, 6, 7, 8, 8, 8, 9)
TERM_MODEL = (2, 2, 2, 2, 2, 0, 0, 0, 0, 1, 2, 1)


def model_state(fields):
    mass, motion = fields[:NSP], fields[NSP : NSP + 3]
    thermal, vibration = fields[NSP + 3], fields[NSP + 4]
    density = (mass[0] + mass[1]) + (mass[2] + mass[3]) + mass[4]
    inverse = 1.0 / density
    fraction = [m * inverse for m in mass]
    return (
        list(mass)
        + [density * speed for speed in motion]
        + [density * thermal]
        + list(motion)
        + [thermal, vibration]
        + fraction
        + [density]
    )


def level_slope(value, scale):
    bottom, top = level_edges()
    above = jnp.where(top, value, shift_s(value, -2))
    below = jnp.where(bottom, value, shift_s(value, 2))
    return scale * (above - below)


def strain(slopes):
    diagonal = [2.0 * slopes[k][k] for k in range(3)]
    third = (diagonal[0] + diagonal[1] + diagonal[2]) * (1.0 / 3.0)
    first, second = diagonal[0] - third, diagonal[1] - third
    mixed = [slopes[0][1] + slopes[1][0], slopes[0][2] + slopes[2][0], slopes[1][2] + slopes[2][1]]
    last = diagonal[2] - third
    square = (
        first * first + second * second + last * last
        + 2.0 * (mixed[0] * mixed[0] + mixed[1] * mixed[1] + mixed[2] * mixed[2])
    )
    magnitude = jnp.sqrt(0.125 * square + 1e-06)
    return [first, second] + mixed + [last], magnitude


def grid_terms(here, slopes):
    deviator, magnitude = strain(slopes[:3])
    eddy = FILTER_SQUARE * here(DENSITY) * magnitude
    speed = [here(SPEED + k) for k in range(3)]
    momentum = [here(MOMENTUM + k) for k in range(3)]
    thermal = here(THERMAL)
    stress = [eddy * part for part in deviator]
    tiles = [momentum[i] * speed[j] for i, j in PAIR_INDEX]
    tiles += stress[:5]
    tiles += [m * thermal for m in momentum]
    tiles += [eddy * slopes[3][d] for d in range(3)]
    tiles += [here(MASS + s) * speed[d] for s in range(4) for d in range(3)]
    tiles += [eddy * slopes[5 + s][d] for s in range(4) for d in range(3)]
    vibration = [eddy * slopes[4][d] for d in range(3)]
    return tiles, vibration, stress[5]


def subgrid_terms(tiles, vibration, last_stress, speed, d):
    stress = tiles[STRESS : STRESS + 5] + [last_stress]
    full = ((0, 2, 3), (2, 1, 4), (3, 4, 5))
    tau = [stress[full[i][d]] for i in range(3)]
    species = [tiles[MASS_SLOPE + 3 * s + d] for s in range(4)]
    species.append(-((species[0] + species[1]) + (species[2] + species[3])))
    work = speed[0] * tau[0] + speed[1] * tau[1] + speed[2] * tau[2]
    heat = 3.5 * tiles[HEAT_SLOPE + d] + vibration[d]
    formed = FORMATION[2] * species[2] + FORMATION[3] * species[3] + FORMATION[4] * species[4]
    return species + tau + [work, heat, formed, vibration[d]]


def favre(hat):
    density = (hat[0] + hat[1]) + (hat[2] + hat[3]) + hat[4]
    inverse = 1.0 / density
    return density, [hat[5 + k] * inverse for k in range(3)], hat[8] * inverse, [
        hat[s] * inverse for s in range(4)
    ]


def contractions(hat, density, momentum, favre_here, slopes):
    speed, thermal, fraction = favre_here
    deviator, magnitude = strain(slopes[:3])
    eddy = TEST_SQUARE * density * magnitude
    stress = list(hat[STRESS : STRESS + 5])
    stress.append(-(stress[0] + stress[1]))
    sums = []
    top = bottom = None

    def add(total, value):
        return value if total is None else total + value

    off_top = off_bottom = None
    for n, (i, j) in enumerate(PAIR_INDEX):
        resolved = hat[PRODUCT + n] - momentum[i] * speed[j]
        model = stress[n] - eddy * deviator[n]
        if i == j:
            top, bottom = add(top, resolved * model), add(bottom, model * model)
        else:
            off_top, off_bottom = add(off_top, resolved * model), add(off_bottom, model * model)
    sums += [top + (off_top + off_top), bottom + (off_bottom + off_bottom)]
    top = bottom = None
    for d in range(3):
        resolved = hat[HEAT_FLUX + d] - momentum[d] * thermal
        model = hat[HEAT_SLOPE + d] - eddy * slopes[3][d]
        top, bottom = add(top, resolved * model), add(bottom, model * model)
    sums += [top, bottom]
    top = bottom = None
    for d in range(3):
        last_resolved = last_model = None
        for s in range(4):
            resolved = hat[MASS_FLUX + 3 * s + d] - momentum[d] * fraction[s]
            model = hat[MASS_SLOPE + 3 * s + d] - eddy * slopes[4 + s][d]
            last_resolved, last_model = add(last_resolved, resolved), add(last_model, model)
            top, bottom = add(top, resolved * model), add(bottom, model * model)
        top, bottom = top + last_resolved * last_model, bottom + last_model * last_model
    return sums + [top, bottom]


def filter_x(tile):
    pair = tile + shift_x(tile, -1)
    return pair + shift_x(pair, 1)


def model_kernel(
    own_ref, edge_ref, below_ref, above_ref,
    totals_ref, terms_ref,
    state_ref, halo_ref, corner_ref, tile_ref, extra_ref, wide_ref, favre_ref, sum_ref,
):
    lane = lanes()
    even = is_even()
    bottom, top = level_edges()
    low = lane < HALO
    high = lane >= LANES - HALO
    scale = jnp.where(bottom | top, 4.0, 2.0)
    packs = halo_packs(edge_ref, below_ref, above_ref)

    for field in range(NF):
        corner_ref[field] = jnp.zeros((TILE, LANES), F32)
    for zz in range(-2, 6):
        block, place = (zz + ROWS) // ROWS, zz % ROWS
        rows, halos = [], []
        start = 8 * (zz + 2)
        for field in range(NF):
            group = field * ROWS + place
            row = row_tile(own_ref, below_ref, above_ref, field, zz)
            halo = spread(packs[0][block], packs[1][block], group)
            rows.append(row)
            halos.append(jnp.where(low | high, halo, row))
            left = shift_x(jnp.where(high, halo, row), start + 3)
            right = shift_x(jnp.where(low, halo, row), 64 + start - 123)
            kept = corner_ref[field]
            kept = jnp.where((lane >= start) & (lane < start + 8), left, kept)
            corner_ref[field] = jnp.where(
                (lane >= 64 + start) & (lane < 72 + start), right, kept
            )
        states = model_state(rows)
        for k in range(STATE_COUNT):
            state_ref[zz + 2, k] = states[k]
        if -1 <= zz <= 4:
            halo_states = model_state(halos)
            for k in range(SLOPED):
                halo_ref[zz + 1, k] = halo_states[SPEED + k]

    def grid_row(row, carry):
        def here(k):
            return state_ref[row + 1, k]

        slopes = []
        for k in range(SLOPED - 1):
            value, halo = here(SPEED + k), halo_ref[row, k]
            along_x = shift_x(jnp.where(lane == 0, halo, value), -1) - shift_x(
                jnp.where(lane == LANES - 1, halo, value), 1
            )
            along_z = state_ref[row + 2, SPEED + k] - state_ref[row, SPEED + k]
            slopes.append((along_x, level_slope(value, scale), along_z))
        tiles, vibration, last = grid_terms(here, slopes)
        for k in range(FILTERED):
            tile_ref[row, k] = tiles[k]
        for d in range(3):
            extra_ref[row, d] = vibration[d]
        extra_ref[row, 3] = last
        hat = []
        for k in range(SPEED):
            total = (state_ref[row, k] + state_ref[row + 2, k]) + 2.0 * here(k)
            hat.append(filter_x(total))
        density, speed, thermal, fraction = favre(hat)
        for k, value in enumerate(speed + [thermal] + fraction):
            favre_ref[row, k] = value
        for k in range(3):
            wide_ref[row, k] = hat[MOMENTUM + k]
        wide_ref[row, 3] = density
        return carry

    lax.fori_loop(0, GRID_ROWS, grid_row, 0)

    corner = model_state([corner_ref[field] for field in range(NF)])

    def corner_slopes(value):
        along_x = shift_x(value, -1) - shift_x(value, 1)
        along_z = shift_x(value, -8) - shift_x(value, 8)
        return along_x, level_slope(value, scale), along_z

    def corner_filter(value):
        pair = value + shift_x(value, -8)
        return filter_x(pair + shift_x(pair, 8))

    slopes = [corner_slopes(corner[SPEED + k]) for k in range(SLOPED - 1)]
    corner_tiles, corner_vibration, corner_last = grid_terms(lambda k: corner[k], slopes)
    hat = [corner_filter(corner[k]) for k in range(SPEED)]
    density, speed, thermal, fraction = favre(hat)
    slopes = [corner_slopes(value) for value in speed + [thermal] + fraction]
    corner_sums = contractions(
        [corner_filter(tile) for tile in corner_tiles],
        density, hat[5:8], (speed, thermal, fraction), slopes,
    )
    corner_totals = []
    for value in corner_sums:
        value = value + shift_x(value, -8)
        corner_totals.append(value + shift_x(value, -16))
    corner_x = subgrid_terms(
        corner_tiles, corner_vibration, corner_last, [corner[SPEED + k] for k in range(3)], 0
    )

    for k in range(6):
        sum_ref[k] = jnp.zeros((TILE, LANES), F32)

    def test_row(zz, carry):
        row = zz + 1
        hat = []
        for k in range(FILTERED):
            total = (tile_ref[row - 1, k] + tile_ref[row + 1, k]) + 2.0 * tile_ref[row, k]
            hat.append(filter_x(total))
        slopes = []
        for k in range(8):
            value = favre_ref[row, k]
            along_x = shift_x(value, -1) - shift_x(value, 1)
            along_z = favre_ref[row + 1, k] - favre_ref[row - 1, k]
            slopes.append((along_x, level_slope(value, scale), along_z))
        values = [favre_ref[row, k] for k in range(8)]
        sums = contractions(
            hat, wide_ref[row, 3], [wide_ref[row, k] for k in range(3)],
            (values[:3], values[3], values[4:]), slopes,
        )
        for k in range(6):
            sum_ref[k] = sum_ref[k] + sums[k]
        return carry

    lax.fori_loop(0, ROWS, test_row, 0)

    edges = jnp.zeros((TILE, LANES), F32)
    for k in range(3):
        packed = []
        for main, side in ((sum_ref[2 * k], corner_totals[2 * k]), (sum_ref[2 * k + 1], corner_totals[2 * k + 1])):
            main = jnp.where(lane < 2, shift_x(side, -19), main)
            main = jnp.where(lane >= LANES - 2, shift_x(side, 126 - 83), main)
            packed.append((main + shift_s(main, 1), side + shift_s(side, 1), main, side))
        top_main = shift_s(packed[0][0], -1) * (1.0 / 512.0)
        top_side = shift_s(packed[0][1], -1) * (1.0 / 512.0)
        totals_ref[pl.ds(k * TILE, TILE), :] = jnp.where(even, top_main, packed[1][0] * (1.0 / 1024.0))
        side = jnp.where(even, top_side, packed[1][1] * (1.0 / 1024.0))
        edges = jnp.where(lane == 2 * k, shift_x(side, 2 * k - 18), edges)
        edges = jnp.where(lane == 2 * k + 1, shift_x(side, 2 * k + 1 - 85), edges)
    totals_ref[pl.ds(3 * TILE, TILE), :] = edges

    for n in range(TERMS):
        corner_ref[n] = corner_x[n]

    def term_row(zz, carry):
        row = zz + 1

        def terms(place, d):
            tiles = {k: tile_ref[place, k] for k in range(STRESS, STRESS + 5)}
            tiles.update({HEAT_SLOPE + d: tile_ref[place, HEAT_SLOPE + d]})
            tiles.update(
                {MASS_SLOPE + 3 * s + d: tile_ref[place, MASS_SLOPE + 3 * s + d] for s in range(4)}
            )
            listed = [tiles.get(k) for k in range(FILTERED)]
            speed = [state_ref[place + 1, SPEED + k] for k in range(3)]
            return subgrid_terms(
                listed, [extra_ref[place, k] for k in range(3)], extra_ref[place, 3], speed, d
            )

        along_x, along_y = terms(row, 0), terms(row, 1)
        before, after = terms(row - 1, 2), terms(row + 1, 2)
        for n in range(TERMS):
            side = corner_ref[n]
            right = pltpu.roll(side, 42 - 8 * zz, 1)
            left = pltpu.roll(side, LANES - 18 - 8 * zz, 1)
            terms_ref[zz, n, 0] = jnp.where(lane == LANES - 1, right, shift_x(along_x[n], -1))
            terms_ref[zz, n, 1] = jnp.where(lane == 0, left, shift_x(along_x[n], 1))
            terms_ref[zz, n, 2] = after[n] - before[n]
            terms_ref[zz, n, 3] = jnp.where(top, along_y[n], shift_s(along_y[n], -2))
            terms_ref[zz, n, 4] = jnp.where(bottom, -along_y[n], shift_s(along_y[n], 2))
        return carry

    lax.fori_loop(0, ROWS, term_row, 0)


def final_kernel(position_ref, *refs, span_count, parts):
    part_refs = refs[:parts]
    base_ref, terms_ref, out_ref, coefficient_ref, scratch = refs[parts:]
    lane = lanes()
    even = is_even()
    bottom, top = level_edges()
    totals = [
        (tile_of(part_refs[0], k) + tile_of(part_refs[1], k))
        + (tile_of(part_refs[2], k) + tile_of(part_refs[3], k))
        for k in range(4)
    ]
    ratios = []
    for total in totals:
        total = total * (1.0 / span_count)
        numerator = jnp.where(even, total, shift_s(total, 1))
        denominator = jnp.where(even, shift_s(total, -1), total)
        ratios.append(numerator / (denominator + RATIO_EPSILON))
    first, last = position_ref[0] == 1, position_ref[1] == 1
    here, ahead, behind, above, below = [], [], [], [], []
    for k in range(3):
        ratio = ratios[k]
        scratch[...] = ratio
        coefficient_ref[k] = scratch[pl.ds(0, 4, stride=2), :]
        before = jnp.where(first, ratio, shift_x(ratios[3], -2 * k))
        after = jnp.where(last, ratio, shift_x(ratios[3], 127 - (2 * k + 1)))
        ratio = 0.25 * ratio
        here.append(ratio)
        ahead.append(jnp.where(lane == LANES - 1, 0.25 * after, shift_x(ratio, -1)))
        behind.append(jnp.where(lane == 0, 0.25 * before, shift_x(ratio, 1)))
        above.append(2.0 * jnp.where(top, ratio, shift_s(ratio, -2)))
        below.append(2.0 * jnp.where(bottom, ratio, shift_s(ratio, 2)))

    for zz in range(ROWS):
        sums = [base_ref[pl.ds((field * ROWS + zz) * TILE, TILE), :] for field in range(NF)]
        for n in range(TERMS):
            k = TERM_MODEL[n]
            change = (
                (ahead[k] * terms_ref[zz, n, 0] - behind[k] * terms_ref[zz, n, 1])
                + here[k] * terms_ref[zz, n, 2]
                + (above[k] * terms_ref[zz, n, 3] - below[k] * terms_ref[zz, n, 4])
            )
            sums[TERM_FIELD[n]] = sums[TERM_FIELD[n]] + change
        for field in range(NF):
            out_ref[pl.ds(field * 32 + zz, TILE, stride=4), :] = sums[field]


def call(kernel, out_shapes, scratch=(), scalars=0, inputs=0, **options):
    smem = pl.BlockSpec(memory_space=pltpu.SMEM)
    shapes = [jax.ShapeDtypeStruct(shape, F32) for shape in out_shapes]
    return pl.pallas_call(
        kernel,
        out_shape=shapes,
        in_specs=[smem] * scalars + [VMEM] * inputs,
        out_specs=[VMEM] * len(shapes),
        scratch_shapes=[pltpu.VMEM(shape, F32) for shape in scratch],
        **options,
    )


def body(constituent_mass, flow_speeds, thermal_pair, blowing_indicator):
    count_x = lax.axis_size("gx")
    count_z = lax.axis_size("gz")
    column = lax.axis_index("gx")
    position = jnp.stack([column == 0, column == count_x - 1]).astype(jnp.int32)

    def ring(axis, count, step):
        return lambda value: lax.ppermute(
            value, axis, [(i, (i + step) % count) for i in range(count)]
        )

    own, to_left, to_right, up, down = call(
        pack_kernel,
        [
            (GROUPS * TILE, LANES), (TILE, LANES), (TILE, LANES),
            (MAIN_ROWS, LANES), (MAIN_ROWS, LANES),
        ],
        inputs=3,
    )(
        constituent_mass.reshape(-1, LANES),
        flow_speeds.reshape(-1, LANES),
        thermal_pair.reshape(-1, LANES),
    )
    got_left = ring("gx", count_x, 1)(to_right)
    got_right = ring("gx", count_x, -1)(to_left)
    up, down, edge = call(
        edge_kernel,
        [(MESSAGE_ROWS, LANES), (MESSAGE_ROWS, LANES), (2 * TILE, LANES)],
        scalars=1,
        inputs=6,
    )(position, got_left, got_right, to_left, to_right, up, down)
    below = ring("gz", count_z, 1)(up)
    above = ring("gz", count_z, -1)(down)

    (part,) = call(
        stream_kernel,
        [(GROUPS * TILE, LANES)],
        scratch=[(NF * TILE, LANES), (4 * TILE, LANES)],
        inputs=3,
    )(own, edge, blowing_indicator)

    totals, terms = call(
        model_kernel,
        [(4 * TILE, LANES), (ROWS, TERMS, 5, TILE, LANES)],
        scratch=[
            (STATE_ROWS, STATE_COUNT, TILE, LANES),
            (GRID_ROWS, SLOPED, TILE, LANES),
            (TERMS, TILE, LANES),
            (GRID_ROWS, FILTERED, TILE, LANES),
            (GRID_ROWS, 4, TILE, LANES),
            (GRID_ROWS, 4, TILE, LANES),
            (GRID_ROWS, 8, TILE, LANES),
            (6, TILE, LANES),
        ],
        inputs=4,
    )(own, edge, below, above)

    (base,) = call(
        span_kernel,
        [(GROUPS * TILE, LANES)],
        scratch=[
            (SPAN_TILES, NF, TILE, LANES), (SPAN_TILES, NF, TILE, LANES), (SPAN_TILES, TILE, LANES)
        ],
        inputs=4,
    )(own, below, above, part)

    def crossed(value, mask):
        return lax.ppermute(value, "gz", [(i, i ^ mask) for i in range(count_z)])

    totals = totals + crossed(totals, 1)
    reach = 2
    while count_z > 4 * reach:
        a, b, c = (crossed(totals, k * reach) for k in (1, 2, 3))
        totals = (totals + a) + (b + c)
        reach *= 4
    parts = [totals] + [
        crossed(totals, k * reach) if k * reach < count_z else jnp.zeros_like(totals)
        for k in (1, 2, 3)
    ]

    def final(position_ref, *refs):
        final_kernel(position_ref, *refs, span_count=TILE * count_z, parts=4)

    tendency, coefficients = call(
        final,
        [(NF * 32, LANES), (3, 4, LANES)],
        scratch=[(TILE, LANES)],
        scalars=1,
        inputs=6,
    )(position, *parts, base, terms)
    return tendency.reshape(NF, 4, TILE, LANES), coefficients


def solution(mesh):
    placed = (
        P(None, None, "gz", "gx"),
        P(None, None, "gz", "gx"),
        P(None, None, "gz", "gx"),
        P("gz", "gx"),
    )
    return jax.shard_map(
        body,
        mesh=mesh,
        in_specs=placed,
        out_specs=(P(None, None, "gz", "gx"), P(None, None, "gx")),
        check_vma=False,
    )
```

time: 78.7 us -> 42.4 us (0.54)
  blocking collectives: 26.6 us -> 0 us
  Pallas kernels: 0 us -> 20.4 us
  other arithmetic: 17.8 us -> 1.31 us
  waiting for transfers between devices: 13.8 us -> 5.6 us
  local copies, waits for them, and re-layouts: 6.52 us -> 1.83 us
  between operations: 1.48 us -> 0.68 us
    psum x1 -> x0, blocking collectives: 26.6 us -> none  [body(): coefficient = dynamic_ratio(lax.psum(totals, 'gz'), span_count)]
    pallas_call x0 -> x6, Pallas kernels: none -> 20.4 us  [the longest x1 8.35 us: body(): call(model_kernel, [(4 * TILE, LANES), (ROWS, TERMS, 5, TILE, LANES)], sc...]
    ppermute x6 -> x8, waiting for transfers between devices: 13.8 us -> 5.6 us  [the longest x4 4.54 us: ring(): lax.ppermute(value, axis, [(i, (i + step) % count) for i in range(count)])]
    add x21 -> x1, other arithmetic: 8.01 us -> 0.72 us  [body(): totals = totals + crossed(totals, 1)]
    unnamed x23 -> x16, local copies, waits for them, and re-layouts: 4.35 us -> 1.83 us
    slice x13 -> x0, local copies, waits for them, and re-layouts: 2.14 us -> none  [the longest x6 1.07 us: test_filter(): stream_pass[..., :-2, :]]
    reduce_sum x13 -> x0, other arithmetic: 1.99 us -> none  [the longest x3 1.07 us: germano_sums(): jnp.sum(contracted, axis=-2)]
    mul x19 -> x0, other arithmetic: 1.65 us -> none  [the longest x1 0.33 us: subgrid_flux(): species_flux = -diffuse * fraction_grad]
  transfers between devices with their start and end apart: 6 -> 8, of which waited for: 4 -> 4; matrix products, arithmetic and copies ran while one was open for 2% -> 1% of each run, Pallas kernels for 0% -> 16%
where the time goes in v1:
time: 42.4 us; the launch traced here: 42.1 us
  Pallas kernels  20.4 us (48%)
  starting transfers between devices  12.3 us (29%)
  waiting for transfers between devices  5.6 us (13%)
  local copies, waits for them, and re-layouts  1.83 us (4%)
  other arithmetic  1.31 us (3%)
  between operations  0.68 us (2%)
    pallas_call x1, Pallas kernels, body(): call(model_kernel, [(4 * TILE, LANES), (ROWS, TERMS, 5, TILE, LANES)], sc...  8.35 us
    ppermute x4, starting transfers between devices, ring(): lax.ppermute(value, axis, [(i, (i + step) % count) for i in range(count)])  7.44 us
    ppermute x4, starting transfers between devices, crossed(): return lax.ppermute(value, 'gz', [(i, i ^ mask) for i in range(count_z)])  4.84 us
    ppermute x4, waiting for transfers between devices, ring(): lax.ppermute(value, axis, [(i, (i + step) % count) for i in range(count)])  4.54 us
    pallas_call x1, Pallas kernels, body(): call(stream_kernel, [(GROUPS * TILE, LANES)], scratch=[(NF * TILE, LANES)...  3.89 us
    pallas_call x1, Pallas kernels, body(): call(span_kernel, [(GROUPS * TILE, LANES)], scratch=[(SPAN_TILES, NF, TIL...  2.69 us
    pallas_call x1, Pallas kernels, body(): call(final, [(NF * 32, LANES), (3, 4, LANES)], scratch=[(TILE, LANES)], s...  2.17 us
    unnamed x16, local copies, waits for them, and re-layouts  1.83 us
  transfers between devices with their start and end apart: 8, of which 4 were waited for; matrix products, arithmetic and copies ran while one was open for 1% of the time, Pallas kernels for 16%

profile of v1, /device:TPU:0, one launch (start us, length us, event | category | flops | bytes accessed | tf_op | source)
XLA Modules:
  0.0 42.1 jit_solution(6233768270669601544)
XLA Ops:
  0.6 1.7 %shard_map.59 = (f32[320,128]{1,0:T(8,128)}, f32[8,128]{1,0:T(8,128)}, f32[8,128]{1,0:T(8,128)}, f32[120,128]{1,0:T(8,128)}, f32[120,128]{1,0:T(8,128)}) custom-call(f32[160,128]{1,0:T(8,128)} %bitcast.6, f32[96,128]{1,0:T(8,128)} %bitcast.7, f32[64,128]{1,0:T(8,128)} %bitcast.8), custom_call_target="tpu_custom_call" | custom-call | tf_op jit(solution)/shard_map/pallas_call | solution.py:741
  2.3 2.9 %collective-permute-start = (f32[8,128]{1,0:T(8,128)}, f32[8,128]{1,0:T(8,128)S(1)}, u32[]{:S(2)}, u32[]{:S(2)}) collective-permute-start(f32[8,128]{1,0:T(8,128)} %get-tuple-element.15.to_right_ref), channel_id=1, source_target_pairs={{0,8},{8,16},{16,24},{24,0},{1,9},{9,17},{17,25},{25,1},{2,10},{10... | collective-permute-start | bytes 12296 | tf_op jit(solution)/shard_map/ppermute | solution.py:737
  5.2 1.0 %collective-permute-start.1 = (f32[8,128]{1,0:T(8,128)}, f32[8,128]{1,0:T(8,128)S(1)}, u32[]{:S(2)}, u32[]{:S(2)}) collective-permute-start(f32[8,128]{1,0:T(8,128)} %get-tuple-element.16.to_left_ref), channel_id=1, source_target_pairs={{0,24},{8,0},{16,8},{24,16},{1,25},{9,1},{17,9},{25,17},{2,26},{10... | collective-permute-start | bytes 12296 | tf_op jit(solution)/shard_map/ppermute | solution.py:737
  6.2 0.6 %add_convert_fusion.position_ref = s32[2]{0:T(128)} fusion(pred[1]{0:T(512)(128)(4,1)} %bitcast.1, pred[1]{0:T(512)(128)(4,1)} %bitcast), kind=kLoop, calls=%fused_computation | loop fusion | flops 4 | bytes 10 | tf_op jit(solution)/shard_map/convert_element_type | solution.py:734
  6.8 1.2 %collective-permute-done.got_left_ref = f32[8,128]{1,0:T(8,128)S(1)} collective-permute-done((f32[8,128]{1,0:T(8,128)}, f32[8,128]{1,0:T(8,128)S(1)}, u32[]{:S(2)}, u32[]{:S(2)}) %collective-permute-start) | collective-permute-done | bytes 4128 | tf_op jit(solution)/shard_map/ppermute | solution.py:737
  8.0 0.0 copy-start.6
  8.0 1.1 %collective-permute-done.1.got_right_ref = f32[8,128]{1,0:T(8,128)S(1)} collective-permute-done((f32[8,128]{1,0:T(8,128)}, f32[8,128]{1,0:T(8,128)S(1)}, u32[]{:S(2)}, u32[]{:S(2)}) %collective-permute-start.1) | collective-permute-done | bytes 4128 | tf_op jit(solution)/shard_map/ppermute | solution.py:737
  9.1 0.0 copy-start.7
  9.1 0.0 copy-done.6
  9.1 0.6 %copy-done.7 = f32[8,128]{1,0:T(8,128)} copy-done((f32[8,128]{1,0:T(8,128)}, f32[8,128]{1,0:T(8,128)S(1)}, u32[]{:S(2)}) %copy-start.7) | copy-done | bytes 4120
  9.6 1.6 %shard_map.60 = (f32[136,128]{1,0:T(8,128)}, f32[136,128]{1,0:T(8,128)}, f32[16,128]{1,0:T(8,128)}) custom-call(s32[2]{0:T(128)} %add_convert_fusion.position_ref, f32[8,128]{1,0:T(8,128)} %copy-done.6, f32[8,128]{1,0:T(8,128)} %copy-done.7, f32[8,128]{1,0:T(8,128)} %get-tuple-element.16.to_left_ref, f32[8,128]{1,0:T(8,128)} %get-tuple-element.15.to_right_ref, ...), custom_call_target="tpu_custom_call" | custom-call | tf_op jit(solution)/shard_map/pallas_call | solution.py:755
  11.3 0.0 collective-permute-start.2
  11.3 3.5 %collective-permute-start.3 = (f32[136,128]{1,0:T(8,128)}, f32[136,128]{1,0:T(8,128)S(1)}, u32[]{:S(2)}, u32[]{:S(2)}) collective-permute-start(f32[136,128]{1,0:T(8,128)} %get-tuple-element.21), channel_id=1, source_target_pairs={{0,7},{1,0},{2,1},{3,2},{4,3},{5,4},{6,5},{7,6},{8,15},{9,8},{10,9... | collective-permute-start | bytes 208904 | tf_op jit(solution)/shard_map/ppermute | solution.py:737
  14.8 2.3 %collective-permute-done.2.below_ref = f32[136,128]{1,0:T(8,128)S(1)} collective-permute-done((f32[136,128]{1,0:T(8,128)}, f32[136,128]{1,0:T(8,128)S(1)}, u32[]{:S(2)}, u32[]{:S(2)}) %collective-permute-start.2) | collective-permute-done | bytes 69664 | tf_op jit(solution)/shard_map/ppermute | solution.py:737
  17.1 0.0 copy-start
  17.1 0.0 collective-permute-done.3.above_ref
  17.1 0.0 copy-start.1
  17.1 0.6 %copy-done = f32[136,128]{1,0:T(8,128)} copy-done((f32[136,128]{1,0:T(8,128)}, f32[136,128]{1,0:T(8,128)S(1)}, u32[]{:S(2)}) %copy-start) | copy-done | bytes 69656
  17.7 0.0 copy-done.1
  17.7 8.4 %shard_map.61 = (f32[32,128]{1,0:T(8,128)}, f32[4,12,5,8,128]{4,3,2,1,0:T(8,128)}) custom-call(f32[320,128]{1,0:T(8,128)} %get-tuple-element.14.own_ref, f32[16,128]{1,0:T(8,128)} %get-tuple-element.19.edge_ref, f32[136,128]{1,0:T(8,128)} %copy-done, f32[136,128]{1,0:T(8,128)} %copy-done.1), custom_call_target="tpu_custom_call" | custom-call | tf_op jit(solution)/shard_map/pallas_call | solution.py:771
  26.1 0.5 %collective-permute-start.4 = (f32[32,128]{1,0:T(8,128)}, f32[32,128]{1,0:T(8,128)S(1)}, u32[]{:S(2)}, u32[]{:S(2)}) collective-permute-start(f32[32,128]{1,0:T(8,128)} %get-tuple-element.22), channel_id=1, source_target_pairs={{0,1},{1,0},{2,3},{3,2},{4,5},{5,4},{6,7},{7,6},{8,9},{9,8},{10,11... | collective-permute-start | bytes 49160 | tf_op jit(solution)/shard_map/ppermute | solution.py:797
  26.5 1.0 %collective-permute-done.4 = f32[32,128]{1,0:T(8,128)S(1)} collective-permute-done((f32[32,128]{1,0:T(8,128)}, f32[32,128]{1,0:T(8,128)S(1)}, u32[]{:S(2)}, u32[]{:S(2)}) %collective-permute-start.4) | collective-permute-done | bytes 16416 | tf_op jit(solution)/shard_map/ppermute | solution.py:797
  27.6 0.7 %add.3.refs_0_ = f32[32,128]{1,0:T(8,128)S(1)} add(f32[32,128]{1,0:T(8,128)} %get-tuple-element.22, f32[32,128]{1,0:T(8,128)S(1)} %collective-permute-done.4) | non-fusion elementwise | flops 4096 | bytes 49152 | tf_op jit(solution)/shard_map/add | solution.py:799
  28.3 0.0 copy-start.2
  28.3 3.4 %collective-permute-start.7 = (f32[32,128]{1,0:T(8,128)S(1)}, f32[32,128]{1,0:T(8,128)S(1)}, u32[]{:S(2)}, u32[]{:S(2)}) collective-permute-start(f32[32,128]{1,0:T(8,128)S(1)} %add.3.refs_0_), channel_id=1, source_target_pairs={{0,6},{1,7},{2,4},{3,5},{4,2},{5,3},{6,0},{7,1},{8,14},{9,15},{10,... | collective-permute-start | bytes 49160 | tf_op jit(solution)/shard_map/ppermute | solution.py:797
  31.7 0.0 collective-permute-start.6
  31.7 1.0 %collective-permute-start.5 = (f32[32,128]{1,0:T(8,128)S(1)}, f32[32,128]{1,0:T(8,128)S(1)}, u32[]{:S(2)}, u32[]{:S(2)}) collective-permute-start(f32[32,128]{1,0:T(8,128)S(1)} %add.3.refs_0_), channel_id=1, source_target_pairs={{0,2},{1,3},{2,0},{3,1},{4,6},{5,7},{6,4},{7,5},{8,10},{9,11},{10,... | collective-permute-start | bytes 49160 | tf_op jit(solution)/shard_map/ppermute | solution.py:797
  32.7 3.9 %shard_map.62.part_ref = f32[320,128]{1,0:T(8,128)} custom-call(f32[320,128]{1,0:T(8,128)} %get-tuple-element.14.own_ref, f32[16,128]{1,0:T(8,128)} %get-tuple-element.19.edge_ref, s32[8,128]{1,0:T(8,128)} %blow_ref.1), custom_call_target="tpu_custom_call" | custom-call | tf_op jit(solution)/shard_map/pallas_call | solution.py:764
  36.6 0.0 copy-done.2
  36.6 2.7 %shard_map.63.refs_4_ = f32[320,128]{1,0:T(8,128)} custom-call(f32[320,128]{1,0:T(8,128)} %get-tuple-element.14.own_ref, f32[136,128]{1,0:T(8,128)} %copy-done, f32[136,128]{1,0:T(8,128)} %copy-done.1, f32[320,128]{1,0:T(8,128)} %shard_map.62.part_ref), custom_call_target="tpu_custom_call" | custom-call | tf_op jit(solution)/shard_map/pallas_call | solution.py:787
  39.3 0.0 collective-permute-done.7.refs_3_
  39.3 0.0 copy-start.3
  39.3 0.0 collective-permute-done.6.refs_2_
  39.3 0.0 copy-start.4
  39.3 0.0 collective-permute-done.5.refs_1_
  39.3 0.0 copy-start.5
  39.3 0.6 %copy-done.3 = f32[32,128]{1,0:T(8,128)} copy-done((f32[32,128]{1,0:T(8,128)}, f32[32,128]{1,0:T(8,128)S(1)}, u32[]{:S(2)}) %copy-start.3) | copy-done | bytes 16408
  39.9 0.0 copy-done.4
  39.9 0.0 copy-done.5
  39.9 2.2 %shard_map.64 = (f32[320,128]{1,0:T(8,128)}, f32[3,4,128]{2,1,0:T(4,128)}) custom-call(s32[2]{0:T(128)} %add_convert_fusion.position_ref, f32[32,128]{1,0:T(8,128)} %copy-done.2, f32[32,128]{1,0:T(8,128)} %copy-done.5, f32[32,128]{1,0:T(8,128)} %copy-done.4, f32[32,128]{1,0:T(8,128)} %copy-done.3, f32[320,128]{1,0:T(8,128)} %shard_map.63.refs_4_, ...), custom_call_target="tpu_custom_call" | custom-call | tf_op jit(solution)/shard_map/pallas_call | solution.py:813
Async XLA Ops:
  2.3 5.7 %collective-permute-start = (f32[8,128]{1,0:T(8,128)}, f32[8,128]{1,0:T(8,128)S(1)}, u32[]{:S(2)}, u32[]{:S(2)}) collective-permute-start(f32[8,128]{1,0:T(8,128)} %get-tuple-element.15.to_right_ref), channel_id=1, source_target_pairs={{0,8},{8,16},{16,24},{24,0},{1,9},{9,17},{17,25},{25,1},{2,10},{10... | collective-permute-start | bytes 12296 | tf_op jit(solution)/shard_map/ppermute | solution.py:737
  5.2 3.8 %collective-permute-start.1 = (f32[8,128]{1,0:T(8,128)}, f32[8,128]{1,0:T(8,128)S(1)}, u32[]{:S(2)}, u32[]{:S(2)}) collective-permute-start(f32[8,128]{1,0:T(8,128)} %get-tuple-element.16.to_left_ref), channel_id=1, source_target_pairs={{0,24},{8,0},{16,8},{24,16},{1,25},{9,1},{17,9},{25,17},{2,26},{10... | collective-permute-start | bytes 12296 | tf_op jit(solution)/shard_map/ppermute | solution.py:737
  8.0 1.1 %copy-start.6 = (f32[8,128]{1,0:T(8,128)}, f32[8,128]{1,0:T(8,128)S(1)}, u32[]{:S(2)}) copy-start(f32[8,128]{1,0:T(8,128)S(1)} %collective-permute-done.got_left_ref) | copy-start | bytes 12292
  9.1 0.6 %copy-start.7 = (f32[8,128]{1,0:T(8,128)}, f32[8,128]{1,0:T(8,128)S(1)}, u32[]{:S(2)}) copy-start(f32[8,128]{1,0:T(8,128)S(1)} %collective-permute-done.1.got_right_ref) | copy-start | bytes 12292
  11.3 5.8 %collective-permute-start.2 = (f32[136,128]{1,0:T(8,128)}, f32[136,128]{1,0:T(8,128)S(1)}, u32[]{:S(2)}, u32[]{:S(2)}) collective-permute-start(f32[136,128]{1,0:T(8,128)} %get-tuple-element.20), channel_id=1, source_target_pairs={{0,1},{1,2},{2,3},{3,4},{4,5},{5,6},{6,7},{7,0},{8,9},{9,10},{10,1... | collective-permute-start | bytes 208904 | tf_op jit(solution)/shard_map/ppermute | solution.py:737
  11.3 5.8 %collective-permute-start.3 = (f32[136,128]{1,0:T(8,128)}, f32[136,128]{1,0:T(8,128)S(1)}, u32[]{:S(2)}, u32[]{:S(2)}) collective-permute-start(f32[136,128]{1,0:T(8,128)} %get-tuple-element.21), channel_id=1, source_target_pairs={{0,7},{1,0},{2,1},{3,2},{4,3},{5,4},{6,5},{7,6},{8,15},{9,8},{10,9... | collective-permute-start | bytes 208904 | tf_op jit(solution)/shard_map/ppermute | solution.py:737
  17.1 0.6 %copy-start = (f32[136,128]{1,0:T(8,128)}, f32[136,128]{1,0:T(8,128)S(1)}, u32[]{:S(2)}) copy-start(f32[136,128]{1,0:T(8,128)S(1)} %collective-permute-done.2.below_ref) | copy-start | bytes 208900
  17.1 0.7 %copy-start.1 = (f32[136,128]{1,0:T(8,128)}, f32[136,128]{1,0:T(8,128)S(1)}, u32[]{:S(2)}) copy-start(f32[136,128]{1,0:T(8,128)S(1)} %collective-permute-done.3.above_ref) | copy-start | bytes 208900
  26.1 1.5 %collective-permute-start.4 = (f32[32,128]{1,0:T(8,128)}, f32[32,128]{1,0:T(8,128)S(1)}, u32[]{:S(2)}, u32[]{:S(2)}) collective-permute-start(f32[32,128]{1,0:T(8,128)} %get-tuple-element.22), channel_id=1, source_target_pairs={{0,1},{1,0},{2,3},{3,2},{4,5},{5,4},{6,7},{7,6},{8,9},{9,8},{10,11... | collective-permute-start | bytes 49160 | tf_op jit(solution)/shard_map/ppermute | solution.py:797
  28.3 8.3 %copy-start.2 = (f32[32,128]{1,0:T(8,128)}, f32[32,128]{1,0:T(8,128)S(1)}, u32[]{:S(2)}) copy-start(f32[32,128]{1,0:T(8,128)S(1)} %add.3.refs_0_) | copy-start | bytes 49156
  28.3 11.0 %collective-permute-start.7 = (f32[32,128]{1,0:T(8,128)S(1)}, f32[32,128]{1,0:T(8,128)S(1)}, u32[]{:S(2)}, u32[]{:S(2)}) collective-permute-start(f32[32,128]{1,0:T(8,128)S(1)} %add.3.refs_0_), channel_id=1, source_target_pairs={{0,6},{1,7},{2,4},{3,5},{4,2},{5,3},{6,0},{7,1},{8,14},{9,15},{10,... | collective-permute-start | bytes 49160 | tf_op jit(solution)/shard_map/ppermute | solution.py:797
  31.7 7.6 %collective-permute-start.6 = (f32[32,128]{1,0:T(8,128)S(1)}, f32[32,128]{1,0:T(8,128)S(1)}, u32[]{:S(2)}, u32[]{:S(2)}) collective-permute-start(f32[32,128]{1,0:T(8,128)S(1)} %add.3.refs_0_), channel_id=1, source_target_pairs={{0,4},{1,5},{2,6},{3,7},{4,0},{5,1},{6,2},{7,3},{8,12},{9,13},{10,... | collective-permute-start | bytes 49160 | tf_op jit(solution)/shard_map/ppermute | solution.py:797
  31.7 7.6 %collective-permute-start.5 = (f32[32,128]{1,0:T(8,128)S(1)}, f32[32,128]{1,0:T(8,128)S(1)}, u32[]{:S(2)}, u32[]{:S(2)}) collective-permute-start(f32[32,128]{1,0:T(8,128)S(1)} %add.3.refs_0_), channel_id=1, source_target_pairs={{0,2},{1,3},{2,0},{3,1},{4,6},{5,7},{6,4},{7,5},{8,10},{9,11},{10,... | collective-permute-start | bytes 49160 | tf_op jit(solution)/shard_map/ppermute | solution.py:797
  39.3 0.6 %copy-start.3 = (f32[32,128]{1,0:T(8,128)}, f32[32,128]{1,0:T(8,128)S(1)}, u32[]{:S(2)}) copy-start(f32[32,128]{1,0:T(8,128)S(1)} %collective-permute-done.7.refs_3_) | copy-start | bytes 49156
  39.3 0.6 %copy-start.4 = (f32[32,128]{1,0:T(8,128)}, f32[32,128]{1,0:T(8,128)S(1)}, u32[]{:S(2)}) copy-start(f32[32,128]{1,0:T(8,128)S(1)} %collective-permute-done.6.refs_2_) | copy-start | bytes 49156
  39.3 0.6 %copy-start.5 = (f32[32,128]{1,0:T(8,128)}, f32[32,128]{1,0:T(8,128)S(1)}, u32[]{:S(2)}) copy-start(f32[32,128]{1,0:T(8,128)S(1)} %collective-permute-done.5.refs_1_) | copy-start | bytes 49156

commit v2 on v1

--- a/solution.py
+++ b/solution.py
@@ -12,10 +12,14 @@
 TILE = 8
 LANES = 128
 HALO = 3
+SPAN = 8
+LAST = LANES - 5
 GROUPS = NF * ROWS
 PAIRS = NF // 2
+PACKS = 3
+PACK_ROWS = PACKS * TILE
 MAIN_ROWS = PAIRS * HALO * TILE
-MESSAGE_ROWS = MAIN_ROWS + 2 * TILE
+MESSAGE_ROWS = MAIN_ROWS + PACK_ROWS
 
 HEAT_RATIO = 1.4
 FILTER_SQUARE = 0.5 ** (2.0 / 3.0)
@@ -27,6 +31,7 @@
 
 VMEM = pl.BlockSpec(memory_space=pltpu.VMEM)
 F32 = jnp.float32
+SMALL = pltpu.CompilerParams(vmem_limit_bytes=8 << 20)
 
 
 def lanes():
@@ -62,12 +67,24 @@
     return ref[pl.ds(index * TILE, TILE), :]
 
 
-def pack_kernel(mass_ref, speed_ref, heat_ref, own_ref, left_ref, right_ref, up_ref, down_ref):
+def pack_kernel(
+    mass_hbm, speed_hbm, heat_hbm, own_ref, left_ref, right_ref, to_left_ref, to_right_ref,
+    up_ref, down_ref, mass_ref, speed_ref, heat_ref, arrived
+):
+    copies = [
+        pltpu.make_async_copy(source, target, arrived.at[k])
+        for k, (source, target) in enumerate(
+            ((mass_hbm, mass_ref), (speed_hbm, speed_ref), (heat_hbm, heat_ref))
+        )
+    ]
+    for copy in copies:
+        copy.start()
+    for copy in copies:
+        copy.wait()
     lane = lanes()
     even = is_even()
-    to_left = jnp.zeros((TILE, LANES), F32)
-    to_right = jnp.zeros((TILE, LANES), F32)
     tiles = {}
+    left = right = jnp.zeros((TILE, LANES), F32)
     for field in range(NF):
         if field < NSP:
             ref, base = mass_ref, field
@@ -76,13 +93,19 @@
         else:
             ref, base = heat_ref, field - NSP - 3
         for zz in range(ROWS):
-            group = field * ROWS + zz
             tile = ref[pl.ds(base * 32 + zz, TILE, stride=4), :]
             tiles[field, zz] = tile
-            own_ref[pl.ds(group * TILE, TILE), :] = tile
-            reached = lane >= 3 * group
-            to_left = jnp.where(reached, shift_x(tile, 3 * group), to_left)
-            to_right = jnp.where(reached, shift_x(tile, 3 * group + 3), to_right)
+            own_ref[pl.ds((field * ROWS + zz) * TILE, TILE), :] = tile
+            start = 32 * (field % 4) + SPAN * zz
+            reached = lane >= start
+            left = jnp.where(reached, shift_x(tile, start + HALO), left)
+            right = jnp.where(reached, shift_x(tile, start - LAST), right)
+        if field % 4 == 3 or field == NF - 1:
+            slot = pl.ds(field // 4 * TILE, TILE)
+            left_ref[slot, :] = left
+            right_ref[slot, :] = right
+            to_left_ref[slot, :] = shift_x(left, 2)
+            to_right_ref[slot, :] = shift_x(right, -2)
         if field % 2:
             pair = field // 2
             for k in range(HALO):
@@ -93,33 +116,35 @@
                 down_ref[slot, :] = jnp.where(
                     even, tiles[field, k], shift_s(tiles[field - 1, k], 1)
                 )
-    left_ref[...] = to_left
-    right_ref[...] = to_right
 
 
 def edge_kernel(
-    position_ref, got_left_ref, got_right_ref, to_left_ref, to_right_ref, up_in, down_in,
+    got_left_ref, got_right_ref, left_ref, right_ref, up_in, down_in,
     up_ref, down_ref, edge_ref
 ):
     up_ref[pl.ds(0, MAIN_ROWS), :] = up_in[...]
     down_ref[pl.ds(0, MAIN_ROWS), :] = down_in[...]
-    lane = lanes()
-    third = lane - 3 * ((lane * 171) >> 9)
-    own_left = to_left_ref[...]
-    own_right = to_right_ref[...]
-    clamp_left = jnp.where(
-        third == 0, own_left,
-        jnp.where(third == 1, shift_x(own_left, 1), shift_x(own_left, 2)),
-    )
-    clamp_right = jnp.where(
-        third == 2, own_right,
-        jnp.where(third == 1, shift_x(own_right, -1), shift_x(own_right, -2)),
-    )
-    left = jnp.where(position_ref[0] == 1, clamp_left, got_left_ref[...])
-    right = jnp.where(position_ref[1] == 1, clamp_right, got_right_ref[...])
-    for ref, start in ((up_ref, MAIN_ROWS), (down_ref, MAIN_ROWS), (edge_ref, 0)):
-        ref[pl.ds(start, TILE), :] = left
-        ref[pl.ds(start + TILE, TILE), :] = right
+    even = is_even()
+    place = lanes() & (SPAN - 1)
+    column = lax.axis_index("gx")
+    first, last = column == 0, column == lax.axis_size("gx") - 1
+    for k in range(PACKS):
+        left, right = tile_of(left_ref, k), tile_of(right_ref, k)
+        clamped = jnp.where(
+            place == 2, shift_x(left, -1),
+            jnp.where(place == 1, shift_x(left, -2), shift_x(left, -3)),
+        )
+        left = jnp.where(place < 3, jnp.where(first, clamped, tile_of(got_left_ref, k)), left)
+        clamped = jnp.where(
+            place == 5, shift_x(right, 1),
+            jnp.where(place == 6, shift_x(right, 2), shift_x(right, 3)),
+        )
+        right = jnp.where(place > 4, jnp.where(last, clamped, tile_of(got_right_ref, k)), right)
+        edge_ref[pl.ds(k * TILE, TILE), :] = left
+        edge_ref[pl.ds((PACKS + k) * TILE, TILE), :] = right
+        slot = pl.ds(MAIN_ROWS + k * TILE, TILE)
+        up_ref[slot, :] = jnp.where(even, shift_s(left, -1), right)
+        down_ref[slot, :] = jnp.where(even, left, shift_s(right, 1))
 
 
 def row_tile(own_ref, below_ref, above_ref, field, zz):
@@ -139,28 +164,21 @@
     return jnp.where(is_even(), shift_s(tile_of(own_ref, field * ROWS + k), -1), halo)
 
 
-def halo_packs(edge_ref, below_ref, above_ref):
+def edge_packs(edge_ref, below_ref, above_ref, k):
     even = is_even()
-    packs = []
-    for side in range(2):
-        own = tile_of(edge_ref, side)
-        low = below_ref[pl.ds(MAIN_ROWS + side * TILE, TILE), :]
-        high = above_ref[pl.ds(MAIN_ROWS + side * TILE, TILE), :]
-        packs.append(
-            (
-                jnp.where(even, shift_s(low, -1), shift_s(own, 1)),
-                own,
-                jnp.where(even, shift_s(own, -1), shift_s(high, 1)),
-            )
-        )
-    return packs
-
-
-def spread(left_pack, right_pack, group):
-    return jnp.where(
-        lanes() < 64,
-        shift_x(right_pack, (LANES - 3 * group)),
-        shift_x(left_pack, LANES - HALO - 3 * group),
+    left, right = tile_of(edge_ref, k), tile_of(edge_ref, PACKS + k)
+    low, high = tile_of(below_ref, MAIN_ROWS // TILE + k), tile_of(above_ref, MAIN_ROWS // TILE + k)
+    return (
+        (
+            jnp.where(even, low, shift_s(left, 1)),
+            left,
+            jnp.where(even, shift_s(left, -1), shift_s(high, 1)),
+        ),
+        (
+            jnp.where(even, shift_s(low, -1), shift_s(right, 1)),
+            right,
+            jnp.where(even, shift_s(right, -1), high),
+        ),
     )
 
 
@@ -211,63 +229,49 @@
     return here + 0.5 * (slopes[2] - waves[2]) + (gain + loss) * (1.0 / 12.0)
 
 
-def stream_kernel(own_ref, edge_ref, blow_ref, out_ref, first_ref, blow_rows):
+def stream_kernel(own_ref, edge_ref, blow_ref, out_ref, edge_face_ref, blow_rows):
     lane = lanes()
     bottom, top = level_edges()
     for level in range(4):
         blow_rows[pl.ds(level * TILE, TILE), :] = blow_ref[...].astype(F32)
-    left_pack = tile_of(edge_ref, 0)
-    right_pack = tile_of(edge_ref, 1)
+
+    def faces_along_x(flux, conserved, signal):
+        slope = shift_x(flux, -1) - flux
+        jump = shift_x(conserved, -1) - conserved
+        slopes = [shift_x(slope, -k) for k in range(-2, 3)]
+        jumps = [shift_x(jump, -k) for k in range(-2, 3)]
+        return face_flux(flux, slopes, jumps, signal)
 
     fields = []
     for field in range(NF):
-        gathered = jnp.zeros((TILE, LANES), F32)
-        for zz in range(ROWS):
-            group = field * ROWS + zz
-            halo = shift_x(left_pack, LANES - 3 - 3 * group)
-            tile = jnp.where(lane >= LANES - HALO, halo, tile_of(own_ref, group))
-            gathered = jnp.where(lane >= 8 * zz, shift_x(tile, 8 * zz + 3), gathered)
-        fields.append(gathered)
+        pack, start = field // 4, 32 * (field % 4)
+        fields.append(
+            jnp.where(
+                lane < 32,
+                shift_x(tile_of(edge_ref, pack), -start),
+                shift_x(tile_of(edge_ref, PACKS + pack), 32 - start),
+            )
+        )
+    fields = [jnp.where(lane < 64, value, shift_x(value, 64)) for value in fields]
     density, pressure, sound, conserved = state_of(fields)
-    speed = fields[NSP]
-    flux = flux_of(conserved, pressure, speed, 0)
-    signal = jnp.abs(speed) + sound
+    flux = flux_of(conserved, pressure, fields[NSP], 0)
+    signal = jnp.abs(fields[NSP]) + sound
     signal = jnp.maximum(signal, shift_x(signal, -1))
     for field in range(NF):
-        slope = shift_x(flux[field], -1) - flux[field]
-        jump = shift_x(conserved[field], -1) - conserved[field]
-        slopes = [shift_x(slope, -k) for k in range(-2, 3)]
-        jumps = [shift_x(jump, -k) for k in range(-2, 3)]
-        first_ref[pl.ds(field * TILE, TILE), :] = face_flux(
-            flux[field], slopes, jumps, signal
+        edge_face_ref[pl.ds(field * TILE, TILE), :] = faces_along_x(
+            flux[field], conserved[field], signal
         )
 
-    low = lane < HALO
-    high = lane >= LANES - HALO
-
     def row(zz, carry):
-        fields, halos = [], []
+        fields = []
         for field in range(NF):
-            group = field * ROWS + zz
-            start = pl.multiple_of(group * TILE, TILE)
+            start = pl.multiple_of((field * ROWS + zz) * TILE, TILE)
             fields.append(own_ref[pl.ds(start, TILE), :])
-            halos.append(
-                jnp.where(
-                    lane < 64,
-                    pltpu.roll(right_pack, (LANES - 3 * group) & (LANES - 1), 1),
-                    pltpu.roll(left_pack, LANES - HALO - 3 * group, 1),
-                )
-            )
         density, pressure, sound, conserved = state_of(fields)
-        halo_density, halo_pressure, halo_sound, halo_conserved = state_of(
-            [jnp.where(low | high, h, f) for h, f in zip(halos, fields)]
-        )
-        speed, halo_speed = fields[NSP], jnp.where(low | high, halos[NSP], fields[NSP])
+        speed = fields[NSP]
         flux = flux_of(conserved, pressure, speed, 0)
-        halo_flux = flux_of(halo_conserved, halo_pressure, halo_speed, 0)
         signal = jnp.abs(speed) + sound
-        halo_signal = jnp.abs(halo_speed) + halo_sound
-        signal = jnp.maximum(signal, shift_x(jnp.where(lane == 0, halo_signal, signal), -1))
+        signal = jnp.maximum(signal, shift_x(signal, -1))
 
         normal_speed = fields[NSP + 1]
         normal_flux = flux_of(conserved, pressure, normal_speed, 1)
@@ -284,26 +288,12 @@
         ]
 
         for field in range(NF):
-            def differences(value, halo):
-                left, right = jnp.where(high, halo, value), jnp.where(low, halo, value)
-                near = shift_x(left, -1) - left
-                far = shift_x(right, -1) - right
-                here = jnp.where(low, near, far)
-                return [
-                    shift_x(jnp.where(lane >= LANES - 2, near, here), 2),
-                    shift_x(jnp.where(lane >= LANES - 1, near, here), 1),
-                    here,
-                    shift_x(jnp.where(lane < 1, far, here), -1),
-                    shift_x(jnp.where(lane < 2, far, here), -2),
-                ]
-
-            slopes = differences(flux[field], halo_flux[field])
-            jumps = differences(conserved[field], halo_conserved[field])
-            face = face_flux(flux[field], slopes, jumps, signal)
-            first = pltpu.roll(
-                first_ref[pl.ds(field * TILE, TILE), :], LANES - 2 - 8 * zz, 1
-            )
-            change = jnp.where(lane == 0, first, shift_x(face, 1)) - face
+            face = faces_along_x(flux[field], conserved[field], signal)
+            edge_face = edge_face_ref[pl.ds(field * TILE, TILE), :]
+            left = pltpu.roll(edge_face, LANES - 3 - SPAN * zz, 1)
+            right = pltpu.roll(edge_face, LANES - 37 - SPAN * zz, 1)
+            face = jnp.where(lane < 2, left, jnp.where(lane >= LANES - 3, right, face))
+            change = shift_x(jnp.where(lane == LANES - 1, left, face), 1) - face
 
             value, above = conserved[field], shift_s(conserved[field], -2)
             level_face = 0.5 * (normal_flux[field] + shift_s(normal_flux[field], -2)) - normal_signal * (
@@ -495,43 +485,35 @@
 
 def model_kernel(
     own_ref, edge_ref, below_ref, above_ref,
-    totals_ref, terms_ref,
-    state_ref, halo_ref, corner_ref, tile_ref, extra_ref, wide_ref, favre_ref, sum_ref,
+    totals_ref, tile_ref, extra_ref, corner_x_ref, state_ref,
+    corner_ref, wide_ref, favre_ref, sum_ref,
 ):
     lane = lanes()
     even = is_even()
     bottom, top = level_edges()
-    low = lane < HALO
-    high = lane >= LANES - HALO
     scale = jnp.where(bottom | top, 4.0, 2.0)
-    packs = halo_packs(edge_ref, below_ref, above_ref)
-
+
+    corner = []
     for field in range(NF):
-        corner_ref[field] = jnp.zeros((TILE, LANES), F32)
+        if field % 4 == 0:
+            packs = edge_packs(edge_ref, below_ref, above_ref, field // 4)
+        start = 32 * (field % 4)
+        tile = None
+        for side in range(2):
+            for block, (bound, move) in enumerate(((0, -16), (16, 16), (48, 48))):
+                moved = shift_x(packs[side][block], 64 * side + move - start)
+                tile = moved if tile is None else jnp.where(lane >= 64 * side + bound, moved, tile)
+        corner.append(tile)
+    corner = model_state(corner)
+    for k in range(SLOPED - 1):
+        corner_ref[k] = corner[SPEED + k]
+
     for zz in range(-2, 6):
-        block, place = (zz + ROWS) // ROWS, zz % ROWS
-        rows, halos = [], []
-        start = 8 * (zz + 2)
-        for field in range(NF):
-            group = field * ROWS + place
-            row = row_tile(own_ref, below_ref, above_ref, field, zz)
-            halo = spread(packs[0][block], packs[1][block], group)
-            rows.append(row)
-            halos.append(jnp.where(low | high, halo, row))
-            left = shift_x(jnp.where(high, halo, row), start + 3)
-            right = shift_x(jnp.where(low, halo, row), 64 + start - 123)
-            kept = corner_ref[field]
-            kept = jnp.where((lane >= start) & (lane < start + 8), left, kept)
-            corner_ref[field] = jnp.where(
-                (lane >= 64 + start) & (lane < 72 + start), right, kept
-            )
-        states = model_state(rows)
+        states = model_state(
+            [row_tile(own_ref, below_ref, above_ref, field, zz) for field in range(NF)]
+        )
         for k in range(STATE_COUNT):
             state_ref[zz + 2, k] = states[k]
-        if -1 <= zz <= 4:
-            halo_states = model_state(halos)
-            for k in range(SLOPED):
-                halo_ref[zz + 1, k] = halo_states[SPEED + k]
 
     def grid_row(row, carry):
         def here(k):
@@ -539,10 +521,10 @@
 
         slopes = []
         for k in range(SLOPED - 1):
-            value, halo = here(SPEED + k), halo_ref[row, k]
-            along_x = shift_x(jnp.where(lane == 0, halo, value), -1) - shift_x(
-                jnp.where(lane == LANES - 1, halo, value), 1
-            )
+            value, side = here(SPEED + k), corner_ref[k]
+            ahead = jnp.where(lane == 0, pltpu.roll(side, 51 - SPAN * row, 1), value)
+            behind = jnp.where(lane == LANES - 1, pltpu.roll(side, 117 - SPAN * row, 1), value)
+            along_x = shift_x(ahead, -1) - shift_x(behind, 1)
             along_z = state_ref[row + 2, SPEED + k] - state_ref[row, SPEED + k]
             slopes.append((along_x, level_slope(value, scale), along_z))
         tiles, vibration, last = grid_terms(here, slopes)
@@ -565,16 +547,14 @@
 
     lax.fori_loop(0, GRID_ROWS, grid_row, 0)
 
-    corner = model_state([corner_ref[field] for field in range(NF)])
-
     def corner_slopes(value):
         along_x = shift_x(value, -1) - shift_x(value, 1)
-        along_z = shift_x(value, -8) - shift_x(value, 8)
+        along_z = shift_x(value, -SPAN) - shift_x(value, SPAN)
         return along_x, level_slope(value, scale), along_z
 
     def corner_filter(value):
-        pair = value + shift_x(value, -8)
-        return filter_x(pair + shift_x(pair, 8))
+        pair = value + shift_x(value, -SPAN)
+        return filter_x(pair + shift_x(pair, SPAN))
 
     slopes = [corner_slopes(corner[SPEED + k]) for k in range(SLOPED - 1)]
     corner_tiles, corner_vibration, corner_last = grid_terms(lambda k: corner[k], slopes)
@@ -587,11 +567,13 @@
     )
     corner_totals = []
     for value in corner_sums:
-        value = value + shift_x(value, -8)
-        corner_totals.append(value + shift_x(value, -16))
+        value = value + shift_x(value, -SPAN)
+        corner_totals.append(value + shift_x(value, -2 * SPAN))
     corner_x = subgrid_terms(
         corner_tiles, corner_vibration, corner_last, [corner[SPEED + k] for k in range(3)], 0
     )
+    for n in range(TERMS):
+        corner_x_ref[n] = corner_x[n]
 
     for k in range(6):
         sum_ref[k] = jnp.zeros((TILE, LANES), F32)
@@ -634,30 +616,28 @@
         edges = jnp.where(lane == 2 * k + 1, shift_x(side, 2 * k + 1 - 85), edges)
     totals_ref[pl.ds(3 * TILE, TILE), :] = edges
 
-    for n in range(TERMS):
-        corner_ref[n] = corner_x[n]
+
+def term_kernel(tile_ref, extra_ref, corner_ref, state_ref, terms_ref):
+    lane = lanes()
+    bottom, top = level_edges()
 
     def term_row(zz, carry):
         row = zz + 1
 
         def terms(place, d):
-            tiles = {k: tile_ref[place, k] for k in range(STRESS, STRESS + 5)}
-            tiles.update({HEAT_SLOPE + d: tile_ref[place, HEAT_SLOPE + d]})
-            tiles.update(
-                {MASS_SLOPE + 3 * s + d: tile_ref[place, MASS_SLOPE + 3 * s + d] for s in range(4)}
-            )
-            listed = [tiles.get(k) for k in range(FILTERED)]
+            needed = list(range(STRESS, STRESS + 5)) + [HEAT_SLOPE + d]
+            needed += [MASS_SLOPE + 3 * s + d for s in range(4)]
+            tiles = [tile_ref[place, k] if k in needed else None for k in range(FILTERED)]
+            vibration = [extra_ref[place, k] if k == d else None for k in range(3)]
             speed = [state_ref[place + 1, SPEED + k] for k in range(3)]
-            return subgrid_terms(
-                listed, [extra_ref[place, k] for k in range(3)], extra_ref[place, 3], speed, d
-            )
+            return subgrid_terms(tiles, vibration, extra_ref[place, 3], speed, d)
 
         along_x, along_y = terms(row, 0), terms(row, 1)
         before, after = terms(row - 1, 2), terms(row + 1, 2)
         for n in range(TERMS):
             side = corner_ref[n]
-            right = pltpu.roll(side, 42 - 8 * zz, 1)
-            left = pltpu.roll(side, LANES - 18 - 8 * zz, 1)
+            right = pltpu.roll(side, 42 - SPAN * zz, 1)
+            left = pltpu.roll(side, LANES - 18 - SPAN * zz, 1)
             terms_ref[zz, n, 0] = jnp.where(lane == LANES - 1, right, shift_x(along_x[n], -1))
             terms_ref[zz, n, 1] = jnp.where(lane == 0, left, shift_x(along_x[n], 1))
             terms_ref[zz, n, 2] = after[n] - before[n]
@@ -668,7 +648,7 @@
     lax.fori_loop(0, ROWS, term_row, 0)
 
 
-def final_kernel(position_ref, *refs, span_count, parts):
+def final_kernel(*refs, parts):
     part_refs = refs[:parts]
     base_ref, terms_ref, out_ref, coefficient_ref, scratch = refs[parts:]
     lane = lanes()
@@ -681,11 +661,12 @@
     ]
     ratios = []
     for total in totals:
-        total = total * (1.0 / span_count)
+        total = total * (1.0 / (TILE * lax.axis_size("gz")))
         numerator = jnp.where(even, total, shift_s(total, 1))
         denominator = jnp.where(even, shift_s(total, -1), total)
         ratios.append(numerator / (denominator + RATIO_EPSILON))
-    first, last = position_ref[0] == 1, position_ref[1] == 1
+    column = lax.axis_index("gx")
+    first, last = column == 0, column == lax.axis_size("gx") - 1
     here, ahead, behind, above, below = [], [], [], [], []
     for k in range(3):
         ratio = ratios[k]
@@ -714,50 +695,58 @@
             out_ref[pl.ds(field * 32 + zz, TILE, stride=4), :] = sums[field]
 
 
-def call(kernel, out_shapes, scratch=(), scalars=0, inputs=0, **options):
-    smem = pl.BlockSpec(memory_space=pltpu.SMEM)
-    shapes = [jax.ShapeDtypeStruct(shape, F32) for shape in out_shapes]
-    return pl.pallas_call(
+def call(kernel, out_shapes, scratch=(), inputs=0, final=False):
+    shape_of = jax.ShapeDtypeStruct if final else pltpu.VMEM
+    run = pl.pallas_call(
         kernel,
-        out_shape=shapes,
-        in_specs=[smem] * scalars + [VMEM] * inputs,
-        out_specs=[VMEM] * len(shapes),
+        out_shape=[shape_of(shape, F32) for shape in out_shapes],
+        in_specs=[VMEM] * inputs,
+        out_specs=[VMEM] * len(out_shapes),
         scratch_shapes=[pltpu.VMEM(shape, F32) for shape in scratch],
-        **options,
+        compiler_params=SMALL,
     )
+
+    def placed(*args):
+        return run(*[pltpu.with_memory_space_constraint(arg, pltpu.VMEM) for arg in args])
+
+    return placed
 
 
 def body(constituent_mass, flow_speeds, thermal_pair, blowing_indicator):
     count_x = lax.axis_size("gx")
     count_z = lax.axis_size("gz")
-    column = lax.axis_index("gx")
-    position = jnp.stack([column == 0, column == count_x - 1]).astype(jnp.int32)
 
     def ring(axis, count, step):
         return lambda value: lax.ppermute(
             value, axis, [(i, (i + step) % count) for i in range(count)]
         )
 
-    own, to_left, to_right, up, down = call(
+    arrays = [
+        value.reshape(-1, LANES) for value in (constituent_mass, flow_speeds, thermal_pair)
+    ]
+    packed = (PACK_ROWS, LANES)
+    own, left, right, to_left, to_right, up, down = pl.pallas_call(
         pack_kernel,
-        [
-            (GROUPS * TILE, LANES), (TILE, LANES), (TILE, LANES),
-            (MAIN_ROWS, LANES), (MAIN_ROWS, LANES),
+        out_shape=[
+            pltpu.VMEM(shape, F32)
+            for shape in (
+                (GROUPS * TILE, LANES), packed, packed, packed, packed,
+                (MAIN_ROWS, LANES), (MAIN_ROWS, LANES),
+            )
         ],
-        inputs=3,
-    )(
-        constituent_mass.reshape(-1, LANES),
-        flow_speeds.reshape(-1, LANES),
-        thermal_pair.reshape(-1, LANES),
-    )
+        in_specs=[pl.BlockSpec(memory_space=pltpu.HBM)] * 3,
+        out_specs=[VMEM] * 7,
+        scratch_shapes=[pltpu.VMEM(value.shape, F32) for value in arrays]
+        + [pltpu.SemaphoreType.DMA((3,))],
+        compiler_params=SMALL,
+    )(*[pltpu.with_memory_space_constraint(value, pltpu.HBM) for value in arrays])
     got_left = ring("gx", count_x, 1)(to_right)
     got_right = ring("gx", count_x, -1)(to_left)
     up, down, edge = call(
         edge_kernel,
-        [(MESSAGE_ROWS, LANES), (MESSAGE_ROWS, LANES), (2 * TILE, LANES)],
-        scalars=1,
+        [(MESSAGE_ROWS, LANES), (MESSAGE_ROWS, LANES), (2 * PACK_ROWS, LANES)],
         inputs=6,
-    )(position, got_left, got_right, to_left, to_right, up, down)
+    )(got_left, got_right, left, right, up, down)
     below = ring("gz", count_z, 1)(up)
     above = ring("gz", count_z, -1)(down)
 
@@ -767,16 +756,19 @@
         scratch=[(NF * TILE, LANES), (4 * TILE, LANES)],
         inputs=3,
     )(own, edge, blowing_indicator)
-
-    totals, terms = call(
+    below, above, part = lax.optimization_barrier((below, above, part))
+
+    totals, *kept = call(
         model_kernel,
-        [(4 * TILE, LANES), (ROWS, TERMS, 5, TILE, LANES)],
-        scratch=[
-            (STATE_ROWS, STATE_COUNT, TILE, LANES),
-            (GRID_ROWS, SLOPED, TILE, LANES),
-            (TERMS, TILE, LANES),
+        [
+            (4 * TILE, LANES),
             (GRID_ROWS, FILTERED, TILE, LANES),
             (GRID_ROWS, 4, TILE, LANES),
+            (TERMS, TILE, LANES),
+            (STATE_ROWS, STATE_COUNT, TILE, LANES),
+        ],
+        scratch=[
+            (SLOPED, TILE, LANES),
             (GRID_ROWS, 4, TILE, LANES),
             (GRID_ROWS, 8, TILE, LANES),
             (6, TILE, LANES),
@@ -784,6 +776,7 @@
         inputs=4,
     )(own, edge, below, above)
 
+    (terms,) = call(term_kernel, [(ROWS, TERMS, 5, TILE, LANES)], inputs=4)(*kept)
     (base,) = call(
         span_kernel,
         [(GROUPS * TILE, LANES)],
@@ -807,16 +800,16 @@
         for k in (1, 2, 3)
     ]
 
-    def final(position_ref, *refs):
-        final_kernel(position_ref, *refs, span_count=TILE * count_z, parts=4)
+    def final(*refs):
+        final_kernel(*refs, parts=4)
 
     tendency, coefficients = call(
         final,
         [(NF * 32, LANES), (3, 4, LANES)],
         scratch=[(TILE, LANES)],
-        scalars=1,
         inputs=6,
-    )(position, *parts, base, terms)
+        final=True,
+    )(*parts, base, terms)
     return tendency.reshape(NF, 4, TILE, LANES), coefficients
 
 

time: 42.4 us -> 27.4 us (0.65)
  Pallas kernels: 20.4 us -> 8.15 us
  local copies, waits for them, and re-layouts: 1.83 us -> 0.01 us
  other arithmetic: 1.31 us -> 0.01 us
    pallas_call x6 -> x7, Pallas kernels: 20.4 us -> 8.15 us  [the longest x6 7.01 us: placed(): run(*[pltpu.with_memory_space_constraint(arg, pltpu.VMEM) for arg in args])]
    ppermute x4, waiting for transfers between devices: 1.06 us -> 2.97 us  [crossed(): return lax.ppermute(value, 'gz', [(i, i ^ mask) for i in range(count_z)])]
    unnamed x16 -> x2, local copies, waits for them, and re-layouts: 1.83 us -> 0.01 us
    ppermute x4, waiting for transfers between devices: 4.54 us -> 2.83 us  [ring(): lax.ppermute(value, axis, [(i, (i + step) % count) for i in range(count)])]
    add x1, other arithmetic: 0.72 us -> 0.01 us  [body(): totals = totals + crossed(totals, 1)]
    convert_element_type x1 -> x0, other arithmetic: 0.59 us -> none  [body(): position = jnp.stack([column == 0, column == count_x - 1]).astype(jnp.int32)]
  transfers between devices with their start and end apart: 8 -> 8, of which waited for: 4 -> 5; matrix products, arithmetic and copies ran while one was open for 1% -> 0% of each run, Pallas kernels for 16% -> 12%
where the time goes in v2:
time: 27.4 us; the launch traced here: 27.2 us
  starting transfers between devices  12.6 us (46%)
  Pallas kernels  8.15 us (30%)
  waiting for transfers between devices  5.8 us (21%)
  between operations  0.7 us (3%)
    ppermute x4, starting transfers between devices, ring(): lax.ppermute(value, axis, [(i, (i + step) % count) for i in range(count)])  7.6 us
    pallas_call x6, Pallas kernels, placed(): run(*[pltpu.with_memory_space_constraint(arg, pltpu.VMEM) for arg in args])  7.01 us
    ppermute x4, starting transfers between devices, crossed(): return lax.ppermute(value, 'gz', [(i, i ^ mask) for i in range(count_z)])  4.98 us
    ppermute x4, waiting for transfers between devices, crossed(): return lax.ppermute(value, 'gz', [(i, i ^ mask) for i in range(count_z)])  2.97 us
    ppermute x4, waiting for transfers between devices, ring(): lax.ppermute(value, axis, [(i, (i + step) % count) for i in range(count)])  2.83 us
    pallas_call x1, Pallas kernels, body(): pl.pallas_call(pack_kernel, out_shape=[pltpu.VMEM(shape, F32) for shape i...  1.14 us
  transfers between devices with their start and end apart: 8, of which 5 were waited for; matrix products, arithmetic and copies ran while one was open for 0% of the time, Pallas kernels for 12%

profile of v2, /device:TPU:0, one launch (start us, length us, event | category | flops | bytes accessed | tf_op | source)
XLA Modules:
  0.0 27.2 jit_solution(7482929779904616943)
XLA Ops:
  0.6 1.1 %shard_map.59 = (f32[320,128]{1,0:T(8,128)S(1)}, f32[24,128]{1,0:T(8,128)S(1)}, f32[24,128]{1,0:T(8,128)S(1)}, f32[24,128]{1,0:T(8,128)S(1)}, f32[24,128]{1,0:T(...) custom-call(f32[160,128]{1,0:T(8,128)} %bitcast.4, f32[96,128]{1,0:T(8,128)} %bitcast.5, f32[64,128]{1,0:T(8,128)} %bitcast.6), custom_call_target="tpu_custom_call" | custom-call | tf_op jit(solution)/shard_map/pallas_call | solution.py:728
  1.8 3.0 %collective-permute-start = (f32[24,128]{1,0:T(8,128)S(1)}, f32[24,128]{1,0:T(8,128)S(1)}, u32[]{:S(2)}, u32[]{:S(2)}) collective-permute-start(f32[24,128]{1,0:T(8,128)S(1)} %get-tuple-element.23), channel_id=1, source_target_pairs={{0,8},{8,16},{16,24},{24,0},{1,9},{9,17},{17,25},{25,1},{2,10},{10... | collective-permute-start | bytes 36872 | tf_op jit(solution)/shard_map/ppermute | solution.py:720
  4.8 1.0 %collective-permute-start.1 = (f32[24,128]{1,0:T(8,128)S(1)}, f32[24,128]{1,0:T(8,128)S(1)}, u32[]{:S(2)}, u32[]{:S(2)}) collective-permute-start(f32[24,128]{1,0:T(8,128)S(1)} %get-tuple-element.24), channel_id=1, source_target_pairs={{0,24},{8,0},{16,8},{24,16},{1,25},{9,1},{17,9},{25,17},{2,26},{10... | collective-permute-start | bytes 36872 | tf_op jit(solution)/shard_map/ppermute | solution.py:720
  5.8 1.6 %collective-permute-done.got_left_ref = f32[24,128]{1,0:T(8,128)S(1)} collective-permute-done((f32[24,128]{1,0:T(8,128)S(1)}, f32[24,128]{1,0:T(8,128)S(1)}, u32[]{:S(2)}, u32[]{:S(2)}) %collective-permute-start) | collective-permute-done | bytes 12320 | tf_op jit(solution)/shard_map/ppermute | solution.py:720
  7.4 1.1 %collective-permute-done.1.got_right_ref = f32[24,128]{1,0:T(8,128)S(1)} collective-permute-done((f32[24,128]{1,0:T(8,128)S(1)}, f32[24,128]{1,0:T(8,128)S(1)}, u32[]{:S(2)}, u32[]{:S(2)}) %collective-permute-start.1) | collective-permute-done | bytes 12320 | tf_op jit(solution)/shard_map/ppermute | solution.py:720
  8.5 0.1 shard_map.60
  8.6 0.0 copy-start
  8.6 0.1 collective-permute-start.2
  8.6 3.5 %collective-permute-start.3 = (f32[144,128]{1,0:T(8,128)S(1)}, f32[144,128]{1,0:T(8,128)S(1)}, u32[]{:S(2)}, u32[]{:S(2)}) collective-permute-start(f32[144,128]{1,0:T(8,128)S(1)} %get-tuple-element.31), channel_id=1, source_target_pairs={{0,7},{1,0},{2,1},{3,2},{4,3},{5,4},{6,5},{7,6},{8,15},{9,8},{10,9... | collective-permute-start | bytes 221192 | tf_op jit(solution)/shard_map/ppermute | solution.py:720
  12.2 0.0 copy-done
  12.2 1.9 %shard_map.61.part_ref = f32[320,128]{1,0:T(8,128)S(1)} custom-call(f32[320,128]{1,0:T(8,128)S(1)} %get-tuple-element.22.own_ref, f32[48,128]{1,0:T(8,128)S(1)} %get-tuple-element.29.edge_ref, s32[8,128]{1,0:T(8,128)S(1)} %copy-done), custom_call_target="tpu_custom_call" | custom-call | tf_op jit(solution)/shard_map/pallas_call | solution.py:710
  14.1 0.2 collective-permute-done.2.below_ref
  14.3 0.0 collective-permute-done.3.above_ref
  14.3 2.7 %shard_map.62 = (f32[32,128]{1,0:T(8,128)S(1)}, f32[6,41,8,128]{3,2,1,0:T(8,128)S(1)}, f32[6,4,8,128]{3,2,1,0:T(8,128)S(1)}, f32[12,8,128]{2,1,0:T(8,128)S(1)}, f32[8,20,8,128]{3,2,1,0:T(8,128)S(1)}) custom-call(f32[320,128]{1,0:T(8,128)S(1)} %get-tuple-element.22.own_ref, f32[48,128]{1,0:T(8,128)S(1)} %get-tuple-element.29.edge_ref, ...), custom_call_target="tpu_custom_call" | custom-call | tf_op jit(solution)/shard_map/pallas_call | solution.py:710
  17.0 0.6 %collective-permute-start.4 = (f32[32,128]{1,0:T(8,128)S(1)}, f32[32,128]{1,0:T(8,128)S(1)}, u32[]{:S(2)}, u32[]{:S(2)}) collective-permute-start(f32[32,128]{1,0:T(8,128)S(1)} %get-tuple-element.34), channel_id=1, source_target_pairs={{0,1},{1,0},{2,3},{3,2},{4,5},{5,4},{6,7},{7,6},{8,9},{9,8},{10,11... | collective-permute-start | bytes 49160 | tf_op jit(solution)/shard_map/ppermute | solution.py:790
  17.6 0.8 %collective-permute-done.4 = f32[32,128]{1,0:T(8,128)S(1)} collective-permute-done((f32[32,128]{1,0:T(8,128)S(1)}, f32[32,128]{1,0:T(8,128)S(1)}, u32[]{:S(2)}, u32[]{:S(2)}) %collective-permute-start.4) | collective-permute-done | bytes 16416 | tf_op jit(solution)/shard_map/ppermute | solution.py:790
  18.5 3.3 %collective-permute-start.7 = (f32[32,128]{1,0:T(8,128)S(1)}, f32[32,128]{1,0:T(8,128)S(1)}, u32[]{:S(2)}, u32[]{:S(2)}) collective-permute-start(f32[32,128]{1,0:T(8,128)S(1)} %add.3.refs_0_), channel_id=1, source_target_pairs={{0,6},{1,7},{2,4},{3,5},{4,2},{5,3},{6,0},{7,1},{8,14},{9,15},{10,... | collective-permute-start | bytes 49160 | tf_op jit(solution)/shard_map/ppermute | solution.py:790
  21.8 0.0 collective-permute-start.6
  21.8 1.1 %collective-permute-start.5 = (f32[32,128]{1,0:T(8,128)S(1)}, f32[32,128]{1,0:T(8,128)S(1)}, u32[]{:S(2)}, u32[]{:S(2)}) collective-permute-start(f32[32,128]{1,0:T(8,128)S(1)} %add.3.refs_0_), channel_id=1, source_target_pairs={{0,2},{1,3},{2,0},{3,1},{4,6},{5,7},{6,4},{7,5},{8,10},{9,11},{10,... | collective-permute-start | bytes 49160 | tf_op jit(solution)/shard_map/ppermute | solution.py:790
  22.8 1.0 %shard_map.63.refs_4_ = f32[320,128]{1,0:T(8,128)S(1)} custom-call(f32[320,128]{1,0:T(8,128)S(1)} %get-tuple-element.22.own_ref, f32[144,128]{1,0:T(8,128)S(1)} %collective-permute-done.2.below_ref, f32[144,128]{1,0:T(8,128)S(1)} %collective-permute-done.3.above_ref, f32[320,128]{1,0:T(8,128)S(1)} %shard_map.61.part_ref), custom_call_target="tpu_custom_call" | custom-call | tf_op jit(solution)/shard_map/pallas_call | solution.py:710
  23.8 0.5 %shard_map.64.refs_5_ = f32[4,12,5,8,128]{4,3,2,1,0:T(8,128)S(1)} custom-call(f32[6,41,8,128]{3,2,1,0:T(8,128)S(1)} %get-tuple-element.36.tile_ref, f32[6,4,8,128]{3,2,1,0:T(8,128)S(1)} %get-tuple-element.37.extra_ref, f32[12,8,128]{2,1,0:T(8,128)S(1)} %get-tuple-element.38.corner_ref, f32[8,20,8,128]{3,2,1,0:T(8,128)S(1)} %get-tuple-element.39.state_ref), custom_call_target="tpu_custom_call" | custom-call | tf_op jit(solution)/shard_map/pallas_call | solution.py:710
  24.3 0.0 collective-permute-done.7.refs_3_
  24.3 2.1 %collective-permute-done.6.refs_2_ = f32[32,128]{1,0:T(8,128)S(1)} collective-permute-done((f32[32,128]{1,0:T(8,128)S(1)}, f32[32,128]{1,0:T(8,128)S(1)}, u32[]{:S(2)}, u32[]{:S(2)}) %collective-permute-start.6) | collective-permute-done | bytes 16416 | tf_op jit(solution)/shard_map/ppermute | solution.py:790
  26.4 0.0 collective-permute-done.5.refs_1_
  26.4 0.8 %shard_map.65 = (f32[320,128]{1,0:T(8,128)}, f32[3,4,128]{2,1,0:T(4,128)}) custom-call(f32[32,128]{1,0:T(8,128)S(1)} %add.3.refs_0_, f32[32,128]{1,0:T(8,128)S(1)} %collective-permute-done.5.refs_1_, f32[32,128]{1,0:T(8,128)S(1)} %collective-permute-done.6.refs_2_, f32[32,128]{1,0:T(8,128)S(1)} %collective-permute-done.7.refs_3_, ...), custom_call_target="tpu_custom_call" | custom-call | tf_op jit(solution)/shard_map/pallas_call | solution.py:710
  (1 shorter events, 0.0 us)
Async XLA Ops:
  1.8 5.6 %collective-permute-start = (f32[24,128]{1,0:T(8,128)S(1)}, f32[24,128]{1,0:T(8,128)S(1)}, u32[]{:S(2)}, u32[]{:S(2)}) collective-permute-start(f32[24,128]{1,0:T(8,128)S(1)} %get-tuple-element.23), channel_id=1, source_target_pairs={{0,8},{8,16},{16,24},{24,0},{1,9},{9,17},{17,25},{25,1},{2,10},{10... | collective-permute-start | bytes 36872 | tf_op jit(solution)/shard_map/ppermute | solution.py:720
  4.8 3.7 %collective-permute-start.1 = (f32[24,128]{1,0:T(8,128)S(1)}, f32[24,128]{1,0:T(8,128)S(1)}, u32[]{:S(2)}, u32[]{:S(2)}) collective-permute-start(f32[24,128]{1,0:T(8,128)S(1)} %get-tuple-element.24), channel_id=1, source_target_pairs={{0,24},{8,0},{16,8},{24,16},{1,25},{9,1},{17,9},{25,17},{2,26},{10... | collective-permute-start | bytes 36872 | tf_op jit(solution)/shard_map/ppermute | solution.py:720
  8.6 3.6 %copy-start = (s32[8,128]{1,0:T(8,128)S(1)}, s32[8,128]{1,0:T(8,128)}, u32[]{:S(2)}) copy-start(s32[8,128]{1,0:T(8,128)} %blow_ref.1) | copy-start | bytes 12292
  8.6 5.7 %collective-permute-start.2 = (f32[144,128]{1,0:T(8,128)S(1)}, f32[144,128]{1,0:T(8,128)S(1)}, u32[]{:S(2)}, u32[]{:S(2)}) collective-permute-start(f32[144,128]{1,0:T(8,128)S(1)} %get-tuple-element.30), channel_id=1, source_target_pairs={{0,1},{1,2},{2,3},{3,4},{4,5},{5,6},{6,7},{7,0},{8,9},{9,10},{10,1... | collective-permute-start | bytes 221192 | tf_op jit(solution)/shard_map/ppermute | solution.py:720
  8.6 5.6 %collective-permute-start.3 = (f32[144,128]{1,0:T(8,128)S(1)}, f32[144,128]{1,0:T(8,128)S(1)}, u32[]{:S(2)}, u32[]{:S(2)}) collective-permute-start(f32[144,128]{1,0:T(8,128)S(1)} %get-tuple-element.31), channel_id=1, source_target_pairs={{0,7},{1,0},{2,1},{3,2},{4,3},{5,4},{6,5},{7,6},{8,15},{9,8},{10,9... | collective-permute-start | bytes 221192 | tf_op jit(solution)/shard_map/ppermute | solution.py:720
  17.0 1.4 %collective-permute-start.4 = (f32[32,128]{1,0:T(8,128)S(1)}, f32[32,128]{1,0:T(8,128)S(1)}, u32[]{:S(2)}, u32[]{:S(2)}) collective-permute-start(f32[32,128]{1,0:T(8,128)S(1)} %get-tuple-element.34), channel_id=1, source_target_pairs={{0,1},{1,0},{2,3},{3,2},{4,5},{5,4},{6,7},{7,6},{8,9},{9,8},{10,11... | collective-permute-start | bytes 49160 | tf_op jit(solution)/shard_map/ppermute | solution.py:790
  18.5 5.8 %collective-permute-start.7 = (f32[32,128]{1,0:T(8,128)S(1)}, f32[32,128]{1,0:T(8,128)S(1)}, u32[]{:S(2)}, u32[]{:S(2)}) collective-permute-start(f32[32,128]{1,0:T(8,128)S(1)} %add.3.refs_0_), channel_id=1, source_target_pairs={{0,6},{1,7},{2,4},{3,5},{4,2},{5,3},{6,0},{7,1},{8,14},{9,15},{10,... | collective-permute-start | bytes 49160 | tf_op jit(solution)/shard_map/ppermute | solution.py:790
  21.8 4.6 %collective-permute-start.6 = (f32[32,128]{1,0:T(8,128)S(1)}, f32[32,128]{1,0:T(8,128)S(1)}, u32[]{:S(2)}, u32[]{:S(2)}) collective-permute-start(f32[32,128]{1,0:T(8,128)S(1)} %add.3.refs_0_), channel_id=1, source_target_pairs={{0,4},{1,5},{2,6},{3,7},{4,0},{5,1},{6,2},{7,3},{8,12},{9,13},{10,... | collective-permute-start | bytes 49160 | tf_op jit(solution)/shard_map/ppermute | solution.py:790
  21.8 4.6 %collective-permute-start.5 = (f32[32,128]{1,0:T(8,128)S(1)}, f32[32,128]{1,0:T(8,128)S(1)}, u32[]{:S(2)}, u32[]{:S(2)}) collective-permute-start(f32[32,128]{1,0:T(8,128)S(1)} %add.3.refs_0_), channel_id=1, source_target_pairs={{0,2},{1,3},{2,0},{3,1},{4,6},{5,7},{6,4},{7,5},{8,10},{9,11},{10,... | collective-permute-start | bytes 49160 | tf_op jit(solution)/shard_map/ppermute | solution.py:790

commit v3 on v2

v3 whole, which is shorter than its diff:
```python
import jax
import jax.numpy as jnp
from jax import lax
from jax.experimental import pallas as pl
from jax.experimental.pallas import tpu as pltpu
from jax.sharding import PartitionSpec as P


NSP = 5
NF = 10
ROWS = 4
TILE = 8
LANES = 128
HALO = 3
SPAN = 8
LAST = LANES - 5
GROUPS = NF * ROWS
PAIRS = NF // 2
PACKS = 3
PACK_ROWS = PACKS * TILE
MAIN_ROWS = PAIRS * HALO * TILE
MESSAGE_ROWS = MAIN_ROWS + PACK_ROWS

HEAT_RATIO = 1.4
FILTER_SQUARE = 0.5 ** (2.0 / 3.0)
TEST_SQUARE = 2.0 ** (2.0 / 3.0)
FORMATION = (0.0, 0.0, 0.1, 0.5, 0.25)
BLOWING = 0.3
SMOOTH_FLOOR = 0.01
RATIO_EPSILON = 1e-06

VMEM = pl.BlockSpec(memory_space=pltpu.VMEM)
F32 = jnp.float32
SMALL = pltpu.CompilerParams(vmem_limit_bytes=8 << 20)


def lanes():
    return lax.broadcasted_iota(jnp.int32, (TILE, LANES), 1)


def sublanes():
    return lax.broadcasted_iota(jnp.int32, (TILE, LANES), 0)


def shift_x(tile, step):
    if isinstance(step, int):
        step = step % LANES
        if step == 0:
            return tile
    return pltpu.roll(tile, step, 1)


def shift_s(tile, step):
    return pltpu.roll(tile, step % TILE, 0)


def is_even():
    return (sublanes() & 1) == 0


def level_edges():
    level = sublanes() >> 1
    return level == 0, level == 3


def slot_of(index):
    start = index * TILE
    return pl.ds(start if isinstance(index, int) else pl.multiple_of(start, TILE), TILE)


def tile_of(ref, index):
    return ref[slot_of(index), :]


def is_first_of_pair(axis):
    return (lax.axis_index(axis) & 1) == 0


def halo_tile(far_ref, near_ref, below, index):
    first, second = (far_ref, near_ref) if below else (near_ref, far_ref)
    return jnp.where(is_first_of_pair("gz"), tile_of(first, index), tile_of(second, index))


def pack_kernel(
    mass_hbm, speed_hbm, heat_hbm, blow_hbm, own_ref, left_ref, right_ref, far_ref, near_ref,
    blow_rows, given_ref, blow_ref, arrived
):
    start, copies = 0, []
    for k, source in enumerate((mass_hbm, speed_hbm, heat_hbm)):
        target = given_ref.at[pl.ds(start, source.shape[0])]
        copies.append(pltpu.make_async_copy(source, target, arrived.at[k]))
        start += source.shape[0]
    copies.append(pltpu.make_async_copy(blow_hbm, blow_ref, arrived.at[3]))
    for copy in copies:
        copy.start()
    for copy in copies:
        copy.wait()
    lane = lanes()
    even = is_even()
    first_core = is_first_of_pair("gz")

    def post(index, up, down):
        far_ref[slot_of(index), :] = jnp.where(first_core, down, up)
        near_ref[slot_of(index), :] = jnp.where(first_core, up, down)

    tiles = {}
    left = right = jnp.zeros((TILE, LANES), F32)
    for field in range(NF):
        for zz in range(ROWS):
            tile = given_ref[pl.ds(field * 32 + zz, TILE, stride=4), :]
            tiles[field, zz] = tile
            own_ref[slot_of(field * ROWS + zz), :] = tile
            start = 32 * (field % 4) + SPAN * zz
            reached = lane >= start
            left = jnp.where(reached, shift_x(tile, start + HALO), left)
            right = jnp.where(reached, shift_x(tile, start - LAST), right)
        if field % 4 == 3 or field == NF - 1:
            k = field // 4
            left_ref[slot_of(k), :] = left
            right_ref[slot_of(k), :] = right
            post(
                MAIN_ROWS // TILE + k,
                jnp.where(even, shift_s(left, -1), right),
                jnp.where(even, left, shift_s(right, 1)),
            )
        if field % 2:
            for k in range(HALO):
                post(
                    field // 2 * HALO + k,
                    jnp.where(even, shift_s(tiles[field - 1, k + 1], -1), tiles[field, k + 1]),
                    jnp.where(even, tiles[field, k], shift_s(tiles[field - 1, k], 1)),
                )
    for level in range(4):
        blow_rows[pl.ds(level * TILE, TILE), :] = blow_ref[...].astype(F32)


def gather_rows(own_ref, far_ref, near_ref, raw_ref):
    even = is_even()
    for field in range(NF):
        pair, second = divmod(field, 2)
        own = [tile_of(own_ref, field * ROWS + zz) for zz in range(ROWS)]
        for zz in range(ROWS):
            raw_ref[zz + HALO, field] = own[zz]
        for k in range(HALO):
            low = halo_tile(far_ref, near_ref, True, pair * HALO + k)
            high = halo_tile(far_ref, near_ref, False, pair * HALO + k)
            if second:
                low, high = shift_s(low, -1), shift_s(high, 1)
            raw_ref[k, field] = jnp.where(even, low, shift_s(own[k + 1], 1))
            raw_ref[k + HALO + ROWS, field] = jnp.where(even, shift_s(own[k], -1), high)


def edge_packs(left_ref, right_ref, far_ref, near_ref, k):
    even = is_even()
    left, right = tile_of(left_ref, k), tile_of(right_ref, k)
    low, high = (halo_tile(far_ref, near_ref, below, MAIN_ROWS // TILE + k) for below in (True, False))
    return (
        (
            jnp.where(even, low, shift_s(left, 1)),
            left,
            jnp.where(even, shift_s(left, -1), shift_s(high, 1)),
        ),
        (
            jnp.where(even, shift_s(low, -1), shift_s(right, 1)),
            right,
            jnp.where(even, shift_s(right, -1), high),
        ),
    )


def corner_pack_kernel(left_ref, right_ref, far_ref, near_ref, corner_ref, one_ref, other_ref):
    lane = lanes()
    even_column = is_first_of_pair("gx")
    corners = []
    for k in range(PACKS):
        packs = edge_packs(left_ref, right_ref, far_ref, near_ref, k)
        for j in range(min(4, NF - 4 * k)):
            start = 32 * j
            tile = None
            for side in range(2):
                for block, (bound, move) in enumerate(((0, -16), (16, 16), (48, 48))):
                    moved = shift_x(packs[side][block], 64 * side + move - start)
                    tile = (
                        moved if tile is None
                        else jnp.where(lane >= 64 * side + bound, moved, tile)
                    )
            corner_ref[4 * k + j] = tile
            corners.append(tile)
    for pair in range(PAIRS):
        first, second = corners[2 * pair], corners[2 * pair + 1]
        to_left = jnp.where(lane >= 64, shift_x(first, 66), shift_x(second, 2))
        to_right = jnp.where(lane < 64, shift_x(first, -66), shift_x(second, -2))
        one_ref[slot_of(pair), :] = jnp.where(even_column, to_right, to_left)
        other_ref[slot_of(pair), :] = jnp.where(even_column, to_left, to_right)


def state_of(fields):
    mass, motion = fields[:NSP], fields[NSP : NSP + 3]
    thermal, vibration = fields[NSP + 3], fields[NSP + 4]
    density = (mass[0] + mass[1]) + (mass[2] + mass[3]) + mass[4]
    formed = FORMATION[2] * mass[2] + FORMATION[3] * mass[3] + FORMATION[4] * mass[4]
    motion_square = motion[0] * motion[0] + motion[1] * motion[1] + motion[2] * motion[2]
    energy = density * (2.5 * thermal + vibration + 0.5 * motion_square) + formed
    conserved = (
        list(mass) + [density * speed for speed in motion] + [energy, density * vibration]
    )
    return density, density * thermal, jnp.sqrt(HEAT_RATIO * thermal), conserved


def flux_of(conserved, pressure, speed, component):
    flux = [value * speed for value in conserved]
    flux[NSP + component] = flux[NSP + component] + pressure
    flux[NSP + 3] = flux[NSP + 3] + pressure * speed
    return flux


def correction(d0, d1, d2, d3):
    floor = 4.0 * SMOOTH_FLOOR * 12.0 / 13.0
    share = 3.0 / 13.0
    e0, e1, e2 = d1 - d0, d2 - d1, d3 - d2
    g0, g1, g2 = e0 + (d1 + d1), d1 + d2, e2 - (d2 + d2)
    b0 = (e0 * e0 + floor) + share * (g0 * g0)
    b1 = (e1 * e1 + floor) + share * (g1 * g1)
    b2 = (e2 * e2 + floor) + share * (g2 * g2)
    p0, p1, p2 = b1 * b2, b0 * b2, b0 * b1
    w0 = p0 * p0
    w1 = 6.0 * (p1 * p1)
    w2 = 3.0 * (p2 * p2)
    r0 = 5.0 * d1 - (d0 + d0)
    r1 = d1 + (d2 + d2)
    r2 = 4.0 * d2 - d3
    return (w0 * r0 + w1 * r1 + w2 * r2) / (w0 + w1 + w2)


def face_flux(here, slopes, jumps, signal):
    waves = [signal * jump for jump in jumps]
    plus = [slopes[k] + waves[k] for k in range(4)]
    minus = [waves[k] - slopes[k] for k in range(1, 5)]
    gain = correction(*plus)
    loss = correction(minus[3], minus[2], minus[1], minus[0])
    return here + 0.5 * (slopes[2] - waves[2]) + (gain + loss) * (1.0 / 12.0)


def faces_along_x(flux, conserved, signal):
    slope = shift_x(flux, -1) - flux
    jump = shift_x(conserved, -1) - conserved
    slopes = [shift_x(slope, -k) for k in range(-2, 3)]
    jumps = [shift_x(jump, -k) for k in range(-2, 3)]
    return face_flux(flux, slopes, jumps, signal)


def stream_kernel(own_ref, blow_rows, face_ref, part_ref):
    bottom, top = level_edges()

    def row(zz, carry):
        fields = [tile_of(own_ref, field * ROWS + zz) for field in range(NF)]
        density, pressure, sound, conserved = state_of(fields)
        speed = fields[NSP]
        flux = flux_of(conserved, pressure, speed, 0)
        signal = jnp.abs(speed) + sound
        signal = jnp.maximum(signal, shift_x(signal, -1))

        normal_speed = fields[NSP + 1]
        normal_flux = flux_of(conserved, pressure, normal_speed, 1)
        normal_signal = jnp.abs(normal_speed) + sound
        normal_signal = 0.5 * jnp.maximum(normal_signal, shift_s(normal_signal, -2))
        blown = BLOWING * blow_rows[pl.ds(zz, TILE, stride=4), :]
        lift = blown / density
        enthalpy = 3.5 * fields[NSP + 3] + fields[NSP + 4] + 0.5 * lift * lift
        wall = [lift * fields[s] for s in range(NSP)]
        formed = FORMATION[2] * wall[2] + FORMATION[3] * wall[3] + FORMATION[4] * wall[4]
        zero = jnp.zeros((TILE, LANES), F32)
        wall = wall + [
            zero, blown * lift + pressure, zero, blown * enthalpy + formed, blown * fields[NSP + 4]
        ]
        relaxation = 2.0 * density * (fields[NSP + 3] - fields[NSP + 4])
        for field in range(NF):
            value, normal = conserved[field], normal_flux[field]
            slot = slot_of(field * ROWS + zz)
            face_ref[slot, :] = faces_along_x(flux[field], value, signal)
            above = shift_s(value, -2)
            level_face = 0.5 * (normal + shift_s(normal, -2)) - normal_signal * (above - value)
            level_face = jnp.where(top, normal, level_face)
            change = 2.0 * (jnp.where(bottom, wall[field], shift_s(level_face, 2)) - level_face)
            part_ref[slot, :] = change + relaxation if field == NF - 1 else change
        return carry

    lax.fori_loop(0, ROWS, row, 0)


def ends_kernel(corner_ref, face_ref, part_ref, out_ref):
    lane = lanes()
    fields = [corner_ref[field] for field in range(NF)]
    density, pressure, sound, conserved = state_of(fields)
    flux = flux_of(conserved, pressure, fields[NSP], 0)
    signal = jnp.abs(fields[NSP]) + sound
    signal = jnp.maximum(signal, shift_x(signal, -1))
    for field in range(NF):
        end_face = faces_along_x(flux[field], conserved[field], signal)
        for zz in range(ROWS):
            left = shift_x(end_face, 109 - SPAN * zz)
            right = shift_x(end_face, 43 - SPAN * zz)
            slot = slot_of(field * ROWS + zz)
            face = jnp.where(
                lane < 2, left, jnp.where(lane >= LANES - 3, right, face_ref[slot, :])
            )
            before = shift_x(jnp.where(lane == LANES - 1, left, face), 1)
            out_ref[slot, :] = part_ref[slot, :] + (before - face)


SPAN_TILES = ROWS + 2 * HALO


def span_kernel(raw_ref, part_ref, out_ref, value_ref, flux_ref, signal_ref):
    for place in range(SPAN_TILES):
        fields = [raw_ref[place, field] for field in range(NF)]
        _, pressure, sound, conserved = state_of(fields)
        speed = fields[NSP + 2]
        flux = flux_of(conserved, pressure, speed, 2)
        signal_ref[place] = jnp.abs(speed) + sound
        for field in range(NF):
            value_ref[place, field] = conserved[field]
            flux_ref[place, field] = flux[field]

    def faces_of(place):
        signal = jnp.maximum(signal_ref[place], signal_ref[place + 1])
        faces = []
        for field in range(NF):
            flux = [flux_ref[place + k, field] for k in range(-2, 4)]
            value = [value_ref[place + k, field] for k in range(-2, 4)]
            slopes = [flux[k + 1] - flux[k] for k in range(5)]
            jumps = [value[k + 1] - value[k] for k in range(5)]
            faces.append(face_flux(flux[2], slopes, jumps, signal))
        return tuple(faces)

    def row(zz, before):
        faces = faces_of(zz + HALO)
        for field in range(NF):
            slot = slot_of(field * ROWS + zz)
            out_ref[slot, :] = part_ref[slot, :] + (before[field] - faces[field])
        return faces

    lax.fori_loop(0, ROWS, row, faces_of(HALO - 1))


MASS, MOMENTUM, HEAT = 0, 5, 8
SPEED, THERMAL, VIBRATION, FRACTION, DENSITY = 9, 12, 13, 14, 19
STATE_COUNT = 20
SLOPED = 10
STATE_ROWS = 8
GRID_ROWS = 6
PAIR_INDEX = ((0, 0), (1, 1), (0, 1), (0, 2), (1, 2), (2, 2))

PRODUCT, STRESS, HEAT_FLUX, HEAT_SLOPE, MASS_FLUX, MASS_SLOPE = 0, 6, 11, 14, 17, 29
LAST_STRESS = 41
FILTERED = 42
SIDE_SLOPE = FILTERED
TILES = FILTERED + 3

TERMS = 12
TERM_FIELD = (0, 1, 2, 3, 4, 5, 6, 7, 8, 8, 8, 9)
TERM_MODEL = (2, 2, 2, 2, 2, 0, 0, 0, 0, 1, 2, 1)


def model_state(fields):
    mass, motion = fields[:NSP], fields[NSP : NSP + 3]
    thermal, vibration = fields[NSP + 3], fields[NSP + 4]
    density = (mass[0] + mass[1]) + (mass[2] + mass[3]) + mass[4]
    inverse = 1.0 / density
    fraction = [m * inverse for m in mass]
    return (
        list(mass)
        + [density * speed for speed in motion]
        + [density * thermal]
        + list(motion)
        + [thermal, vibration]
        + fraction
        + [density]
    )


def level_slope(value, scale):
    bottom, top = level_edges()
    above = jnp.where(top, value, shift_s(value, -2))
    below = jnp.where(bottom, value, shift_s(value, 2))
    return scale * (above - below)


def strain(slopes):
    diagonal = [2.0 * slopes[k][k] for k in range(3)]
    third = (diagonal[0] + diagonal[1] + diagonal[2]) * (1.0 / 3.0)
    first, second = diagonal[0] - third, diagonal[1] - third
    mixed = [slopes[0][1] + slopes[1][0], slopes[0][2] + slopes[2][0], slopes[1][2] + slopes[2][1]]
    last = diagonal[2] - third
    square = (
        first * first + second * second + last * last
        + 2.0 * (mixed[0] * mixed[0] + mixed[1] * mixed[1] + mixed[2] * mixed[2])
    )
    magnitude = jnp.sqrt(0.125 * square + 1e-06)
    return [first, second] + mixed + [last], magnitude


def grid_terms(here, slopes):
    deviator, magnitude = strain(slopes[:3])
    eddy = FILTER_SQUARE * here(DENSITY) * magnitude
    speed = [here(SPEED + k) for k in range(3)]
    momentum = [here(MOMENTUM + k) for k in range(3)]
    thermal = here(THERMAL)
    stress = [eddy * part for part in deviator]
    tiles = [momentum[i] * speed[j] for i, j in PAIR_INDEX]
    tiles += stress[:5]
    tiles += [m * thermal for m in momentum]
    tiles += [eddy * slopes[3][d] for d in range(3)]
    tiles += [here(MASS + s) * speed[d] for s in range(4) for d in range(3)]
    tiles += [eddy * slopes[5 + s][d] for s in range(4) for d in range(3)]
    tiles.append(stress[5])
    return tiles + [eddy * slopes[4][d] for d in range(3)]


def subgrid_terms(tile, speed, d):
    places = (STRESS, STRESS + 1, STRESS + 2, STRESS + 3, STRESS + 4, LAST_STRESS)
    full = ((0, 2, 3), (2, 1, 4), (3, 4, 5))
    tau = [tile(places[full[i][d]]) for i in range(3)]
    species = [tile(MASS_SLOPE + 3 * s + d) for s in range(4)]
    species.append(-((species[0] + species[1]) + (species[2] + species[3])))
    work = speed[0] * tau[0] + speed[1] * tau[1] + speed[2] * tau[2]
    vibration = tile(SIDE_SLOPE + d)
    heat = 3.5 * tile(HEAT_SLOPE + d) + vibration
    formed = FORMATION[2] * species[2] + FORMATION[3] * species[3] + FORMATION[4] * species[4]
    return species + tau + [work, heat, formed, vibration]


def favre(hat):
    density = (hat[0] + hat[1]) + (hat[2] + hat[3]) + hat[4]
    inverse = 1.0 / density
    return density, [hat[5 + k] * inverse for k in range(3)], hat[8] * inverse, [
        hat[s] * inverse for s in range(4)
    ]


def contractions(hat, density, momentum, favre_here, slopes):
    speed, thermal, fraction = favre_here
    deviator, magnitude = strain(slopes[:3])
    eddy = TEST_SQUARE * density * magnitude
    stress = [hat(STRESS + n) for n in range(5)] + [hat(LAST_STRESS)]
    sums = []
    top = bottom = None

    def add(total, value):
        return value if total is None else total + value

    off_top = off_bottom = None
    for n, (i, j) in enumerate(PAIR_INDEX):
        resolved = hat(PRODUCT + n) - momentum[i] * speed[j]
        model = stress[n] - eddy * deviator[n]
        if i == j:
            top, bottom = add(top, resolved * model), add(bottom, model * model)
        else:
            off_top, off_bottom = add(off_top, resolved * model), add(off_bottom, model * model)
    sums += [top + (off_top + off_top), bottom + (off_bottom + off_bottom)]
    top = bottom = None
    for d in range(3):
        resolved = hat(HEAT_FLUX + d) - momentum[d] * thermal
        model = hat(HEAT_SLOPE + d) - eddy * slopes[3][d]
        top, bottom = add(top, resolved * model), add(bottom, model * model)
    sums += [top, bottom]
    top = bottom = None
    for d in range(3):
        last_resolved = last_model = None
        for s in range(4):
            resolved = hat(MASS_FLUX + 3 * s + d) - momentum[d] * fraction[s]
            model = hat(MASS_SLOPE + 3 * s + d) - eddy * slopes[4 + s][d]
            last_resolved, last_model = add(last_resolved, resolved), add(last_model, model)
            top, bottom = add(top, resolved * model), add(bottom, model * model)
        top, bottom = top + last_resolved * last_model, bottom + last_model * last_model
    return sums + [top, bottom]


def filter_x(tile):
    pair = tile + shift_x(tile, -1)
    return pair + shift_x(pair, 1)


def slope_scale():
    bottom, top = level_edges()
    return jnp.where(bottom | top, 4.0, 2.0)


def model_kernel(
    own_ref, far_ref, near_ref, corner_own_ref,
    sum_ref, clamped_ref, tile_ref, state_ref, raw_ref,
    wide_ref, favre_ref,
):
    scale = slope_scale()
    gather_rows(own_ref, far_ref, near_ref, raw_ref)
    for row in range(STATE_ROWS):
        states = model_state([raw_ref[row + 1, field] for field in range(NF)])
        for k in range(STATE_COUNT):
            state_ref[row, k] = states[k]

    def grid_row(row, carry):
        def here(k):
            return state_ref[row + 1, k]

        slopes = []
        for k in range(SLOPED - 1):
            value = here(SPEED + k)
            along_x = shift_x(value, -1) - shift_x(value, 1)
            along_z = state_ref[row + 2, SPEED + k] - state_ref[row, SPEED + k]
            slopes.append((along_x, level_slope(value, scale), along_z))
        for k, tile in enumerate(grid_terms(here, slopes)):
            tile_ref[row, k] = tile
        hat = []
        for k in range(SPEED):
            total = (state_ref[row, k] + state_ref[row + 2, k]) + 2.0 * here(k)
            hat.append(filter_x(total))
        density, speed, thermal, fraction = favre(hat)
        for k, value in enumerate(speed + [thermal] + fraction):
            favre_ref[row, k] = value
        for k in range(3):
            wide_ref[row, k] = hat[MOMENTUM + k]
        wide_ref[row, 3] = density
        return carry

    lax.fori_loop(0, GRID_ROWS, grid_row, 0)
    for k in range(6):
        sum_ref[k] = jnp.zeros((TILE, LANES), F32)

    def test_row(zz, carry):
        row = zz + 1

        def hat(k):
            total = (tile_ref[row - 1, k] + tile_ref[row + 1, k]) + 2.0 * tile_ref[row, k]
            return filter_x(total)

        slopes = []
        for k in range(8):
            value = favre_ref[row, k]
            along_x = shift_x(value, -1) - shift_x(value, 1)
            along_z = favre_ref[row + 1, k] - favre_ref[row - 1, k]
            slopes.append((along_x, level_slope(value, scale), along_z))
        values = [favre_ref[row, k] for k in range(8)]
        sums = contractions(
            hat, wide_ref[row, 3], [wide_ref[row, k] for k in range(3)],
            (values[:3], values[3], values[4:]), slopes,
        )
        for k in range(6):
            sum_ref[k] = sum_ref[k] + sums[k]
        return carry

    lax.fori_loop(0, ROWS, test_row, 0)

    on_left = lanes() < 64
    place = lanes() & (SPAN - 1)
    place = jnp.where(on_left, place, SPAN - 1 - place)
    for field in range(NF):
        tile = clamped = corner_own_ref[field]
        for c in range(HALO):
            copied = jnp.where(on_left, shift_x(tile, c - HALO), shift_x(tile, HALO - c))
            clamped = jnp.where(place == c, copied, clamped)
        clamped_ref[field] = clamped


def corner_kernel(
    clamped_ref, got_one_ref, got_other_ref, sum_ref,
    totals_ref, corner_ref, tile_ref, speed_ref
):
    lane = lanes()
    even = is_even()
    scale = slope_scale()
    even_column = is_first_of_pair("gx")
    column = lax.axis_index("gx")
    first, last = column == 0, column == lax.axis_size("gx") - 1
    place = lane & (SPAN - 1)
    on_left = lane < 64
    low, high = jnp.where(first, 0, HALO), jnp.where(last, SPAN, SPAN - HALO)
    halo = (on_left & (place < low)) | (jnp.logical_not(on_left) & (place >= high))
    fields = []
    for field in range(NF):
        pair, second = divmod(field, 2)
        one, other = tile_of(got_one_ref, pair), tile_of(got_other_ref, pair)
        from_left = jnp.where(even_column, other, one)
        from_right = jnp.where(even_column, one, other)
        if second:
            got = shift_x(jnp.where(on_left, from_right, from_left), 64)
        else:
            got = jnp.where(on_left, from_left, from_right)
        fields.append(jnp.where(halo, got, clamped_ref[field]))
        corner_ref[field] = fields[field]
    state = model_state(fields)

    def slopes_of(value):
        along_x = shift_x(value, -1) - shift_x(value, 1)
        along_z = shift_x(value, -SPAN) - shift_x(value, SPAN)
        return along_x, level_slope(value, scale), along_z

    def filtered(value):
        pair = value + shift_x(value, -SPAN)
        return filter_x(pair + shift_x(pair, SPAN))

    tiles = grid_terms(lambda k: state[k], [slopes_of(state[SPEED + k]) for k in range(SLOPED - 1)])
    for k in range(STRESS, TILES):
        tile_ref[k] = tiles[k]
    for k in range(3):
        speed_ref[k] = state[SPEED + k]
    wide = [filtered(state[k]) for k in range(SPEED)]
    density, speed, thermal, fraction = favre(wide)
    sums = contractions(
        lambda k: filtered(tiles[k]), density, wide[MOMENTUM : MOMENTUM + 3],
        (speed, thermal, fraction), [slopes_of(value) for value in speed + [thermal] + fraction],
    )
    main_totals, corner_totals = [sum_ref[k] for k in range(6)], []
    for value in sums:
        value = value + shift_x(value, -SPAN)
        corner_totals.append(value + shift_x(value, -2 * SPAN))
    edges = jnp.zeros((TILE, LANES), F32)
    for k in range(3):
        packed = []
        for main, side in zip(main_totals[2 * k : 2 * k + 2], corner_totals[2 * k : 2 * k + 2]):
            main = jnp.where(lane < 2, shift_x(side, -19), main)
            main = jnp.where(lane >= LANES - 2, shift_x(side, 126 - 83), main)
            packed.append((main + shift_s(main, 1), side + shift_s(side, 1), main, side))
        top_main = shift_s(packed[0][0], -1) * (1.0 / 512.0)
        top_side = shift_s(packed[0][1], -1) * (1.0 / 512.0)
        totals_ref[pl.ds(k * TILE, TILE), :] = jnp.where(even, top_main, packed[1][0] * (1.0 / 1024.0))
        side = jnp.where(even, top_side, packed[1][1] * (1.0 / 1024.0))
        edges = jnp.where(lane == 2 * k, shift_x(side, 2 * k - 18), edges)
        edges = jnp.where(lane == 2 * k + 1, shift_x(side, 2 * k + 1 - 85), edges)
    totals_ref[pl.ds(3 * TILE, TILE), :] = edges


def term_kernel(tile_ref, state_ref, corner_ref, corner_speed_ref, terms_ref):
    lane = lanes()
    bottom, top = level_edges()

    def terms(place, d):
        speed = [state_ref[place + 1, SPEED + k] for k in range(3)]
        return subgrid_terms(lambda k: tile_ref[place, k], speed, d)

    corner_speed = [corner_speed_ref[k] for k in range(3)]
    corner = [subgrid_terms(lambda k: corner_ref[k], corner_speed, d) for d in range(3)]
    corner[2] = [shift_x(value, -SPAN) - shift_x(value, SPAN) for value in corner[2]]

    def patched(value, side, zz):
        value = jnp.where(lane == 0, shift_x(side, -19 - SPAN * zz), value)
        return jnp.where(lane == LANES - 1, shift_x(side, 43 - SPAN * zz), value)

    for zz in range(ROWS):
        row = zz + 1
        along_x, along_y = terms(row, 0), terms(row, 1)
        before, after = terms(row - 1, 2), terms(row + 1, 2)
        for n in range(TERMS):
            right = shift_x(corner[0][n], 42 - SPAN * zz)
            left = shift_x(corner[0][n], -18 - SPAN * zz)
            terms_ref[zz, n, 0] = jnp.where(lane >= LANES - 2, right, shift_x(along_x[n], -1))
            terms_ref[zz, n, 1] = jnp.where(lane < 2, left, shift_x(along_x[n], 1))
            terms_ref[zz, n, 2] = patched(after[n] - before[n], corner[2][n], zz)
            along = patched(along_y[n], corner[1][n], zz)
            terms_ref[zz, n, 3] = jnp.where(top, along, shift_s(along, -2))
            terms_ref[zz, n, 4] = jnp.where(bottom, -along, shift_s(along, 2))


def final_kernel(*refs, parts):
    part_refs = refs[:parts]
    base_ref, terms_ref, out_ref, coefficient_ref, scratch = refs[parts:]
    lane = lanes()
    even = is_even()
    bottom, top = level_edges()
    totals = [
        (tile_of(part_refs[0], k) + tile_of(part_refs[1], k))
        + (tile_of(part_refs[2], k) + tile_of(part_refs[3], k))
        for k in range(4)
    ]
    ratios = []
    for total in totals:
        total = total * (1.0 / (TILE * lax.axis_size("gz")))
        numerator = jnp.where(even, total, shift_s(total, 1))
        denominator = jnp.where(even, shift_s(total, -1), total)
        ratios.append(numerator / (denominator + RATIO_EPSILON))
    column = lax.axis_index("gx")
    first, last = column == 0, column == lax.axis_size("gx") - 1
    here, ahead, behind, above, below = [], [], [], [], []
    for k in range(3):
        ratio = ratios[k]
        scratch[...] = ratio
        coefficient_ref[k] = scratch[pl.ds(0, 4, stride=2), :]
        before = jnp.where(first, ratio, shift_x(ratios[3], -2 * k))
        after = jnp.where(last, ratio, shift_x(ratios[3], 127 - (2 * k + 1)))
        ratio = 0.25 * ratio
        here.append(ratio)
        ahead.append(jnp.where(lane == LANES - 1, 0.25 * after, shift_x(ratio, -1)))
        behind.append(jnp.where(lane == 0, 0.25 * before, shift_x(ratio, 1)))
        above.append(2.0 * jnp.where(top, ratio, shift_s(ratio, -2)))
        below.append(2.0 * jnp.where(bottom, ratio, shift_s(ratio, 2)))

    def row(zz, carry):
        sums = [tile_of(base_ref, field * ROWS + zz) for field in range(NF)]
        for n in range(TERMS):
            k = TERM_MODEL[n]
            change = (
                (ahead[k] * terms_ref[zz, n, 0] - behind[k] * terms_ref[zz, n, 1])
                + here[k] * terms_ref[zz, n, 2]
                + (above[k] * terms_ref[zz, n, 3] - below[k] * terms_ref[zz, n, 4])
            )
            sums[TERM_FIELD[n]] = sums[TERM_FIELD[n]] + change
        for field in range(NF):
            out_ref[pl.ds(field * 32 + zz, TILE, stride=4), :] = sums[field]
        return carry

    lax.fori_loop(0, ROWS, row, 0)


def call(kernel, out_shapes, scratch=(), inputs=0, final=False):
    shape_of = jax.ShapeDtypeStruct if final else pltpu.VMEM
    run = pl.pallas_call(
        kernel,
        out_shape=[shape_of(shape, F32) for shape in out_shapes],
        in_specs=[VMEM] * inputs,
        out_specs=[VMEM] * len(out_shapes),
        scratch_shapes=[pltpu.VMEM(shape, F32) for shape in scratch],
        compiler_params=SMALL,
    )

    def placed(*args):
        return run(*[pltpu.with_memory_space_constraint(arg, pltpu.VMEM) for arg in args])

    return placed


def body(constituent_mass, flow_speeds, thermal_pair, blowing_indicator):
    count_x = lax.axis_size("gx")
    count_z = lax.axis_size("gz")

    def swap(axis, count, near):
        step = [1, -1] if near else [-1, 1]
        return lambda value: lax.ppermute(
            value, axis, [(i, (i + step[i % 2]) % count) for i in range(count)]
        )

    arrays = [
        value.reshape(-1, LANES) for value in (constituent_mass, flow_speeds, thermal_pair)
    ]
    packed = (PACK_ROWS, LANES)
    rows = (GROUPS * TILE, LANES)
    fields = (NF, TILE, LANES)
    own, left, right, far, near, blown = pl.pallas_call(
        pack_kernel,
        out_shape=[
            pltpu.VMEM(shape, F32)
            for shape in (
                rows, packed, packed, (MESSAGE_ROWS, LANES), (MESSAGE_ROWS, LANES),
                (4 * TILE, LANES),
            )
        ],
        in_specs=[pl.BlockSpec(memory_space=pltpu.HBM)] * 4,
        out_specs=[VMEM] * 6,
        scratch_shapes=[
            pltpu.VMEM((NF * 4 * TILE, LANES), F32),
            pltpu.VMEM(blowing_indicator.shape, jnp.int32),
            pltpu.SemaphoreType.DMA((4,)),
        ],
        compiler_params=SMALL,
    )(*[
        pltpu.with_memory_space_constraint(value, pltpu.HBM)
        for value in arrays + [blowing_indicator]
    ])
    far = swap("gz", count_z, False)(far)
    near = swap("gz", count_z, True)(near)
    face, part = call(stream_kernel, [rows, rows], inputs=2)(own, blown)
    far, near, face, part = lax.optimization_barrier((far, near, face, part))

    corner, one, other = call(
        corner_pack_kernel,
        [fields, (PAIRS * TILE, LANES), (PAIRS * TILE, LANES)],
        inputs=4,
    )(left, right, far, near)
    got_one = swap("gx", count_x, True)(one)
    got_other = swap("gx", count_x, False)(other)
    sums, clamped, tiles, state, raw = call(
        model_kernel,
        [
            (6, TILE, LANES),
            fields,
            (GRID_ROWS, TILES, TILE, LANES),
            (STATE_ROWS, STATE_COUNT, TILE, LANES),
            (SPAN_TILES, NF, TILE, LANES),
        ],
        scratch=[(GRID_ROWS, 4, TILE, LANES), (GRID_ROWS, 8, TILE, LANES)],
        inputs=4,
    )(own, far, near, corner)
    got_one, got_other, sums = lax.optimization_barrier((got_one, got_other, sums))
    totals, corner, corner_tiles, corner_speed = call(
        corner_kernel,
        [(4 * TILE, LANES), fields, (TILES, TILE, LANES), (3, TILE, LANES)],
        inputs=4,
    )(clamped, got_one, got_other, sums)

    (terms,) = call(term_kernel, [(ROWS, TERMS, 5, TILE, LANES)], inputs=4)(
        tiles, state, corner_tiles, corner_speed
    )
    (part,) = call(ends_kernel, [rows], inputs=3)(corner, face, part)
    (base,) = call(
        span_kernel,
        [rows],
        scratch=[
            (SPAN_TILES, NF, TILE, LANES), (SPAN_TILES, NF, TILE, LANES), (SPAN_TILES, TILE, LANES),
        ],
        inputs=2,
    )(raw, part)

    def crossed(value, mask):
        return lax.ppermute(value, "gz", [(i, i ^ mask) for i in range(count_z)])

    totals = totals + crossed(totals, 1)
    reach = 2
    while count_z > 4 * reach:
        a, b, c = (crossed(totals, k * reach) for k in (1, 2, 3))
        totals = (totals + a) + (b + c)
        reach *= 4
    parts = [totals] + [
        crossed(totals, k * reach) if k * reach < count_z else jnp.zeros_like(totals)
        for k in (1, 2, 3)
    ]

    def final(*refs):
        final_kernel(*refs, parts=4)

    tendency, coefficients = call(
        final,
        [(NF * 32, LANES), (3, 4, LANES)],
        scratch=[(TILE, LANES)],
        inputs=6,
        final=True,
    )(*parts, base, terms)
    return tendency.reshape(NF, 4, TILE, LANES), coefficients


def solution(mesh):
    placed = (
        P(None, None, "gz", "gx"),
        P(None, None, "gz", "gx"),
        P(None, None, "gz", "gx"),
        P("gz", "gx"),
    )
    return jax.shard_map(
        body,
        mesh=mesh,
        in_specs=placed,
        out_specs=(P(None, None, "gz", "gx"), P(None, None, "gx")),
        check_vma=False,
    )
```

time: 27.4 us -> 26.2 us (0.956)
  waiting for transfers between devices: 5.8 us -> 4.34 us
  starting transfers between devices: 12.6 us -> 13 us
    ppermute x4, starting transfers between devices: 7.6 us -> 8.52 us  [swap(): lax.ppermute(value, axis, [(i, (i + step[i % 2]) % count) for i in range(...]
    ppermute x4, waiting for transfers between devices: 2.97 us -> 2.2 us  [crossed(): return lax.ppermute(value, 'gz', [(i, i ^ mask) for i in range(count_z)])]
    ppermute x4, waiting for transfers between devices: 2.83 us -> 2.13 us  [swap(): lax.ppermute(value, axis, [(i, (i + step[i % 2]) % count) for i in range(...]
    ppermute x4, starting transfers between devices: 4.98 us -> 4.46 us  [crossed(): return lax.ppermute(value, 'gz', [(i, i ^ mask) for i in range(count_z)])]
    pallas_call x6 -> x8, Pallas kernels: 7.01 us -> 6.92 us  [placed(): run(*[pltpu.with_memory_space_constraint(arg, pltpu.VMEM) for arg in args])]
  transfers between devices with their start and end apart: 8 -> 8, of which waited for: 5 -> 4; matrix products, arithmetic and copies ran while one was open for 0% -> 0% of each run, Pallas kernels for 12% -> 20%
where the time goes in v3:
time: 26.2 us; the launch traced here: 26 us
  starting transfers between devices  13 us (50%)
  Pallas kernels  8 us (31%)
  waiting for transfers between devices  4.34 us (17%)
  between operations  0.72 us (3%)
    ppermute x4, starting transfers between devices, swap(): lax.ppermute(value, axis, [(i, (i + step[i % 2]) % count) for i in range(...  8.52 us
    pallas_call x8, Pallas kernels, placed(): run(*[pltpu.with_memory_space_constraint(arg, pltpu.VMEM) for arg in args])  6.92 us
    ppermute x4, starting transfers between devices, crossed(): return lax.ppermute(value, 'gz', [(i, i ^ mask) for i in range(count_z)])  4.46 us
    ppermute x4, waiting for transfers between devices, crossed(): return lax.ppermute(value, 'gz', [(i, i ^ mask) for i in range(count_z)])  2.2 us
    ppermute x4, waiting for transfers between devices, swap(): lax.ppermute(value, axis, [(i, (i + step[i % 2]) % count) for i in range(...  2.13 us
    pallas_call x1, Pallas kernels, body(): pl.pallas_call(pack_kernel, out_shape=[pltpu.VMEM(shape, F32) for shape i...  1.08 us
  transfers between devices with their start and end apart: 8, of which 4 were waited for; matrix products, arithmetic and copies ran while one was open for 0% of the time, Pallas kernels for 20%

profile of v3, /device:TPU:0, one launch (start us, length us, event | category | flops | bytes accessed | tf_op | source)
XLA Modules:
  0.0 26.0 jit_solution(14071422059074223018)
XLA Ops:
  0.6 1.1 %shard_map.59 = (f32[320,128]{1,0:T(8,128)S(1)}, f32[24,128]{1,0:T(8,128)S(1)}, f32[24,128]{1,0:T(8,128)S(1)}, f32[144,128]{1,0:T(8,128)S(1)}, f32[144,128]{1,0:T(8,128)S(1)}, /*index=5*/f32[32,128]{1,0:T(8,128)S(1)}) custom-call(f32[160,128]{1,0:T(8,128)} %bitcast.4, f32[96,128]{1,0:T(8,128)} %bitcast.5, f32[64,128]{1,0:T(8,128)} %bitcast.6, s32[8,128]{1,0:T(8,128)} %blow_hbm.1), custom_call_target="tpu_custom_call" | custom-call | tf_op jit(solution)/shard_map/pallas_call | solution.py:746
  1.7 4.6 %collective-permute-start = (f32[144,128]{1,0:T(8,128)S(1)}, f32[144,128]{1,0:T(8,128)S(1)}, u32[]{:S(2)}, u32[]{:S(2)}) collective-permute-start(f32[144,128]{1,0:T(8,128)S(1)} %get-tuple-element.32), channel_id=1, source_target_pairs={{0,7},{1,2},{2,1},{3,4},{4,3},{5,6},{6,5},{7,0},{8,15},{9,10},{10,... | collective-permute-start | bytes 221192 | tf_op jit(solution)/shard_map/ppermute | solution.py:736
  6.3 0.0 collective-permute-start.1
  6.3 1.2 %shard_map.60 = (f32[320,128]{1,0:T(8,128)S(1)}, f32[320,128]{1,0:T(8,128)S(1)}) custom-call(f32[320,128]{1,0:T(8,128)S(1)} %get-tuple-element.31.own_ref, f32[32,128]{1,0:T(8,128)S(1)} %get-tuple-element.34.blow_rows), custom_call_target="tpu_custom_call" | custom-call | tf_op jit(solution)/shard_map/pallas_call | solution.py:725
  7.5 0.9 %collective-permute-done.far_ref = f32[144,128]{1,0:T(8,128)S(1)} collective-permute-done((f32[144,128]{1,0:T(8,128)S(1)}, f32[144,128]{1,0:T(8,128)S(1)}, u32[]{:S(2)}, u32[]{:S(2)}) %collective-permute-start) | collective-permute-done | bytes 73760 | tf_op jit(solution)/shard_map/ppermute | solution.py:736
  8.4 0.0 collective-permute-done.1.near_ref
  8.4 0.2 shard_map.61
  8.6 2.5 %collective-permute-start.2 = (f32[40,128]{1,0:T(8,128)S(1)}, f32[40,128]{1,0:T(8,128)S(1)}, u32[]{:S(2)}, u32[]{:S(2)}) collective-permute-start(f32[40,128]{1,0:T(8,128)S(1)} %get-tuple-element.43), channel_id=1, source_target_pairs={{0,8},{8,0},{16,24},{24,16},{1,9},{9,1},{17,25},{25,17},{2,10},{10... | collective-permute-start | bytes 61448 | tf_op jit(solution)/shard_map/ppermute | solution.py:736
  11.1 1.5 %collective-permute-start.3 = (f32[40,128]{1,0:T(8,128)S(1)}, f32[40,128]{1,0:T(8,128)S(1)}, u32[]{:S(2)}, u32[]{:S(2)}) collective-permute-start(f32[40,128]{1,0:T(8,128)S(1)} %get-tuple-element.44), channel_id=1, source_target_pairs={{0,24},{8,16},{16,8},{24,0},{1,25},{9,17},{17,9},{25,1},{2,26},{10... | collective-permute-start | bytes 61448 | tf_op jit(solution)/shard_map/ppermute | solution.py:736
  12.6 2.0 %shard_map.62 = (f32[6,8,128]{2,1,0:T(8,128)S(1)}, f32[10,8,128]{2,1,0:T(8,128)S(1)}, f32[6,45,8,128]{3,2,1,0:T(8,128)S(1)}, f32[8,20,8,128]{3,2,1,0:T(8,128)S(1)}, f32[10,10,8,128]{3,2,1,0:T(8,128)S(1)}) custom-call(f32[320,128]{1,0:T(8,128)S(1)} %get-tuple-element.31.own_ref, f32[144,128]{1,0:T(8,128)S(1)} %collective-permute-done.far_ref, ...), custom_call_target="tpu_custom_call" | custom-call | tf_op jit(solution)/shard_map/pallas_call | solution.py:725
  14.6 0.0 collective-permute-done.2.got_one_ref
  14.6 1.2 %collective-permute-done.3.got_other_ref = f32[40,128]{1,0:T(8,128)S(1)} collective-permute-done((f32[40,128]{1,0:T(8,128)S(1)}, f32[40,128]{1,0:T(8,128)S(1)}, u32[]{:S(2)}, u32[]{:S(2)}) %collective-permute-start.3) | collective-permute-done | bytes 20512 | tf_op jit(solution)/shard_map/ppermute | solution.py:736
  15.8 0.7 %shard_map.63 = (f32[32,128]{1,0:T(8,128)S(1)}, f32[10,8,128]{2,1,0:T(8,128)S(1)}, f32[45,8,128]{2,1,0:T(8,128)S(1)}, f32[3,8,128]{2,1,0:T(8,128)S(1)}) custom-call(f32[10,8,128]{2,1,0:T(8,128)S(1)} %get-tuple-element.42.clamped_ref, f32[40,128]{1,0:T(8,128)S(1)} %collective-permute-done.2.got_one_ref, f32[40,128]{1,0:T(8,128)S(1)} %collective-permute-done.3.got_other_ref, ...), custom_call_target="tpu_custom_call" | custom-call | tf_op jit(solution)/shard_map/pallas_call | solution.py:725
  16.5 0.1 collective-permute-start.4
  16.6 1.2 %collective-permute-done.4 = f32[32,128]{1,0:T(8,128)S(1)} collective-permute-done((f32[32,128]{1,0:T(8,128)S(1)}, f32[32,128]{1,0:T(8,128)S(1)}, u32[]{:S(2)}, u32[]{:S(2)}) %collective-permute-start.4) | collective-permute-done | bytes 16416 | tf_op jit(solution)/shard_map/ppermute | solution.py:812
  17.8 0.0 collective-permute-start.5
  17.8 1.8 %collective-permute-start.6 = (f32[32,128]{1,0:T(8,128)S(1)}, f32[32,128]{1,0:T(8,128)S(1)}, u32[]{:S(2)}, u32[]{:S(2)}) collective-permute-start(f32[32,128]{1,0:T(8,128)S(1)} %add.3.refs_0_), channel_id=1, source_target_pairs={{0,4},{1,5},{2,6},{3,7},{4,0},{5,1},{6,2},{7,3},{8,12},{9,13},{10,... | collective-permute-start | bytes 49160 | tf_op jit(solution)/shard_map/ppermute | solution.py:812
  19.6 2.5 %collective-permute-start.7 = (f32[32,128]{1,0:T(8,128)S(1)}, f32[32,128]{1,0:T(8,128)S(1)}, u32[]{:S(2)}, u32[]{:S(2)}) collective-permute-start(f32[32,128]{1,0:T(8,128)S(1)} %add.3.refs_0_), channel_id=1, source_target_pairs={{0,6},{1,7},{2,4},{3,5},{4,2},{5,3},{6,0},{7,1},{8,14},{9,15},{10,... | collective-permute-start | bytes 49160 | tf_op jit(solution)/shard_map/ppermute | solution.py:812
  22.2 0.5 %shard_map.64.part_ref = f32[320,128]{1,0:T(8,128)S(1)} custom-call(f32[10,8,128]{2,1,0:T(8,128)S(1)} %get-tuple-element.51.corner_ref, f32[320,128]{1,0:T(8,128)S(1)} %get-tuple-element.52.face_ref, f32[320,128]{1,0:T(8,128)S(1)} %get-tuple-element.53.part_ref), custom_call_target="tpu_custom_call" | custom-call | tf_op jit(solution)/shard_map/pallas_call | solution.py:725
  22.7 0.9 %shard_map.65.refs_4_ = f32[320,128]{1,0:T(8,128)S(1)} custom-call(f32[10,10,8,128]{3,2,1,0:T(8,128)S(1)} %get-tuple-element.50.raw_ref, f32[320,128]{1,0:T(8,128)S(1)} %shard_map.64.part_ref), custom_call_target="tpu_custom_call" | custom-call | tf_op jit(solution)/shard_map/pallas_call | solution.py:725
  23.6 0.5 %shard_map.66.refs_5_ = f32[4,12,5,8,128]{4,3,2,1,0:T(8,128)S(1)} custom-call(f32[6,45,8,128]{3,2,1,0:T(8,128)S(1)} %get-tuple-element.54.tile_ref, f32[8,20,8,128]{3,2,1,0:T(8,128)S(1)} %get-tuple-element.55.state_ref, f32[45,8,128]{2,1,0:T(8,128)S(1)} %get-tuple-element.56.corner_ref, f32[3,8,128]{2,1,0:T(8,128)S(1)} %get-tuple-element.57.corner_speed_ref), custom_call_target="tpu_custom_call" | custom-call | tf_op jit(solution)/shard_map/pallas_call | solution.py:725
  24.1 0.0 collective-permute-done.5.refs_1_
  24.1 0.0 collective-permute-done.6.refs_2_
  24.2 1.0 %collective-permute-done.7.refs_3_ = f32[32,128]{1,0:T(8,128)S(1)} collective-permute-done((f32[32,128]{1,0:T(8,128)S(1)}, f32[32,128]{1,0:T(8,128)S(1)}, u32[]{:S(2)}, u32[]{:S(2)}) %collective-permute-start.7) | collective-permute-done | bytes 16416 | tf_op jit(solution)/shard_map/ppermute | solution.py:812
  25.2 0.9 %shard_map.67 = (f32[320,128]{1,0:T(8,128)}, f32[3,4,128]{2,1,0:T(4,128)}) custom-call(f32[32,128]{1,0:T(8,128)S(1)} %add.3.refs_0_, f32[32,128]{1,0:T(8,128)S(1)} %collective-permute-done.5.refs_1_, f32[32,128]{1,0:T(8,128)S(1)} %collective-permute-done.6.refs_2_, f32[32,128]{1,0:T(8,128)S(1)} %collective-permute-done.7.refs_3_, ...), custom_call_target="tpu_custom_call" | custom-call | tf_op jit(solution)/shard_map/pallas_call | solution.py:725
  (1 shorter events, 0.0 us)
Async XLA Ops:
  1.7 6.7 %collective-permute-start = (f32[144,128]{1,0:T(8,128)S(1)}, f32[144,128]{1,0:T(8,128)S(1)}, u32[]{:S(2)}, u32[]{:S(2)}) collective-permute-start(f32[144,128]{1,0:T(8,128)S(1)} %get-tuple-element.32), channel_id=1, source_target_pairs={{0,7},{1,2},{2,1},{3,4},{4,3},{5,6},{6,5},{7,0},{8,15},{9,10},{10,... | collective-permute-start | bytes 221192 | tf_op jit(solution)/shard_map/ppermute | solution.py:736
  6.3 2.1 %collective-permute-start.1 = (f32[144,128]{1,0:T(8,128)S(1)}, f32[144,128]{1,0:T(8,128)S(1)}, u32[]{:S(2)}, u32[]{:S(2)}) collective-permute-start(f32[144,128]{1,0:T(8,128)S(1)} %get-tuple-element.33), channel_id=1, source_target_pairs={{0,1},{1,0},{2,3},{3,2},{4,5},{5,4},{6,7},{7,6},{8,9},{9,8},{10,11... | collective-permute-start | bytes 221192 | tf_op jit(solution)/shard_map/ppermute | solution.py:736
  8.6 5.9 %collective-permute-start.2 = (f32[40,128]{1,0:T(8,128)S(1)}, f32[40,128]{1,0:T(8,128)S(1)}, u32[]{:S(2)}, u32[]{:S(2)}) collective-permute-start(f32[40,128]{1,0:T(8,128)S(1)} %get-tuple-element.43), channel_id=1, source_target_pairs={{0,8},{8,0},{16,24},{24,16},{1,9},{9,1},{17,25},{25,17},{2,10},{10... | collective-permute-start | bytes 61448 | tf_op jit(solution)/shard_map/ppermute | solution.py:736
  11.1 4.7 %collective-permute-start.3 = (f32[40,128]{1,0:T(8,128)S(1)}, f32[40,128]{1,0:T(8,128)S(1)}, u32[]{:S(2)}, u32[]{:S(2)}) collective-permute-start(f32[40,128]{1,0:T(8,128)S(1)} %get-tuple-element.44), channel_id=1, source_target_pairs={{0,24},{8,16},{16,8},{24,0},{1,25},{9,17},{17,9},{25,1},{2,26},{10... | collective-permute-start | bytes 61448 | tf_op jit(solution)/shard_map/ppermute | solution.py:736
  16.5 1.2 %collective-permute-start.4 = (f32[32,128]{1,0:T(8,128)S(1)}, f32[32,128]{1,0:T(8,128)S(1)}, u32[]{:S(2)}, u32[]{:S(2)}) collective-permute-start(f32[32,128]{1,0:T(8,128)S(1)} %get-tuple-element.49), channel_id=1, source_target_pairs={{0,1},{1,0},{2,3},{3,2},{4,5},{5,4},{6,7},{7,6},{8,9},{9,8},{10,11... | collective-permute-start | bytes 49160 | tf_op jit(solution)/shard_map/ppermute | solution.py:812
  17.8 6.3 %collective-permute-start.5 = (f32[32,128]{1,0:T(8,128)S(1)}, f32[32,128]{1,0:T(8,128)S(1)}, u32[]{:S(2)}, u32[]{:S(2)}) collective-permute-start(f32[32,128]{1,0:T(8,128)S(1)} %add.3.refs_0_), channel_id=1, source_target_pairs={{0,2},{1,3},{2,0},{3,1},{4,6},{5,7},{6,4},{7,5},{8,10},{9,11},{10,... | collective-permute-start | bytes 49160 | tf_op jit(solution)/shard_map/ppermute | solution.py:812
  17.8 6.3 %collective-permute-start.6 = (f32[32,128]{1,0:T(8,128)S(1)}, f32[32,128]{1,0:T(8,128)S(1)}, u32[]{:S(2)}, u32[]{:S(2)}) collective-permute-start(f32[32,128]{1,0:T(8,128)S(1)} %add.3.refs_0_), channel_id=1, source_target_pairs={{0,4},{1,5},{2,6},{3,7},{4,0},{5,1},{6,2},{7,3},{8,12},{9,13},{10,... | collective-permute-start | bytes 49160 | tf_op jit(solution)/shard_map/ppermute | solution.py:812
  19.6 5.5 %collective-permute-start.7 = (f32[32,128]{1,0:T(8,128)S(1)}, f32[32,128]{1,0:T(8,128)S(1)}, u32[]{:S(2)}, u32[]{:S(2)}) collective-permute-start(f32[32,128]{1,0:T(8,128)S(1)} %add.3.refs_0_), channel_id=1, source_target_pairs={{0,6},{1,7},{2,4},{3,5},{4,2},{5,3},{6,0},{7,1},{8,14},{9,15},{10,... | collective-permute-start | bytes 49160 | tf_op jit(solution)/shard_map/ppermute | solution.py:812

commit v4 on v3

--- a/solution.py
+++ b/solution.py
@@ -819,7 +819,7 @@
         reach *= 4
     parts = [totals] + [
         crossed(totals, k * reach) if k * reach < count_z else jnp.zeros_like(totals)
-        for k in (1, 2, 3)
+        for k in (2, 3, 1)
     ]
 
     def final(*refs):

time: 26.2 us -> 24.6 us (0.939)
  starting transfers between devices: 13 us -> 12.1 us
  waiting for transfers between devices: 4.34 us -> 3.69 us
    ppermute x4, starting transfers between devices: 4.46 us -> 3.56 us  [crossed(): return lax.ppermute(value, 'gz', [(i, i ^ mask) for i in range(count_z)])]
    ppermute x4, waiting for transfers between devices: 2.2 us -> 1.56 us  [crossed(): return lax.ppermute(value, 'gz', [(i, i ^ mask) for i in range(count_z)])]
  transfers between devices with their start and end apart: 8 -> 8, of which waited for: 4 -> 4; matrix products, arithmetic and copies ran while one was open for 0% -> 0% of each run, Pallas kernels for 20% -> 21%
where the time goes in v4:
time: 24.6 us; the launch traced here: 24.5 us
  starting transfers between devices  12.1 us (49%)
  Pallas kernels  8 us (33%)
  waiting for transfers between devices  3.69 us (15%)
  between operations  0.71 us (3%)
    ppermute x4, starting transfers between devices, swap(): lax.ppermute(value, axis, [(i, (i + step[i % 2]) % count) for i in range(...  8.52 us
    pallas_call x8, Pallas kernels, placed(): run(*[pltpu.with_memory_space_constraint(arg, pltpu.VMEM) for arg in args])  6.92 us
    ppermute x4, starting transfers between devices, crossed(): return lax.ppermute(value, 'gz', [(i, i ^ mask) for i in range(count_z)])  3.56 us
    ppermute x4, waiting for transfers between devices, swap(): lax.ppermute(value, axis, [(i, (i + step[i % 2]) % count) for i in range(...  2.13 us
    ppermute x4, waiting for transfers between devices, crossed(): return lax.ppermute(value, 'gz', [(i, i ^ mask) for i in range(count_z)])  1.56 us
    pallas_call x1, Pallas kernels, body(): pl.pallas_call(pack_kernel, out_shape=[pltpu.VMEM(shape, F32) for shape i...  1.08 us
  transfers between devices with their start and end apart: 8, of which 4 were waited for; matrix products, arithmetic and copies ran while one was open for 0% of the time, Pallas kernels for 21%

profile of v4, /device:TPU:0, one launch (start us, length us, event | category | flops | bytes accessed | tf_op | source)
XLA Modules:
  0.0 24.5 jit_solution(7136303992933845976)
XLA Ops:
  0.6 1.1 %shard_map.59 = (f32[320,128]{1,0:T(8,128)S(1)}, f32[24,128]{1,0:T(8,128)S(1)}, f32[24,128]{1,0:T(8,128)S(1)}, f32[144,128]{1,0:T(8,128)S(1)}, f32[144,128]{1,0:T(8,128)S(1)}, /*index=5*/f32[32,128]{1,0:T(8,128)S(1)}) custom-call(f32[160,128]{1,0:T(8,128)} %bitcast.4, f32[96,128]{1,0:T(8,128)} %bitcast.5, f32[64,128]{1,0:T(8,128)} %bitcast.6, s32[8,128]{1,0:T(8,128)} %blow_hbm.1), custom_call_target="tpu_custom_call" | custom-call | tf_op jit(solution)/shard_map/pallas_call | solution.py:746
  1.7 4.6 %collective-permute-start = (f32[144,128]{1,0:T(8,128)S(1)}, f32[144,128]{1,0:T(8,128)S(1)}, u32[]{:S(2)}, u32[]{:S(2)}) collective-permute-start(f32[144,128]{1,0:T(8,128)S(1)} %get-tuple-element.32), channel_id=1, source_target_pairs={{0,7},{1,2},{2,1},{3,4},{4,3},{5,6},{6,5},{7,0},{8,15},{9,10},{10,... | collective-permute-start | bytes 221192 | tf_op jit(solution)/shard_map/ppermute | solution.py:736
  6.3 0.0 collective-permute-start.1
  6.3 1.2 %shard_map.60 = (f32[320,128]{1,0:T(8,128)S(1)}, f32[320,128]{1,0:T(8,128)S(1)}) custom-call(f32[320,128]{1,0:T(8,128)S(1)} %get-tuple-element.31.own_ref, f32[32,128]{1,0:T(8,128)S(1)} %get-tuple-element.34.blow_rows), custom_call_target="tpu_custom_call" | custom-call | tf_op jit(solution)/shard_map/pallas_call | solution.py:725
  7.5 0.9 %collective-permute-done.far_ref = f32[144,128]{1,0:T(8,128)S(1)} collective-permute-done((f32[144,128]{1,0:T(8,128)S(1)}, f32[144,128]{1,0:T(8,128)S(1)}, u32[]{:S(2)}, u32[]{:S(2)}) %collective-permute-start) | collective-permute-done | bytes 73760 | tf_op jit(solution)/shard_map/ppermute | solution.py:736
  8.4 0.0 collective-permute-done.1.near_ref
  8.4 0.2 shard_map.61
  8.6 2.5 %collective-permute-start.2 = (f32[40,128]{1,0:T(8,128)S(1)}, f32[40,128]{1,0:T(8,128)S(1)}, u32[]{:S(2)}, u32[]{:S(2)}) collective-permute-start(f32[40,128]{1,0:T(8,128)S(1)} %get-tuple-element.43), channel_id=1, source_target_pairs={{0,8},{8,0},{16,24},{24,16},{1,9},{9,1},{17,25},{25,17},{2,10},{10... | collective-permute-start | bytes 61448 | tf_op jit(solution)/shard_map/ppermute | solution.py:736
  11.1 1.5 %collective-permute-start.3 = (f32[40,128]{1,0:T(8,128)S(1)}, f32[40,128]{1,0:T(8,128)S(1)}, u32[]{:S(2)}, u32[]{:S(2)}) collective-permute-start(f32[40,128]{1,0:T(8,128)S(1)} %get-tuple-element.44), channel_id=1, source_target_pairs={{0,24},{8,16},{16,8},{24,0},{1,25},{9,17},{17,9},{25,1},{2,26},{10... | collective-permute-start | bytes 61448 | tf_op jit(solution)/shard_map/ppermute | solution.py:736
  12.6 2.0 %shard_map.62 = (f32[6,8,128]{2,1,0:T(8,128)S(1)}, f32[10,8,128]{2,1,0:T(8,128)S(1)}, f32[6,45,8,128]{3,2,1,0:T(8,128)S(1)}, f32[8,20,8,128]{3,2,1,0:T(8,128)S(1)}, f32[10,10,8,128]{3,2,1,0:T(8,128)S(1)}) custom-call(f32[320,128]{1,0:T(8,128)S(1)} %get-tuple-element.31.own_ref, f32[144,128]{1,0:T(8,128)S(1)} %collective-permute-done.far_ref, ...), custom_call_target="tpu_custom_call" | custom-call | tf_op jit(solution)/shard_map/pallas_call | solution.py:725
  14.6 0.0 collective-permute-done.2.got_one_ref
  14.6 1.2 %collective-permute-done.3.got_other_ref = f32[40,128]{1,0:T(8,128)S(1)} collective-permute-done((f32[40,128]{1,0:T(8,128)S(1)}, f32[40,128]{1,0:T(8,128)S(1)}, u32[]{:S(2)}, u32[]{:S(2)}) %collective-permute-start.3) | collective-permute-done | bytes 20512 | tf_op jit(solution)/shard_map/ppermute | solution.py:736
  15.8 0.7 %shard_map.63 = (f32[32,128]{1,0:T(8,128)S(1)}, f32[10,8,128]{2,1,0:T(8,128)S(1)}, f32[45,8,128]{2,1,0:T(8,128)S(1)}, f32[3,8,128]{2,1,0:T(8,128)S(1)}) custom-call(f32[10,8,128]{2,1,0:T(8,128)S(1)} %get-tuple-element.42.clamped_ref, f32[40,128]{1,0:T(8,128)S(1)} %collective-permute-done.2.got_one_ref, f32[40,128]{1,0:T(8,128)S(1)} %collective-permute-done.3.got_other_ref, ...), custom_call_target="tpu_custom_call" | custom-call | tf_op jit(solution)/shard_map/pallas_call | solution.py:725
  16.5 0.1 collective-permute-start.4
  16.6 1.2 %collective-permute-done.4 = f32[32,128]{1,0:T(8,128)S(1)} collective-permute-done((f32[32,128]{1,0:T(8,128)S(1)}, f32[32,128]{1,0:T(8,128)S(1)}, u32[]{:S(2)}, u32[]{:S(2)}) %collective-permute-start.4) | collective-permute-done | bytes 16416 | tf_op jit(solution)/shard_map/ppermute | solution.py:812
  17.8 0.3 %collective-permute-start.5 = (f32[32,128]{1,0:T(8,128)S(1)}, f32[32,128]{1,0:T(8,128)S(1)}, u32[]{:S(2)}, u32[]{:S(2)}) collective-permute-start(f32[32,128]{1,0:T(8,128)S(1)} %add.3.refs_0_), channel_id=1, source_target_pairs={{0,4},{1,5},{2,6},{3,7},{4,0},{5,1},{6,2},{7,3},{8,12},{9,13},{10,... | collective-permute-start | bytes 49160 | tf_op jit(solution)/shard_map/ppermute | solution.py:812
  18.1 1.3 %collective-permute-start.6 = (f32[32,128]{1,0:T(8,128)S(1)}, f32[32,128]{1,0:T(8,128)S(1)}, u32[]{:S(2)}, u32[]{:S(2)}) collective-permute-start(f32[32,128]{1,0:T(8,128)S(1)} %add.3.refs_0_), channel_id=1, source_target_pairs={{0,6},{1,7},{2,4},{3,5},{4,2},{5,3},{6,0},{7,1},{8,14},{9,15},{10,... | collective-permute-start | bytes 49160 | tf_op jit(solution)/shard_map/ppermute | solution.py:812
  19.4 1.9 %collective-permute-start.7 = (f32[32,128]{1,0:T(8,128)S(1)}, f32[32,128]{1,0:T(8,128)S(1)}, u32[]{:S(2)}, u32[]{:S(2)}) collective-permute-start(f32[32,128]{1,0:T(8,128)S(1)} %add.3.refs_0_), channel_id=1, source_target_pairs={{0,2},{1,3},{2,0},{3,1},{4,6},{5,7},{6,4},{7,5},{8,10},{9,11},{10,... | collective-permute-start | bytes 49160 | tf_op jit(solution)/shard_map/ppermute | solution.py:812
  21.3 0.5 %shard_map.64.part_ref = f32[320,128]{1,0:T(8,128)S(1)} custom-call(f32[10,8,128]{2,1,0:T(8,128)S(1)} %get-tuple-element.51.corner_ref, f32[320,128]{1,0:T(8,128)S(1)} %get-tuple-element.52.face_ref, f32[320,128]{1,0:T(8,128)S(1)} %get-tuple-element.53.part_ref), custom_call_target="tpu_custom_call" | custom-call | tf_op jit(solution)/shard_map/pallas_call | solution.py:725
  21.8 0.9 %shard_map.65.refs_4_ = f32[320,128]{1,0:T(8,128)S(1)} custom-call(f32[10,10,8,128]{3,2,1,0:T(8,128)S(1)} %get-tuple-element.50.raw_ref, f32[320,128]{1,0:T(8,128)S(1)} %shard_map.64.part_ref), custom_call_target="tpu_custom_call" | custom-call | tf_op jit(solution)/shard_map/pallas_call | solution.py:725
  22.7 0.5 %shard_map.66.refs_5_ = f32[4,12,5,8,128]{4,3,2,1,0:T(8,128)S(1)} custom-call(f32[6,45,8,128]{3,2,1,0:T(8,128)S(1)} %get-tuple-element.54.tile_ref, f32[8,20,8,128]{3,2,1,0:T(8,128)S(1)} %get-tuple-element.55.state_ref, f32[45,8,128]{2,1,0:T(8,128)S(1)} %get-tuple-element.56.corner_ref, f32[3,8,128]{2,1,0:T(8,128)S(1)} %get-tuple-element.57.corner_speed_ref), custom_call_target="tpu_custom_call" | custom-call | tf_op jit(solution)/shard_map/pallas_call | solution.py:725
  23.2 0.0 collective-permute-done.5.refs_1_
  23.2 0.4 %collective-permute-done.6.refs_2_ = f32[32,128]{1,0:T(8,128)S(1)} collective-permute-done((f32[32,128]{1,0:T(8,128)S(1)}, f32[32,128]{1,0:T(8,128)S(1)}, u32[]{:S(2)}, u32[]{:S(2)}) %collective-permute-start.6) | collective-permute-done | bytes 16416 | tf_op jit(solution)/shard_map/ppermute | solution.py:812
  23.6 0.0 collective-permute-done.7.refs_3_
  23.6 0.9 %shard_map.67 = (f32[320,128]{1,0:T(8,128)}, f32[3,4,128]{2,1,0:T(4,128)}) custom-call(f32[32,128]{1,0:T(8,128)S(1)} %add.3.refs_0_, f32[32,128]{1,0:T(8,128)S(1)} %collective-permute-done.5.refs_1_, f32[32,128]{1,0:T(8,128)S(1)} %collective-permute-done.6.refs_2_, f32[32,128]{1,0:T(8,128)S(1)} %collective-permute-done.7.refs_3_, ...), custom_call_target="tpu_custom_call" | custom-call | tf_op jit(solution)/shard_map/pallas_call | solution.py:725
  (1 shorter events, 0.0 us)
Async XLA Ops:
  1.7 6.7 %collective-permute-start = (f32[144,128]{1,0:T(8,128)S(1)}, f32[144,128]{1,0:T(8,128)S(1)}, u32[]{:S(2)}, u32[]{:S(2)}) collective-permute-start(f32[144,128]{1,0:T(8,128)S(1)} %get-tuple-element.32), channel_id=1, source_target_pairs={{0,7},{1,2},{2,1},{3,4},{4,3},{5,6},{6,5},{7,0},{8,15},{9,10},{10,... | collective-permute-start | bytes 221192 | tf_op jit(solution)/shard_map/ppermute | solution.py:736
  6.3 2.1 %collective-permute-start.1 = (f32[144,128]{1,0:T(8,128)S(1)}, f32[144,128]{1,0:T(8,128)S(1)}, u32[]{:S(2)}, u32[]{:S(2)}) collective-permute-start(f32[144,128]{1,0:T(8,128)S(1)} %get-tuple-element.33), channel_id=1, source_target_pairs={{0,1},{1,0},{2,3},{3,2},{4,5},{5,4},{6,7},{7,6},{8,9},{9,8},{10,11... | collective-permute-start | bytes 221192 | tf_op jit(solution)/shard_map/ppermute | solution.py:736
  8.6 5.9 %collective-permute-start.2 = (f32[40,128]{1,0:T(8,128)S(1)}, f32[40,128]{1,0:T(8,128)S(1)}, u32[]{:S(2)}, u32[]{:S(2)}) collective-permute-start(f32[40,128]{1,0:T(8,128)S(1)} %get-tuple-element.43), channel_id=1, source_target_pairs={{0,8},{8,0},{16,24},{24,16},{1,9},{9,1},{17,25},{25,17},{2,10},{10... | collective-permute-start | bytes 61448 | tf_op jit(solution)/shard_map/ppermute | solution.py:736
  11.1 4.7 %collective-permute-start.3 = (f32[40,128]{1,0:T(8,128)S(1)}, f32[40,128]{1,0:T(8,128)S(1)}, u32[]{:S(2)}, u32[]{:S(2)}) collective-permute-start(f32[40,128]{1,0:T(8,128)S(1)} %get-tuple-element.44), channel_id=1, source_target_pairs={{0,24},{8,16},{16,8},{24,0},{1,25},{9,17},{17,9},{25,1},{2,26},{10... | collective-permute-start | bytes 61448 | tf_op jit(solution)/shard_map/ppermute | solution.py:736
  16.5 1.2 %collective-permute-start.4 = (f32[32,128]{1,0:T(8,128)S(1)}, f32[32,128]{1,0:T(8,128)S(1)}, u32[]{:S(2)}, u32[]{:S(2)}) collective-permute-start(f32[32,128]{1,0:T(8,128)S(1)} %get-tuple-element.49), channel_id=1, source_target_pairs={{0,1},{1,0},{2,3},{3,2},{4,5},{5,4},{6,7},{7,6},{8,9},{9,8},{10,11... | collective-permute-start | bytes 49160 | tf_op jit(solution)/shard_map/ppermute | solution.py:812
  17.8 5.4 %collective-permute-start.5 = (f32[32,128]{1,0:T(8,128)S(1)}, f32[32,128]{1,0:T(8,128)S(1)}, u32[]{:S(2)}, u32[]{:S(2)}) collective-permute-start(f32[32,128]{1,0:T(8,128)S(1)} %add.3.refs_0_), channel_id=1, source_target_pairs={{0,4},{1,5},{2,6},{3,7},{4,0},{5,1},{6,2},{7,3},{8,12},{9,13},{10,... | collective-permute-start | bytes 49160 | tf_op jit(solution)/shard_map/ppermute | solution.py:812
  18.1 5.5 %collective-permute-start.6 = (f32[32,128]{1,0:T(8,128)S(1)}, f32[32,128]{1,0:T(8,128)S(1)}, u32[]{:S(2)}, u32[]{:S(2)}) collective-permute-start(f32[32,128]{1,0:T(8,128)S(1)} %add.3.refs_0_), channel_id=1, source_target_pairs={{0,6},{1,7},{2,4},{3,5},{4,2},{5,3},{6,0},{7,1},{8,14},{9,15},{10,... | collective-permute-start | bytes 49160 | tf_op jit(solution)/shard_map/ppermute | solution.py:812
  19.4 4.2 %collective-permute-start.7 = (f32[32,128]{1,0:T(8,128)S(1)}, f32[32,128]{1,0:T(8,128)S(1)}, u32[]{:S(2)}, u32[]{:S(2)}) collective-permute-start(f32[32,128]{1,0:T(8,128)S(1)} %add.3.refs_0_), channel_id=1, source_target_pairs={{0,2},{1,3},{2,0},{3,1},{4,6},{5,7},{6,4},{7,5},{8,10},{9,11},{10,... | collective-permute-start | bytes 49160 | tf_op jit(solution)/shard_map/ppermute | solution.py:812

commit v5 on v4

--- a/solution.py
+++ b/solution.py
@@ -19,7 +19,6 @@
 PACKS = 3
 PACK_ROWS = PACKS * TILE
 MAIN_ROWS = PAIRS * HALO * TILE
-MESSAGE_ROWS = MAIN_ROWS + PACK_ROWS
 
 HEAT_RATIO = 1.4
 FILTER_SQUARE = 0.5 ** (2.0 / 3.0)
@@ -82,8 +81,8 @@
 
 
 def pack_kernel(
-    mass_hbm, speed_hbm, heat_hbm, blow_hbm, own_ref, left_ref, right_ref, far_ref, near_ref,
-    blow_rows, given_ref, blow_ref, arrived
+    mass_hbm, speed_hbm, heat_hbm, blow_hbm, own_ref, far_ref, near_ref, blow_rows,
+    given_ref, blow_ref, arrived
 ):
     start, copies = 0, []
     for k, source in enumerate((mass_hbm, speed_hbm, heat_hbm)):
@@ -95,41 +94,21 @@
         copy.start()
     for copy in copies:
         copy.wait()
-    lane = lanes()
     even = is_even()
     first_core = is_first_of_pair("gz")
-
-    def post(index, up, down):
-        far_ref[slot_of(index), :] = jnp.where(first_core, down, up)
-        near_ref[slot_of(index), :] = jnp.where(first_core, up, down)
-
     tiles = {}
-    left = right = jnp.zeros((TILE, LANES), F32)
     for field in range(NF):
         for zz in range(ROWS):
             tile = given_ref[pl.ds(field * 32 + zz, TILE, stride=4), :]
             tiles[field, zz] = tile
             own_ref[slot_of(field * ROWS + zz), :] = tile
-            start = 32 * (field % 4) + SPAN * zz
-            reached = lane >= start
-            left = jnp.where(reached, shift_x(tile, start + HALO), left)
-            right = jnp.where(reached, shift_x(tile, start - LAST), right)
-        if field % 4 == 3 or field == NF - 1:
-            k = field // 4
-            left_ref[slot_of(k), :] = left
-            right_ref[slot_of(k), :] = right
-            post(
-                MAIN_ROWS // TILE + k,
-                jnp.where(even, shift_s(left, -1), right),
-                jnp.where(even, left, shift_s(right, 1)),
-            )
         if field % 2:
             for k in range(HALO):
-                post(
-                    field // 2 * HALO + k,
-                    jnp.where(even, shift_s(tiles[field - 1, k + 1], -1), tiles[field, k + 1]),
-                    jnp.where(even, tiles[field, k], shift_s(tiles[field - 1, k], 1)),
-                )
+                up = jnp.where(even, shift_s(tiles[field - 1, k + 1], -1), tiles[field, k + 1])
+                down = jnp.where(even, tiles[field, k], shift_s(tiles[field - 1, k], 1))
+                slot = slot_of(field // 2 * HALO + k)
+                far_ref[slot, :] = jnp.where(first_core, down, up)
+                near_ref[slot, :] = jnp.where(first_core, up, down)
     for level in range(4):
         blow_rows[pl.ds(level * TILE, TILE), :] = blow_ref[...].astype(F32)
 
@@ -150,48 +129,60 @@
             raw_ref[k + HALO + ROWS, field] = jnp.where(even, shift_s(own[k], -1), high)
 
 
-def edge_packs(left_ref, right_ref, far_ref, near_ref, k):
+def own_corner_kernel(own_ref, corner_ref):
+    lane = lanes()
+    within = lane & 63
+    for field in range(NF):
+        tile = None
+        for side in range(2):
+            for zz in range(ROWS):
+                start = 64 * side + SPAN * (zz + 2)
+                moved = shift_x(
+                    tile_of(own_ref, field * ROWS + zz), start - LAST if side else start + HALO
+                )
+                tile = moved if tile is None else jnp.where(lane >= start, moved, tile)
+        low, high = shift_s(shift_x(tile, -32), 1), shift_s(shift_x(tile, 32), -1)
+        corner_ref[field] = jnp.where(within < 16, low, jnp.where(within >= 48, high, tile))
+
+
+def corner_pack_kernel(own_corner_ref, far_ref, near_ref, corner_ref, one_ref, other_ref):
+    lane = lanes()
     even = is_even()
-    left, right = tile_of(left_ref, k), tile_of(right_ref, k)
-    low, high = (halo_tile(far_ref, near_ref, below, MAIN_ROWS // TILE + k) for below in (True, False))
-    return (
-        (
-            jnp.where(even, low, shift_s(left, 1)),
-            left,
-            jnp.where(even, shift_s(left, -1), shift_s(high, 1)),
-        ),
-        (
-            jnp.where(even, shift_s(low, -1), shift_s(right, 1)),
-            right,
-            jnp.where(even, shift_s(right, -1), high),
-        ),
-    )
-
-
-def corner_pack_kernel(left_ref, right_ref, far_ref, near_ref, corner_ref, one_ref, other_ref):
-    lane = lanes()
     even_column = is_first_of_pair("gx")
+    within = lane & 63
+    halo = (even & (within < 16)) | (jnp.logical_not(even) & (within >= 48))
     corners = []
+    for pair in range(PAIRS):
+        rows = [
+            (SPAN * (zz + 2), halo_tile(far_ref, near_ref, zz < 0, pair * HALO + zz % 4 - (zz < 0)))
+            for zz in (-2, -1, 4, 5)
+        ]
+        tile = None
+        for side in range(2):
+            for start, row in rows:
+                start += 64 * side
+                moved = shift_x(row, start - LAST if side else start + HALO)
+                tile = moved if tile is None else jnp.where(lane >= start, moved, tile)
+        swapped = jnp.where(within < 32, shift_s(tile, -1), shift_s(tile, 1))
+        for n, got in enumerate((tile, swapped)):
+            corners.append(jnp.where(halo, got, own_corner_ref[2 * pair + n]))
+            corner_ref[2 * pair + n] = corners[-1]
+    ahead = (lane & (SPAN - 1)) < HALO
+
+    def packed(group, move):
+        halves = [
+            jnp.where(
+                ahead, shift_x(group[n], 32 * n + move), shift_x(group[n + 1], 32 * n + HALO + move)
+            )
+            for n in range(0, len(group), 2)
+        ]
+        return halves[0] if len(halves) == 1 else jnp.where(lane < 64, *halves)
+
     for k in range(PACKS):
-        packs = edge_packs(left_ref, right_ref, far_ref, near_ref, k)
-        for j in range(min(4, NF - 4 * k)):
-            start = 32 * j
-            tile = None
-            for side in range(2):
-                for block, (bound, move) in enumerate(((0, -16), (16, 16), (48, 48))):
-                    moved = shift_x(packs[side][block], 64 * side + move - start)
-                    tile = (
-                        moved if tile is None
-                        else jnp.where(lane >= 64 * side + bound, moved, tile)
-                    )
-            corner_ref[4 * k + j] = tile
-            corners.append(tile)
-    for pair in range(PAIRS):
-        first, second = corners[2 * pair], corners[2 * pair + 1]
-        to_left = jnp.where(lane >= 64, shift_x(first, 66), shift_x(second, 2))
-        to_right = jnp.where(lane < 64, shift_x(first, -66), shift_x(second, -2))
-        one_ref[slot_of(pair), :] = jnp.where(even_column, to_right, to_left)
-        other_ref[slot_of(pair), :] = jnp.where(even_column, to_left, to_right)
+        group = corners[4 * k : 4 * k + 4]
+        to_left, to_right = packed(group, -3), packed(group, -66)
+        one_ref[slot_of(k), :] = jnp.where(even_column, to_right, to_left)
+        other_ref[slot_of(k), :] = jnp.where(even_column, to_left, to_right)
 
 
 def state_of(fields):
@@ -577,14 +568,13 @@
     halo = (on_left & (place < low)) | (jnp.logical_not(on_left) & (place >= high))
     fields = []
     for field in range(NF):
-        pair, second = divmod(field, 2)
-        one, other = tile_of(got_one_ref, pair), tile_of(got_other_ref, pair)
-        from_left = jnp.where(even_column, other, one)
-        from_right = jnp.where(even_column, one, other)
-        if second:
-            got = shift_x(jnp.where(on_left, from_right, from_left), 64)
-        else:
-            got = jnp.where(on_left, from_left, from_right)
+        k, j = divmod(field, 4)
+        if j == 0:
+            one, other = tile_of(got_one_ref, k), tile_of(got_other_ref, k)
+            from_left = jnp.where(even_column, other, one)
+            from_right = jnp.where(even_column, one, other)
+        move = 64 * (j // 2) + HALO * (j % 2)
+        got = jnp.where(on_left, shift_x(from_left, -move), shift_x(from_right, 69 - move))
         fields.append(jnp.where(halo, got, clamped_ref[field]))
         corner_ref[field] = fields[field]
     state = model_state(fields)
@@ -710,21 +700,20 @@
     lax.fori_loop(0, ROWS, row, 0)
 
 
-def call(kernel, out_shapes, scratch=(), inputs=0, final=False):
-    shape_of = jax.ShapeDtypeStruct if final else pltpu.VMEM
+def call(kernel, out_shapes, scratch=(), inputs=0):
     run = pl.pallas_call(
         kernel,
-        out_shape=[shape_of(shape, F32) for shape in out_shapes],
+        out_shape=[pltpu.VMEM(shape, F32) for shape in out_shapes],
         in_specs=[VMEM] * inputs,
         out_specs=[VMEM] * len(out_shapes),
         scratch_shapes=[pltpu.VMEM(shape, F32) for shape in scratch],
         compiler_params=SMALL,
     )
-
-    def placed(*args):
-        return run(*[pltpu.with_memory_space_constraint(arg, pltpu.VMEM) for arg in args])
-
-    return placed
+    return lambda *args: run(*in_vmem(args))
+
+
+def in_vmem(args):
+    return [pltpu.with_memory_space_constraint(arg, pltpu.VMEM) for arg in args]
 
 
 def body(constituent_mass, flow_speeds, thermal_pair, blowing_indicator):
@@ -743,17 +732,16 @@
     packed = (PACK_ROWS, LANES)
     rows = (GROUPS * TILE, LANES)
     fields = (NF, TILE, LANES)
-    own, left, right, far, near, blown = pl.pallas_call(
+    own, far, near, blown = pl.pallas_call(
         pack_kernel,
         out_shape=[
             pltpu.VMEM(shape, F32)
             for shape in (
-                rows, packed, packed, (MESSAGE_ROWS, LANES), (MESSAGE_ROWS, LANES),
-                (4 * TILE, LANES),
+                rows, (MAIN_ROWS, LANES), (MAIN_ROWS, LANES), (4 * TILE, LANES),
             )
         ],
         in_specs=[pl.BlockSpec(memory_space=pltpu.HBM)] * 4,
-        out_specs=[VMEM] * 6,
+        out_specs=[VMEM] * 4,
         scratch_shapes=[
             pltpu.VMEM((NF * 4 * TILE, LANES), F32),
             pltpu.VMEM(blowing_indicator.shape, jnp.int32),
@@ -767,13 +755,14 @@
     far = swap("gz", count_z, False)(far)
     near = swap("gz", count_z, True)(near)
     face, part = call(stream_kernel, [rows, rows], inputs=2)(own, blown)
-    far, near, face, part = lax.optimization_barrier((far, near, face, part))
+    (corner,) = call(own_corner_kernel, [fields], inputs=1)(own)
+    far, near, face, part, corner = lax.optimization_barrier((far, near, face, part, corner))
 
     corner, one, other = call(
         corner_pack_kernel,
-        [fields, (PAIRS * TILE, LANES), (PAIRS * TILE, LANES)],
-        inputs=4,
-    )(left, right, far, near)
+        [fields, packed, packed],
+        inputs=3,
+    )(corner, far, near)
     got_one = swap("gx", count_x, True)(one)
     got_other = swap("gx", count_x, False)(other)
     sums, clamped, tiles, state, raw = call(
@@ -825,13 +814,14 @@
     def final(*refs):
         final_kernel(*refs, parts=4)
 
-    tendency, coefficients = call(
+    tendency, coefficients = pl.pallas_call(
         final,
-        [(NF * 32, LANES), (3, 4, LANES)],
-        scratch=[(TILE, LANES)],
-        inputs=6,
-        final=True,
-    )(*parts, base, terms)
+        out_shape=[jax.ShapeDtypeStruct(shape, F32) for shape in ((NF * 32, LANES), (3, 4, LANES))],
+        in_specs=[VMEM] * 6,
+        out_specs=[VMEM] * 2,
+        scratch_shapes=[pltpu.VMEM((TILE, LANES), F32)],
+        compiler_params=SMALL,
+    )(*in_vmem(parts + [base, terms]))
     return tendency.reshape(NF, 4, TILE, LANES), coefficients
 
 

time: 24.6 us -> 24.3 us (0.988)
  waiting for transfers between devices: 3.69 us -> 3.32 us
    ppermute x4, waiting for transfers between devices: 2.13 us -> 1.66 us  [swap(): lax.ppermute(value, axis, [(i, (i + step[i % 2]) % count) for i in range(...]
    pallas_call x8 -> x9, Pallas kernels: 6.92 us -> 7.17 us  [the longest x8 6.32 us: call(): return lambda *args: run(*in_vmem(args))]
  transfers between devices with their start and end apart: 8 -> 8, of which waited for: 4 -> 4; matrix products, arithmetic and copies ran while one was open for 0% -> 0% of each run, Pallas kernels for 21% -> 22%
where the time goes in v5:
time: 24.3 us; the launch traced here: 24.1 us
  starting transfers between devices  11.9 us (49%)
  Pallas kernels  8.12 us (33%)
  waiting for transfers between devices  3.32 us (14%)
  between operations  0.72 us (3%)
    ppermute x4, starting transfers between devices, swap(): lax.ppermute(value, axis, [(i, (i + step[i % 2]) % count) for i in range(...  8.38 us
    pallas_call x8, Pallas kernels, call(): return lambda *args: run(*in_vmem(args))  6.32 us
    ppermute x4, starting transfers between devices, crossed(): return lax.ppermute(value, 'gz', [(i, i ^ mask) for i in range(count_z)])  3.56 us
    ppermute x4, waiting for transfers between devices, crossed(): return lax.ppermute(value, 'gz', [(i, i ^ mask) for i in range(count_z)])  1.67 us
    ppermute x4, waiting for transfers between devices, swap(): lax.ppermute(value, axis, [(i, (i + step[i % 2]) % count) for i in range(...  1.66 us
    pallas_call x1, Pallas kernels, body(): pl.pallas_call(pack_kernel, out_shape=[pltpu.VMEM(shape, F32) for shape i...  0.95 us
    pallas_call x1, Pallas kernels, body(): pl.pallas_call(final, out_shape=[jax.ShapeDtypeStruct(shape, F32) for sha...  0.85 us
  transfers between devices with their start and end apart: 8, of which 4 were waited for; matrix products, arithmetic and copies ran while one was open for 0% of the time, Pallas kernels for 22%

profile of v5, /device:TPU:0, one launch (start us, length us, event | category | flops | bytes accessed | tf_op | source)
XLA Modules:
  0.0 24.1 jit_solution(13667428935013402077)
XLA Ops:
  0.6 1.0 %shard_map.59 = (f32[320,128]{1,0:T(8,128)S(1)}, f32[120,128]{1,0:T(8,128)S(1)}, f32[120,128]{1,0:T(8,128)S(1)}, f32[32,128]{1,0:T(8,128)S(1)}) custom-call(f32[160,128]{1,0:T(8,128)} %bitcast.4, f32[96,128]{1,0:T(8,128)} %bitcast.5, f32[64,128]{1,0:T(8,128)} %bitcast.6, s32[8,128]{1,0:T(8,128)} %blow_hbm.1), custom_call_target="tpu_custom_call" | custom-call | tf_op jit(solution)/shard_map/pallas_call | solution.py:735
  1.6 4.6 %collective-permute-start = (f32[120,128]{1,0:T(8,128)S(1)}, f32[120,128]{1,0:T(8,128)S(1)}, u32[]{:S(2)}, u32[]{:S(2)}) collective-permute-start(f32[120,128]{1,0:T(8,128)S(1)} %get-tuple-element.31), channel_id=1, source_target_pairs={{0,7},{1,2},{2,1},{3,4},{4,3},{5,6},{6,5},{7,0},{8,15},{9,10},{10,... | collective-permute-start | bytes 184328 | tf_op jit(solution)/shard_map/ppermute | solution.py:725
  6.1 0.0 collective-permute-start.1
  6.1 0.2 %shard_map.61.own_corner_ref = f32[10,8,128]{2,1,0:T(8,128)S(1)} custom-call(f32[320,128]{1,0:T(8,128)S(1)} %get-tuple-element.30.own_ref), custom_call_target="tpu_custom_call" | custom-call | tf_op jit(solution)/shard_map/pallas_call | solution.py:712
  6.4 1.2 %shard_map.60 = (f32[320,128]{1,0:T(8,128)S(1)}, f32[320,128]{1,0:T(8,128)S(1)}) custom-call(f32[320,128]{1,0:T(8,128)S(1)} %get-tuple-element.30.own_ref, f32[32,128]{1,0:T(8,128)S(1)} %get-tuple-element.33.blow_rows), custom_call_target="tpu_custom_call" | custom-call | tf_op jit(solution)/shard_map/pallas_call | solution.py:712
  7.6 0.5 %collective-permute-done.far_ref = f32[120,128]{1,0:T(8,128)S(1)} collective-permute-done((f32[120,128]{1,0:T(8,128)S(1)}, f32[120,128]{1,0:T(8,128)S(1)}, u32[]{:S(2)}, u32[]{:S(2)}) %collective-permute-start) | collective-permute-done | bytes 61472 | tf_op jit(solution)/shard_map/ppermute | solution.py:725
  8.2 0.0 collective-permute-done.1.near_ref
  8.2 0.2 shard_map.62
  8.4 2.3 %collective-permute-start.2 = (f32[24,128]{1,0:T(8,128)S(1)}, f32[24,128]{1,0:T(8,128)S(1)}, u32[]{:S(2)}, u32[]{:S(2)}) collective-permute-start(f32[24,128]{1,0:T(8,128)S(1)} %get-tuple-element.41), channel_id=1, source_target_pairs={{0,8},{8,0},{16,24},{24,16},{1,9},{9,1},{17,25},{25,17},{2,10},{10... | collective-permute-start | bytes 36872 | tf_op jit(solution)/shard_map/ppermute | solution.py:725
  10.7 1.5 %collective-permute-start.3 = (f32[24,128]{1,0:T(8,128)S(1)}, f32[24,128]{1,0:T(8,128)S(1)}, u32[]{:S(2)}, u32[]{:S(2)}) collective-permute-start(f32[24,128]{1,0:T(8,128)S(1)} %get-tuple-element.42), channel_id=1, source_target_pairs={{0,24},{8,16},{16,8},{24,0},{1,25},{9,17},{17,9},{25,1},{2,26},{10... | collective-permute-start | bytes 36872 | tf_op jit(solution)/shard_map/ppermute | solution.py:725
  12.2 2.0 %shard_map.63 = (f32[6,8,128]{2,1,0:T(8,128)S(1)}, f32[10,8,128]{2,1,0:T(8,128)S(1)}, f32[6,45,8,128]{3,2,1,0:T(8,128)S(1)}, f32[8,20,8,128]{3,2,1,0:T(8,128)S(1)}, f32[10,10,8,128]{3,2,1,0:T(8,128)S(1)}) custom-call(f32[320,128]{1,0:T(8,128)S(1)} %get-tuple-element.30.own_ref, f32[120,128]{1,0:T(8,128)S(1)} %collective-permute-done.far_ref, ...), custom_call_target="tpu_custom_call" | custom-call | tf_op jit(solution)/shard_map/pallas_call | solution.py:712
  14.2 0.0 collective-permute-done.2.got_one_ref
  14.2 1.1 %collective-permute-done.3.got_other_ref = f32[24,128]{1,0:T(8,128)S(1)} collective-permute-done((f32[24,128]{1,0:T(8,128)S(1)}, f32[24,128]{1,0:T(8,128)S(1)}, u32[]{:S(2)}, u32[]{:S(2)}) %collective-permute-start.3) | collective-permute-done | bytes 12320 | tf_op jit(solution)/shard_map/ppermute | solution.py:725
  15.3 0.8 %shard_map.64 = (f32[32,128]{1,0:T(8,128)S(1)}, f32[10,8,128]{2,1,0:T(8,128)S(1)}, f32[45,8,128]{2,1,0:T(8,128)S(1)}, f32[3,8,128]{2,1,0:T(8,128)S(1)}) custom-call(f32[10,8,128]{2,1,0:T(8,128)S(1)} %get-tuple-element.40.clamped_ref, f32[24,128]{1,0:T(8,128)S(1)} %collective-permute-done.2.got_one_ref, f32[24,128]{1,0:T(8,128)S(1)} %collective-permute-done.3.got_other_ref, ...), custom_call_target="tpu_custom_call" | custom-call | tf_op jit(solution)/shard_map/pallas_call | solution.py:712
  16.1 0.1 collective-permute-start.4
  16.1 1.2 %collective-permute-done.4 = f32[32,128]{1,0:T(8,128)S(1)} collective-permute-done((f32[32,128]{1,0:T(8,128)S(1)}, f32[32,128]{1,0:T(8,128)S(1)}, u32[]{:S(2)}, u32[]{:S(2)}) %collective-permute-start.4) | collective-permute-done | bytes 16416 | tf_op jit(solution)/shard_map/ppermute | solution.py:801
  17.3 0.4 %collective-permute-start.5 = (f32[32,128]{1,0:T(8,128)S(1)}, f32[32,128]{1,0:T(8,128)S(1)}, u32[]{:S(2)}, u32[]{:S(2)}) collective-permute-start(f32[32,128]{1,0:T(8,128)S(1)} %add.3.refs_0_), channel_id=1, source_target_pairs={{0,4},{1,5},{2,6},{3,7},{4,0},{5,1},{6,2},{7,3},{8,12},{9,13},{10,... | collective-permute-start | bytes 49160 | tf_op jit(solution)/shard_map/ppermute | solution.py:801
  17.7 1.3 %collective-permute-start.6 = (f32[32,128]{1,0:T(8,128)S(1)}, f32[32,128]{1,0:T(8,128)S(1)}, u32[]{:S(2)}, u32[]{:S(2)}) collective-permute-start(f32[32,128]{1,0:T(8,128)S(1)} %add.3.refs_0_), channel_id=1, source_target_pairs={{0,6},{1,7},{2,4},{3,5},{4,2},{5,3},{6,0},{7,1},{8,14},{9,15},{10,... | collective-permute-start | bytes 49160 | tf_op jit(solution)/shard_map/ppermute | solution.py:801
  19.1 1.7 %collective-permute-start.7 = (f32[32,128]{1,0:T(8,128)S(1)}, f32[32,128]{1,0:T(8,128)S(1)}, u32[]{:S(2)}, u32[]{:S(2)}) collective-permute-start(f32[32,128]{1,0:T(8,128)S(1)} %add.3.refs_0_), channel_id=1, source_target_pairs={{0,2},{1,3},{2,0},{3,1},{4,6},{5,7},{6,4},{7,5},{8,10},{9,11},{10,... | collective-permute-start | bytes 49160 | tf_op jit(solution)/shard_map/ppermute | solution.py:801
  20.8 0.5 %shard_map.65.part_ref = f32[320,128]{1,0:T(8,128)S(1)} custom-call(f32[10,8,128]{2,1,0:T(8,128)S(1)} %get-tuple-element.49.corner_ref, f32[320,128]{1,0:T(8,128)S(1)} %get-tuple-element.50.face_ref, f32[320,128]{1,0:T(8,128)S(1)} %get-tuple-element.51.part_ref), custom_call_target="tpu_custom_call" | custom-call | tf_op jit(solution)/shard_map/pallas_call | solution.py:712
  21.3 0.9 %shard_map.66.refs_4_ = f32[320,128]{1,0:T(8,128)S(1)} custom-call(f32[10,10,8,128]{3,2,1,0:T(8,128)S(1)} %get-tuple-element.48.raw_ref, f32[320,128]{1,0:T(8,128)S(1)} %shard_map.65.part_ref), custom_call_target="tpu_custom_call" | custom-call | tf_op jit(solution)/shard_map/pallas_call | solution.py:712
  22.2 0.5 %shard_map.67.refs_5_ = f32[4,12,5,8,128]{4,3,2,1,0:T(8,128)S(1)} custom-call(f32[6,45,8,128]{3,2,1,0:T(8,128)S(1)} %get-tuple-element.52.tile_ref, f32[8,20,8,128]{3,2,1,0:T(8,128)S(1)} %get-tuple-element.53.state_ref, f32[45,8,128]{2,1,0:T(8,128)S(1)} %get-tuple-element.54.corner_ref, f32[3,8,128]{2,1,0:T(8,128)S(1)} %get-tuple-element.55.corner_speed_ref), custom_call_target="tpu_custom_call" | custom-call | tf_op jit(solution)/shard_map/pallas_call | solution.py:712
  22.8 0.0 collective-permute-done.5.refs_1_
  22.8 0.5 %collective-permute-done.6.refs_2_ = f32[32,128]{1,0:T(8,128)S(1)} collective-permute-done((f32[32,128]{1,0:T(8,128)S(1)}, f32[32,128]{1,0:T(8,128)S(1)}, u32[]{:S(2)}, u32[]{:S(2)}) %collective-permute-start.6) | collective-permute-done | bytes 16416 | tf_op jit(solution)/shard_map/ppermute | solution.py:801
  23.3 0.0 collective-permute-done.7.refs_3_
  23.3 0.9 %shard_map.68 = (f32[320,128]{1,0:T(8,128)}, f32[3,4,128]{2,1,0:T(4,128)}) custom-call(f32[32,128]{1,0:T(8,128)S(1)} %add.3.refs_0_, f32[32,128]{1,0:T(8,128)S(1)} %collective-permute-done.5.refs_1_, f32[32,128]{1,0:T(8,128)S(1)} %collective-permute-done.6.refs_2_, f32[32,128]{1,0:T(8,128)S(1)} %collective-permute-done.7.refs_3_, ...), custom_call_target="tpu_custom_call" | custom-call | tf_op jit(solution)/shard_map/pallas_call | solution.py:817
  (1 shorter events, 0.0 us)
Async XLA Ops:
  1.6 6.6 %collective-permute-start = (f32[120,128]{1,0:T(8,128)S(1)}, f32[120,128]{1,0:T(8,128)S(1)}, u32[]{:S(2)}, u32[]{:S(2)}) collective-permute-start(f32[120,128]{1,0:T(8,128)S(1)} %get-tuple-element.31), channel_id=1, source_target_pairs={{0,7},{1,2},{2,1},{3,4},{4,3},{5,6},{6,5},{7,0},{8,15},{9,10},{10,... | collective-permute-start | bytes 184328 | tf_op jit(solution)/shard_map/ppermute | solution.py:725
  6.1 2.0 %collective-permute-start.1 = (f32[120,128]{1,0:T(8,128)S(1)}, f32[120,128]{1,0:T(8,128)S(1)}, u32[]{:S(2)}, u32[]{:S(2)}) collective-permute-start(f32[120,128]{1,0:T(8,128)S(1)} %get-tuple-element.32), channel_id=1, source_target_pairs={{0,1},{1,0},{2,3},{3,2},{4,5},{5,4},{6,7},{7,6},{8,9},{9,8},{10,11... | collective-permute-start | bytes 184328 | tf_op jit(solution)/shard_map/ppermute | solution.py:725
  8.4 5.8 %collective-permute-start.2 = (f32[24,128]{1,0:T(8,128)S(1)}, f32[24,128]{1,0:T(8,128)S(1)}, u32[]{:S(2)}, u32[]{:S(2)}) collective-permute-start(f32[24,128]{1,0:T(8,128)S(1)} %get-tuple-element.41), channel_id=1, source_target_pairs={{0,8},{8,0},{16,24},{24,16},{1,9},{9,1},{17,25},{25,17},{2,10},{10... | collective-permute-start | bytes 36872 | tf_op jit(solution)/shard_map/ppermute | solution.py:725
  10.7 4.6 %collective-permute-start.3 = (f32[24,128]{1,0:T(8,128)S(1)}, f32[24,128]{1,0:T(8,128)S(1)}, u32[]{:S(2)}, u32[]{:S(2)}) collective-permute-start(f32[24,128]{1,0:T(8,128)S(1)} %get-tuple-element.42), channel_id=1, source_target_pairs={{0,24},{8,16},{16,8},{24,0},{1,25},{9,17},{17,9},{25,1},{2,26},{10... | collective-permute-start | bytes 36872 | tf_op jit(solution)/shard_map/ppermute | solution.py:725
  16.1 1.2 %collective-permute-start.4 = (f32[32,128]{1,0:T(8,128)S(1)}, f32[32,128]{1,0:T(8,128)S(1)}, u32[]{:S(2)}, u32[]{:S(2)}) collective-permute-start(f32[32,128]{1,0:T(8,128)S(1)} %get-tuple-element.47), channel_id=1, source_target_pairs={{0,1},{1,0},{2,3},{3,2},{4,5},{5,4},{6,7},{7,6},{8,9},{9,8},{10,11... | collective-permute-start | bytes 49160 | tf_op jit(solution)/shard_map/ppermute | solution.py:801
  17.3 5.4 %collective-permute-start.5 = (f32[32,128]{1,0:T(8,128)S(1)}, f32[32,128]{1,0:T(8,128)S(1)}, u32[]{:S(2)}, u32[]{:S(2)}) collective-permute-start(f32[32,128]{1,0:T(8,128)S(1)} %add.3.refs_0_), channel_id=1, source_target_pairs={{0,4},{1,5},{2,6},{3,7},{4,0},{5,1},{6,2},{7,3},{8,12},{9,13},{10,... | collective-permute-start | bytes 49160 | tf_op jit(solution)/shard_map/ppermute | solution.py:801
  17.7 5.5 %collective-permute-start.6 = (f32[32,128]{1,0:T(8,128)S(1)}, f32[32,128]{1,0:T(8,128)S(1)}, u32[]{:S(2)}, u32[]{:S(2)}) collective-permute-start(f32[32,128]{1,0:T(8,128)S(1)} %add.3.refs_0_), channel_id=1, source_target_pairs={{0,6},{1,7},{2,4},{3,5},{4,2},{5,3},{6,0},{7,1},{8,14},{9,15},{10,... | collective-permute-start | bytes 49160 | tf_op jit(solution)/shard_map/ppermute | solution.py:801
  19.1 4.2 %collective-permute-start.7 = (f32[32,128]{1,0:T(8,128)S(1)}, f32[32,128]{1,0:T(8,128)S(1)}, u32[]{:S(2)}, u32[]{:S(2)}) collective-permute-start(f32[32,128]{1,0:T(8,128)S(1)} %add.3.refs_0_), channel_id=1, source_target_pairs={{0,2},{1,3},{2,0},{3,1},{4,6},{5,7},{6,4},{7,5},{8,10},{9,11},{10,... | collective-permute-start | bytes 49160 | tf_op jit(solution)/shard_map/ppermute | solution.py:801

commit v6 on v5

--- a/solution.py
+++ b/solution.py
@@ -145,10 +145,9 @@
         corner_ref[field] = jnp.where(within < 16, low, jnp.where(within >= 48, high, tile))
 
 
-def corner_pack_kernel(own_corner_ref, far_ref, near_ref, corner_ref, one_ref, other_ref):
+def corner_pack_kernel(own_corner_ref, far_ref, near_ref, corner_ref, right_ref, left_ref):
     lane = lanes()
     even = is_even()
-    even_column = is_first_of_pair("gx")
     within = lane & 63
     halo = (even & (within < 16)) | (jnp.logical_not(even) & (within >= 48))
     corners = []
@@ -181,8 +180,8 @@
     for k in range(PACKS):
         group = corners[4 * k : 4 * k + 4]
         to_left, to_right = packed(group, -3), packed(group, -66)
-        one_ref[slot_of(k), :] = jnp.where(even_column, to_right, to_left)
-        other_ref[slot_of(k), :] = jnp.where(even_column, to_left, to_right)
+        right_ref[slot_of(k), :] = to_right
+        left_ref[slot_of(k), :] = to_left
 
 
 def state_of(fields):
@@ -553,13 +552,12 @@
 
 
 def corner_kernel(
-    clamped_ref, got_one_ref, got_other_ref, sum_ref,
+    clamped_ref, got_left_ref, got_right_ref, sum_ref,
     totals_ref, corner_ref, tile_ref, speed_ref
 ):
     lane = lanes()
     even = is_even()
     scale = slope_scale()
-    even_column = is_first_of_pair("gx")
     column = lax.axis_index("gx")
     first, last = column == 0, column == lax.axis_size("gx") - 1
     place = lane & (SPAN - 1)
@@ -570,9 +568,7 @@
     for field in range(NF):
         k, j = divmod(field, 4)
         if j == 0:
-            one, other = tile_of(got_one_ref, k), tile_of(got_other_ref, k)
-            from_left = jnp.where(even_column, other, one)
-            from_right = jnp.where(even_column, one, other)
+            from_left, from_right = tile_of(got_left_ref, k), tile_of(got_right_ref, k)
         move = 64 * (j // 2) + HALO * (j % 2)
         got = jnp.where(on_left, shift_x(from_left, -move), shift_x(from_right, 69 - move))
         fields.append(jnp.where(halo, got, clamped_ref[field]))
@@ -720,10 +716,15 @@
     count_x = lax.axis_size("gx")
     count_z = lax.axis_size("gz")
 
-    def swap(axis, count, near):
+    def swap(near):
         step = [1, -1] if near else [-1, 1]
         return lambda value: lax.ppermute(
-            value, axis, [(i, (i + step[i % 2]) % count) for i in range(count)]
+            value, "gz", [(i, (i + step[i % 2]) % count_z) for i in range(count_z)]
+        )
+
+    def ring(step):
+        return lambda value: lax.ppermute(
+            value, "gx", [(i, (i + step) % count_x) for i in range(count_x)]
         )
 
     arrays = [
@@ -752,19 +753,19 @@
         pltpu.with_memory_space_constraint(value, pltpu.HBM)
         for value in arrays + [blowing_indicator]
     ])
-    far = swap("gz", count_z, False)(far)
-    near = swap("gz", count_z, True)(near)
+    far = swap(False)(far)
+    near = swap(True)(near)
     face, part = call(stream_kernel, [rows, rows], inputs=2)(own, blown)
     (corner,) = call(own_corner_kernel, [fields], inputs=1)(own)
     far, near, face, part, corner = lax.optimization_barrier((far, near, face, part, corner))
 
-    corner, one, other = call(
+    corner, to_right, to_left = call(
         corner_pack_kernel,
         [fields, packed, packed],
         inputs=3,
     )(corner, far, near)
-    got_one = swap("gx", count_x, True)(one)
-    got_other = swap("gx", count_x, False)(other)
+    got_left = ring(1)(to_right)
+    got_right = ring(-1)(to_left)
     sums, clamped, tiles, state, raw = call(
         model_kernel,
         [
@@ -777,12 +778,12 @@
         scratch=[(GRID_ROWS, 4, TILE, LANES), (GRID_ROWS, 8, TILE, LANES)],
         inputs=4,
     )(own, far, near, corner)
-    got_one, got_other, sums = lax.optimization_barrier((got_one, got_other, sums))
+    got_left, got_right, sums = lax.optimization_barrier((got_left, got_right, sums))
     totals, corner, corner_tiles, corner_speed = call(
         corner_kernel,
         [(4 * TILE, LANES), fields, (TILES, TILE, LANES), (3, TILE, LANES)],
         inputs=4,
-    )(clamped, got_one, got_other, sums)
+    )(clamped, got_left, got_right, sums)
 
     (terms,) = call(term_kernel, [(ROWS, TERMS, 5, TILE, LANES)], inputs=4)(
         tiles, state, corner_tiles, corner_speed

time: 24.3 us -> 23.5 us (0.967)
  starting transfers between devices: 11.9 us -> 11.5 us
  waiting for transfers between devices: 3.32 us -> 3.02 us
    ppermute x4, starting transfers between devices: 8.38 us -> 7.9 us  [the longest x2 4.56 us: swap(): lax.ppermute(value, 'gz', [(i, (i + step[i % 2]) % count_z) for i in rang...]
    ppermute x4, waiting for transfers between devices: 1.66 us -> 1.23 us  [the longest x2 0.7 us: ring(): lax.ppermute(value, 'gx', [(i, (i + step) % count_x) for i in range(count...]
  transfers between devices with their start and end apart: 8 -> 8, of which waited for: 4 -> 4; matrix products, arithmetic and copies ran while one was open for 0% -> 0% of each run, Pallas kernels for 22% -> 23%
where the time goes in v6:
time: 23.5 us; the launch traced here: 23.4 us
  starting transfers between devices  11.5 us (49%)
  Pallas kernels  8.14 us (35%)
  waiting for transfers between devices  3.02 us (13%)
  between operations  0.72 us (3%)
    pallas_call x8, Pallas kernels, call(): return lambda *args: run(*in_vmem(args))  6.34 us
    ppermute x2, starting transfers between devices, swap(): lax.ppermute(value, 'gz', [(i, (i + step[i % 2]) % count_z) for i in rang...  4.56 us
    ppermute x4, starting transfers between devices, crossed(): return lax.ppermute(value, 'gz', [(i, i ^ mask) for i in range(count_z)])  3.56 us
    ppermute x2, starting transfers between devices, ring(): lax.ppermute(value, 'gx', [(i, (i + step) % count_x) for i in range(count...  3.34 us
    ppermute x4, waiting for transfers between devices, crossed(): return lax.ppermute(value, 'gz', [(i, i ^ mask) for i in range(count_z)])  1.79 us
    pallas_call x1, Pallas kernels, body(): pl.pallas_call(pack_kernel, out_shape=[pltpu.VMEM(shape, F32) for shape i...  0.95 us
    pallas_call x1, Pallas kernels, body(): pl.pallas_call(final, out_shape=[jax.ShapeDtypeStruct(shape, F32) for sha...  0.85 us
    ppermute x2, waiting for transfers between devices, ring(): lax.ppermute(value, 'gx', [(i, (i + step) % count_x) for i in range(count...  0.7 us
  transfers between devices with their start and end apart: 8, of which 4 were waited for; matrix products, arithmetic and copies ran while one was open for 0% of the time, Pallas kernels for 23%

profile of v6, /device:TPU:0, one launch (start us, length us, event | category | flops | bytes accessed | tf_op | source)
XLA Modules:
  0.0 23.4 jit_solution(14095363400560568356)
XLA Ops:
  0.6 1.0 %shard_map.59 = (f32[320,128]{1,0:T(8,128)S(1)}, f32[120,128]{1,0:T(8,128)S(1)}, f32[120,128]{1,0:T(8,128)S(1)}, f32[32,128]{1,0:T(8,128)S(1)}) custom-call(f32[160,128]{1,0:T(8,128)} %bitcast.4, f32[96,128]{1,0:T(8,128)} %bitcast.5, f32[64,128]{1,0:T(8,128)} %bitcast.6, s32[8,128]{1,0:T(8,128)} %blow_hbm.1), custom_call_target="tpu_custom_call" | custom-call | tf_op jit(solution)/shard_map/pallas_call | solution.py:736
  1.6 4.6 %collective-permute-start = (f32[120,128]{1,0:T(8,128)S(1)}, f32[120,128]{1,0:T(8,128)S(1)}, u32[]{:S(2)}, u32[]{:S(2)}) collective-permute-start(f32[120,128]{1,0:T(8,128)S(1)} %get-tuple-element.31), channel_id=1, source_target_pairs={{0,7},{1,2},{2,1},{3,4},{4,3},{5,6},{6,5},{7,0},{8,15},{9,10},{10,... | collective-permute-start | bytes 184328 | tf_op jit(solution)/shard_map/ppermute | solution.py:721
  6.1 0.0 collective-permute-start.1
  6.1 0.2 %shard_map.61.own_corner_ref = f32[10,8,128]{2,1,0:T(8,128)S(1)} custom-call(f32[320,128]{1,0:T(8,128)S(1)} %get-tuple-element.30.own_ref), custom_call_target="tpu_custom_call" | custom-call | tf_op jit(solution)/shard_map/pallas_call | solution.py:708
  6.4 1.2 %shard_map.60 = (f32[320,128]{1,0:T(8,128)S(1)}, f32[320,128]{1,0:T(8,128)S(1)}) custom-call(f32[320,128]{1,0:T(8,128)S(1)} %get-tuple-element.30.own_ref, f32[32,128]{1,0:T(8,128)S(1)} %get-tuple-element.33.blow_rows), custom_call_target="tpu_custom_call" | custom-call | tf_op jit(solution)/shard_map/pallas_call | solution.py:708
  7.6 0.5 %collective-permute-done.far_ref = f32[120,128]{1,0:T(8,128)S(1)} collective-permute-done((f32[120,128]{1,0:T(8,128)S(1)}, f32[120,128]{1,0:T(8,128)S(1)}, u32[]{:S(2)}, u32[]{:S(2)}) %collective-permute-start) | collective-permute-done | bytes 61472 | tf_op jit(solution)/shard_map/ppermute | solution.py:721
  8.2 0.0 collective-permute-done.1.near_ref
  8.2 0.2 shard_map.62
  8.4 2.3 %collective-permute-start.2 = (f32[24,128]{1,0:T(8,128)S(1)}, f32[24,128]{1,0:T(8,128)S(1)}, u32[]{:S(2)}, u32[]{:S(2)}) collective-permute-start(f32[24,128]{1,0:T(8,128)S(1)} %get-tuple-element.41), channel_id=1, source_target_pairs={{0,8},{8,16},{16,24},{24,0},{1,9},{9,17},{17,25},{25,1},{2,10},{10... | collective-permute-start | bytes 36872 | tf_op jit(solution)/shard_map/ppermute | solution.py:726
  10.7 1.0 %collective-permute-start.3 = (f32[24,128]{1,0:T(8,128)S(1)}, f32[24,128]{1,0:T(8,128)S(1)}, u32[]{:S(2)}, u32[]{:S(2)}) collective-permute-start(f32[24,128]{1,0:T(8,128)S(1)} %get-tuple-element.42), channel_id=1, source_target_pairs={{0,24},{8,0},{16,8},{24,16},{1,25},{9,1},{17,9},{25,17},{2,26},{10... | collective-permute-start | bytes 36872 | tf_op jit(solution)/shard_map/ppermute | solution.py:726
  11.7 2.0 %shard_map.63 = (f32[6,8,128]{2,1,0:T(8,128)S(1)}, f32[10,8,128]{2,1,0:T(8,128)S(1)}, f32[6,45,8,128]{3,2,1,0:T(8,128)S(1)}, f32[8,20,8,128]{3,2,1,0:T(8,128)S(1)}, f32[10,10,8,128]{3,2,1,0:T(8,128)S(1)}) custom-call(f32[320,128]{1,0:T(8,128)S(1)} %get-tuple-element.30.own_ref, f32[120,128]{1,0:T(8,128)S(1)} %collective-permute-done.far_ref, ...), custom_call_target="tpu_custom_call" | custom-call | tf_op jit(solution)/shard_map/pallas_call | solution.py:708
  13.7 0.0 collective-permute-done.2.got_left_ref
  13.7 0.7 %collective-permute-done.3.got_right_ref = f32[24,128]{1,0:T(8,128)S(1)} collective-permute-done((f32[24,128]{1,0:T(8,128)S(1)}, f32[24,128]{1,0:T(8,128)S(1)}, u32[]{:S(2)}, u32[]{:S(2)}) %collective-permute-start.3) | collective-permute-done | bytes 12320 | tf_op jit(solution)/shard_map/ppermute | solution.py:726
  14.4 0.8 %shard_map.64 = (f32[32,128]{1,0:T(8,128)S(1)}, f32[10,8,128]{2,1,0:T(8,128)S(1)}, f32[45,8,128]{2,1,0:T(8,128)S(1)}, f32[3,8,128]{2,1,0:T(8,128)S(1)}) custom-call(f32[10,8,128]{2,1,0:T(8,128)S(1)} %get-tuple-element.40.clamped_ref, f32[24,128]{1,0:T(8,128)S(1)} %collective-permute-done.2.got_left_ref, f32[24,128]{1,0:T(8,128)S(1)} %collective-permute-done.3.got_right_ref, ...), custom_call_target="tpu_custom_call" | custom-call | tf_op jit(solution)/shard_map/pallas_call | solution.py:708
  15.2 0.1 collective-permute-start.4
  15.3 1.2 %collective-permute-done.4 = f32[32,128]{1,0:T(8,128)S(1)} collective-permute-done((f32[32,128]{1,0:T(8,128)S(1)}, f32[32,128]{1,0:T(8,128)S(1)}, u32[]{:S(2)}, u32[]{:S(2)}) %collective-permute-start.4) | collective-permute-done | bytes 16416 | tf_op jit(solution)/shard_map/ppermute | solution.py:802
  16.4 0.4 %collective-permute-start.5 = (f32[32,128]{1,0:T(8,128)S(1)}, f32[32,128]{1,0:T(8,128)S(1)}, u32[]{:S(2)}, u32[]{:S(2)}) collective-permute-start(f32[32,128]{1,0:T(8,128)S(1)} %add.3.refs_0_), channel_id=1, source_target_pairs={{0,4},{1,5},{2,6},{3,7},{4,0},{5,1},{6,2},{7,3},{8,12},{9,13},{10,... | collective-permute-start | bytes 49160 | tf_op jit(solution)/shard_map/ppermute | solution.py:802
  16.8 1.5 %collective-permute-start.6 = (f32[32,128]{1,0:T(8,128)S(1)}, f32[32,128]{1,0:T(8,128)S(1)}, u32[]{:S(2)}, u32[]{:S(2)}) collective-permute-start(f32[32,128]{1,0:T(8,128)S(1)} %add.3.refs_0_), channel_id=1, source_target_pairs={{0,6},{1,7},{2,4},{3,5},{4,2},{5,3},{6,0},{7,1},{8,14},{9,15},{10,... | collective-permute-start | bytes 49160 | tf_op jit(solution)/shard_map/ppermute | solution.py:802
  18.4 1.6 %collective-permute-start.7 = (f32[32,128]{1,0:T(8,128)S(1)}, f32[32,128]{1,0:T(8,128)S(1)}, u32[]{:S(2)}, u32[]{:S(2)}) collective-permute-start(f32[32,128]{1,0:T(8,128)S(1)} %add.3.refs_0_), channel_id=1, source_target_pairs={{0,2},{1,3},{2,0},{3,1},{4,6},{5,7},{6,4},{7,5},{8,10},{9,11},{10,... | collective-permute-start | bytes 49160 | tf_op jit(solution)/shard_map/ppermute | solution.py:802
  19.9 0.5 %shard_map.65.part_ref = f32[320,128]{1,0:T(8,128)S(1)} custom-call(f32[10,8,128]{2,1,0:T(8,128)S(1)} %get-tuple-element.49.corner_ref, f32[320,128]{1,0:T(8,128)S(1)} %get-tuple-element.50.face_ref, f32[320,128]{1,0:T(8,128)S(1)} %get-tuple-element.51.part_ref), custom_call_target="tpu_custom_call" | custom-call | tf_op jit(solution)/shard_map/pallas_call | solution.py:708
  20.4 0.9 %shard_map.66.refs_4_ = f32[320,128]{1,0:T(8,128)S(1)} custom-call(f32[10,10,8,128]{3,2,1,0:T(8,128)S(1)} %get-tuple-element.48.raw_ref, f32[320,128]{1,0:T(8,128)S(1)} %shard_map.65.part_ref), custom_call_target="tpu_custom_call" | custom-call | tf_op jit(solution)/shard_map/pallas_call | solution.py:708
  21.4 0.5 %shard_map.67.refs_5_ = f32[4,12,5,8,128]{4,3,2,1,0:T(8,128)S(1)} custom-call(f32[6,45,8,128]{3,2,1,0:T(8,128)S(1)} %get-tuple-element.52.tile_ref, f32[8,20,8,128]{3,2,1,0:T(8,128)S(1)} %get-tuple-element.53.state_ref, f32[45,8,128]{2,1,0:T(8,128)S(1)} %get-tuple-element.54.corner_ref, f32[3,8,128]{2,1,0:T(8,128)S(1)} %get-tuple-element.55.corner_speed_ref), custom_call_target="tpu_custom_call" | custom-call | tf_op jit(solution)/shard_map/pallas_call | solution.py:708
  21.9 0.0 collective-permute-done.5.refs_1_
  21.9 0.6 %collective-permute-done.6.refs_2_ = f32[32,128]{1,0:T(8,128)S(1)} collective-permute-done((f32[32,128]{1,0:T(8,128)S(1)}, f32[32,128]{1,0:T(8,128)S(1)}, u32[]{:S(2)}, u32[]{:S(2)}) %collective-permute-start.6) | collective-permute-done | bytes 16416 | tf_op jit(solution)/shard_map/ppermute | solution.py:802
  22.5 0.0 collective-permute-done.7.refs_3_
  22.5 0.9 %shard_map.68 = (f32[320,128]{1,0:T(8,128)}, f32[3,4,128]{2,1,0:T(4,128)}) custom-call(f32[32,128]{1,0:T(8,128)S(1)} %add.3.refs_0_, f32[32,128]{1,0:T(8,128)S(1)} %collective-permute-done.5.refs_1_, f32[32,128]{1,0:T(8,128)S(1)} %collective-permute-done.6.refs_2_, f32[32,128]{1,0:T(8,128)S(1)} %collective-permute-done.7.refs_3_, ...), custom_call_target="tpu_custom_call" | custom-call | tf_op jit(solution)/shard_map/pallas_call | solution.py:818
  (1 shorter events, 0.0 us)
Async XLA Ops:
  1.6 6.6 %collective-permute-start = (f32[120,128]{1,0:T(8,128)S(1)}, f32[120,128]{1,0:T(8,128)S(1)}, u32[]{:S(2)}, u32[]{:S(2)}) collective-permute-start(f32[120,128]{1,0:T(8,128)S(1)} %get-tuple-element.31), channel_id=1, source_target_pairs={{0,7},{1,2},{2,1},{3,4},{4,3},{5,6},{6,5},{7,0},{8,15},{9,10},{10,... | collective-permute-start | bytes 184328 | tf_op jit(solution)/shard_map/ppermute | solution.py:721
  6.1 2.0 %collective-permute-start.1 = (f32[120,128]{1,0:T(8,128)S(1)}, f32[120,128]{1,0:T(8,128)S(1)}, u32[]{:S(2)}, u32[]{:S(2)}) collective-permute-start(f32[120,128]{1,0:T(8,128)S(1)} %get-tuple-element.32), channel_id=1, source_target_pairs={{0,1},{1,0},{2,3},{3,2},{4,5},{5,4},{6,7},{7,6},{8,9},{9,8},{10,11... | collective-permute-start | bytes 184328 | tf_op jit(solution)/shard_map/ppermute | solution.py:721
  8.4 5.3 %collective-permute-start.2 = (f32[24,128]{1,0:T(8,128)S(1)}, f32[24,128]{1,0:T(8,128)S(1)}, u32[]{:S(2)}, u32[]{:S(2)}) collective-permute-start(f32[24,128]{1,0:T(8,128)S(1)} %get-tuple-element.41), channel_id=1, source_target_pairs={{0,8},{8,16},{16,24},{24,0},{1,9},{9,17},{17,25},{25,1},{2,10},{10... | collective-permute-start | bytes 36872 | tf_op jit(solution)/shard_map/ppermute | solution.py:726
  10.7 3.7 %collective-permute-start.3 = (f32[24,128]{1,0:T(8,128)S(1)}, f32[24,128]{1,0:T(8,128)S(1)}, u32[]{:S(2)}, u32[]{:S(2)}) collective-permute-start(f32[24,128]{1,0:T(8,128)S(1)} %get-tuple-element.42), channel_id=1, source_target_pairs={{0,24},{8,0},{16,8},{24,16},{1,25},{9,1},{17,9},{25,17},{2,26},{10... | collective-permute-start | bytes 36872 | tf_op jit(solution)/shard_map/ppermute | solution.py:726
  15.2 1.2 %collective-permute-start.4 = (f32[32,128]{1,0:T(8,128)S(1)}, f32[32,128]{1,0:T(8,128)S(1)}, u32[]{:S(2)}, u32[]{:S(2)}) collective-permute-start(f32[32,128]{1,0:T(8,128)S(1)} %get-tuple-element.47), channel_id=1, source_target_pairs={{0,1},{1,0},{2,3},{3,2},{4,5},{5,4},{6,7},{7,6},{8,9},{9,8},{10,11... | collective-permute-start | bytes 49160 | tf_op jit(solution)/shard_map/ppermute | solution.py:802
  16.4 5.4 %collective-permute-start.5 = (f32[32,128]{1,0:T(8,128)S(1)}, f32[32,128]{1,0:T(8,128)S(1)}, u32[]{:S(2)}, u32[]{:S(2)}) collective-permute-start(f32[32,128]{1,0:T(8,128)S(1)} %add.3.refs_0_), channel_id=1, source_target_pairs={{0,4},{1,5},{2,6},{3,7},{4,0},{5,1},{6,2},{7,3},{8,12},{9,13},{10,... | collective-permute-start | bytes 49160 | tf_op jit(solution)/shard_map/ppermute | solution.py:802
  16.8 5.7 %collective-permute-start.6 = (f32[32,128]{1,0:T(8,128)S(1)}, f32[32,128]{1,0:T(8,128)S(1)}, u32[]{:S(2)}, u32[]{:S(2)}) collective-permute-start(f32[32,128]{1,0:T(8,128)S(1)} %add.3.refs_0_), channel_id=1, source_target_pairs={{0,6},{1,7},{2,4},{3,5},{4,2},{5,3},{6,0},{7,1},{8,14},{9,15},{10,... | collective-permute-start | bytes 49160 | tf_op jit(solution)/shard_map/ppermute | solution.py:802
  18.4 4.1 %collective-permute-start.7 = (f32[32,128]{1,0:T(8,128)S(1)}, f32[32,128]{1,0:T(8,128)S(1)}, u32[]{:S(2)}, u32[]{:S(2)}) collective-permute-start(f32[32,128]{1,0:T(8,128)S(1)} %add.3.refs_0_), channel_id=1, source_target_pairs={{0,2},{1,3},{2,0},{3,1},{4,6},{5,7},{6,4},{7,5},{8,10},{9,11},{10,... | collective-permute-start | bytes 49160 | tf_op jit(solution)/shard_map/ppermute | solution.py:802

commit v7 on v6

--- a/solution.py
+++ b/solution.py
@@ -129,7 +129,16 @@
             raw_ref[k + HALO + ROWS, field] = jnp.where(even, shift_s(own[k], -1), high)
 
 
-def own_corner_kernel(own_ref, corner_ref):
+def own_corner_kernel(own_ref, corner_ref, filter_ref):
+    shape = (LANES, LANES)
+    source, target = (lax.broadcasted_iota(jnp.int32, shape, d) for d in range(2))
+
+    def weight(a, b):
+        apart = jnp.abs(a - b)
+        return jnp.where(apart == 0, 2.0, jnp.where(apart == 1, 1.0, 0.0))
+
+    along_x = weight(source & (SPAN - 1), target & (SPAN - 1))
+    filter_ref[...] = along_x * weight(source >> 3, target >> 3)
     lane = lanes()
     within = lane & 63
     for field in range(NF):
@@ -476,10 +485,18 @@
     return jnp.where(bottom | top, 4.0, 2.0)
 
 
+def joined(top, bottom):
+    return jnp.where(
+        is_even(),
+        (top + shift_s(top, -1)) * (1.0 / 512.0),
+        (bottom + shift_s(bottom, 1)) * (1.0 / 1024.0),
+    )
+
+
 def model_kernel(
     own_ref, far_ref, near_ref, corner_own_ref,
-    sum_ref, clamped_ref, tile_ref, state_ref, raw_ref,
-    wide_ref, favre_ref,
+    main_ref, clamped_ref, tile_ref, state_ref, raw_ref,
+    wide_ref, favre_ref, sum_ref,
 ):
     scale = slope_scale()
     gather_rows(own_ref, far_ref, near_ref, raw_ref)
@@ -539,6 +556,8 @@
         return carry
 
     lax.fori_loop(0, ROWS, test_row, 0)
+    for k in range(3):
+        main_ref[k] = joined(sum_ref[2 * k], sum_ref[2 * k + 1])
 
     on_left = lanes() < 64
     place = lanes() & (SPAN - 1)
@@ -552,11 +571,10 @@
 
 
 def corner_kernel(
-    clamped_ref, got_left_ref, got_right_ref, sum_ref,
+    clamped_ref, got_left_ref, got_right_ref, main_ref, filter_ref,
     totals_ref, corner_ref, tile_ref, speed_ref
 ):
     lane = lanes()
-    even = is_even()
     scale = slope_scale()
     column = lax.axis_index("gx")
     first, last = column == 0, column == lax.axis_size("gx") - 1
@@ -580,36 +598,37 @@
         along_z = shift_x(value, -SPAN) - shift_x(value, SPAN)
         return along_x, level_slope(value, scale), along_z
 
-    def filtered(value):
-        pair = value + shift_x(value, -SPAN)
-        return filter_x(pair + shift_x(pair, SPAN))
+    weights = filter_ref[...].astype(jnp.bfloat16)
+
+    def filtered(values):
+        rest, parts = jnp.concatenate(values, axis=0), []
+        for _ in range(3):
+            parts.append(rest.astype(jnp.bfloat16))
+            rest = rest - parts[-1].astype(F32)
+        size = rest.shape[0]
+        result = jnp.dot(jnp.concatenate(parts, axis=0), weights, preferred_element_type=F32)
+        result = (result[:size] + result[size : 2 * size]) + result[2 * size :]
+        return [result[TILE * k : TILE * (k + 1)] for k in range(len(values))]
 
     tiles = grid_terms(lambda k: state[k], [slopes_of(state[SPEED + k]) for k in range(SLOPED - 1)])
     for k in range(STRESS, TILES):
         tile_ref[k] = tiles[k]
     for k in range(3):
         speed_ref[k] = state[SPEED + k]
-    wide = [filtered(state[k]) for k in range(SPEED)]
-    density, speed, thermal, fraction = favre(wide)
+    wide = filtered(state[:SPEED] + tiles[:FILTERED] + [state[0]])
+    hat = wide[SPEED:]
+    density, speed, thermal, fraction = favre(wide[:SPEED])
     sums = contractions(
-        lambda k: filtered(tiles[k]), density, wide[MOMENTUM : MOMENTUM + 3],
+        lambda k: hat[k], density, wide[MOMENTUM : MOMENTUM + 3],
         (speed, thermal, fraction), [slopes_of(value) for value in speed + [thermal] + fraction],
     )
-    main_totals, corner_totals = [sum_ref[k] for k in range(6)], []
-    for value in sums:
-        value = value + shift_x(value, -SPAN)
-        corner_totals.append(value + shift_x(value, -2 * SPAN))
     edges = jnp.zeros((TILE, LANES), F32)
     for k in range(3):
-        packed = []
-        for main, side in zip(main_totals[2 * k : 2 * k + 2], corner_totals[2 * k : 2 * k + 2]):
-            main = jnp.where(lane < 2, shift_x(side, -19), main)
-            main = jnp.where(lane >= LANES - 2, shift_x(side, 126 - 83), main)
-            packed.append((main + shift_s(main, 1), side + shift_s(side, 1), main, side))
-        top_main = shift_s(packed[0][0], -1) * (1.0 / 512.0)
-        top_side = shift_s(packed[0][1], -1) * (1.0 / 512.0)
-        totals_ref[pl.ds(k * TILE, TILE), :] = jnp.where(even, top_main, packed[1][0] * (1.0 / 1024.0))
-        side = jnp.where(even, top_side, packed[1][1] * (1.0 / 1024.0))
+        side = joined(sums[2 * k], sums[2 * k + 1])
+        side = side + shift_x(side, -SPAN)
+        side = side + shift_x(side, -2 * SPAN)
+        main = jnp.where(lane < 2, shift_x(side, -19), main_ref[k])
+        totals_ref[slot_of(k), :] = jnp.where(lane >= LANES - 2, shift_x(side, 126 - 83), main)
         edges = jnp.where(lane == 2 * k, shift_x(side, 2 * k - 18), edges)
         edges = jnp.where(lane == 2 * k + 1, shift_x(side, 2 * k + 1 - 85), edges)
     totals_ref[pl.ds(3 * TILE, TILE), :] = edges
@@ -756,7 +775,7 @@
     far = swap(False)(far)
     near = swap(True)(near)
     face, part = call(stream_kernel, [rows, rows], inputs=2)(own, blown)
-    (corner,) = call(own_corner_kernel, [fields], inputs=1)(own)
+    corner, weights = call(own_corner_kernel, [fields, (LANES, LANES)], inputs=1)(own)
     far, near, face, part, corner = lax.optimization_barrier((far, near, face, part, corner))
 
     corner, to_right, to_left = call(
@@ -769,21 +788,21 @@
     sums, clamped, tiles, state, raw = call(
         model_kernel,
         [
-            (6, TILE, LANES),
+            (3, TILE, LANES),
             fields,
             (GRID_ROWS, TILES, TILE, LANES),
             (STATE_ROWS, STATE_COUNT, TILE, LANES),
             (SPAN_TILES, NF, TILE, LANES),
         ],
-        scratch=[(GRID_ROWS, 4, TILE, LANES), (GRID_ROWS, 8, TILE, LANES)],
+        scratch=[(GRID_ROWS, 4, TILE, LANES), (GRID_ROWS, 8, TILE, LANES), (6, TILE, LANES)],
         inputs=4,
     )(own, far, near, corner)
     got_left, got_right, sums = lax.optimization_barrier((got_left, got_right, sums))
     totals, corner, corner_tiles, corner_speed = call(
         corner_kernel,
         [(4 * TILE, LANES), fields, (TILES, TILE, LANES), (3, TILE, LANES)],
-        inputs=4,
-    )(clamped, got_left, got_right, sums)
+        inputs=5,
+    )(clamped, got_left, got_right, sums, weights)
 
     (terms,) = call(term_kernel, [(ROWS, TERMS, 5, TILE, LANES)], inputs=4)(
         tiles, state, corner_tiles, corner_speed

time: 23.5 us -> 23.4 us (level)
  no operation moved by 1% of the time
where the time goes in v7:
time: 23.4 us; the launch traced here: 23.3 us
  starting transfers between devices  11.5 us (49%)
  Pallas kernels  8.06 us (34%)
  waiting for transfers between devices  3.02 us (13%)
  between operations  0.72 us (3%)
    pallas_call x8, Pallas kernels, call(): return lambda *args: run(*in_vmem(args))  6.26 us
    ppermute x2, starting transfers between devices, swap(): lax.ppermute(value, 'gz', [(i, (i + step[i % 2]) % count_z) for i in rang...  4.56 us
    ppermute x4, starting transfers between devices, crossed(): return lax.ppermute(value, 'gz', [(i, i ^ mask) for i in range(count_z)])  3.56 us
    ppermute x2, starting transfers between devices, ring(): lax.ppermute(value, 'gx', [(i, (i + step) % count_x) for i in range(count...  3.34 us
    ppermute x4, waiting for transfers between devices, crossed(): return lax.ppermute(value, 'gz', [(i, i ^ mask) for i in range(count_z)])  1.79 us
    pallas_call x1, Pallas kernels, body(): pl.pallas_call(pack_kernel, out_shape=[pltpu.VMEM(shape, F32) for shape i...  0.95 us
    pallas_call x1, Pallas kernels, body(): pl.pallas_call(final, out_shape=[jax.ShapeDtypeStruct(shape, F32) for sha...  0.85 us
    ppermute x2, waiting for transfers between devices, ring(): lax.ppermute(value, 'gx', [(i, (i + step) % count_x) for i in range(count...  0.7 us
  transfers between devices with their start and end apart: 8, of which 4 were waited for; matrix products, arithmetic and copies ran while one was open for 0% of the time, Pallas kernels for 23%

profile of v7, /device:TPU:0, one launch (start us, length us, event | category | flops | bytes accessed | tf_op | source)
XLA Modules:
  0.0 23.3 jit_solution(17614735634163500047)
XLA Ops:
  0.6 1.0 %shard_map.59 = (f32[320,128]{1,0:T(8,128)S(1)}, f32[120,128]{1,0:T(8,128)S(1)}, f32[120,128]{1,0:T(8,128)S(1)}, f32[32,128]{1,0:T(8,128)S(1)}) custom-call(f32[160,128]{1,0:T(8,128)} %bitcast.4, f32[96,128]{1,0:T(8,128)} %bitcast.5, f32[64,128]{1,0:T(8,128)} %bitcast.6, s32[8,128]{1,0:T(8,128)} %blow_hbm.1), custom_call_target="tpu_custom_call" | custom-call | tf_op jit(solution)/shard_map/pallas_call | solution.py:755
  1.6 4.6 %collective-permute-start = (f32[120,128]{1,0:T(8,128)S(1)}, f32[120,128]{1,0:T(8,128)S(1)}, u32[]{:S(2)}, u32[]{:S(2)}) collective-permute-start(f32[120,128]{1,0:T(8,128)S(1)} %get-tuple-element.33), channel_id=1, source_target_pairs={{0,7},{1,2},{2,1},{3,4},{4,3},{5,6},{6,5},{7,0},{8,15},{9,10},{10,... | collective-permute-start | bytes 184328 | tf_op jit(solution)/shard_map/ppermute | solution.py:740
  6.1 0.0 collective-permute-start.1
  6.1 0.2 %shard_map.61 = (f32[10,8,128]{2,1,0:T(8,128)S(1)}, f32[128,128]{1,0:T(8,128)S(1)}) custom-call(f32[320,128]{1,0:T(8,128)S(1)} %get-tuple-element.32.own_ref), custom_call_target="tpu_custom_call" | custom-call | tf_op jit(solution)/shard_map/pallas_call | solution.py:727
  6.4 1.2 %shard_map.60 = (f32[320,128]{1,0:T(8,128)S(1)}, f32[320,128]{1,0:T(8,128)S(1)}) custom-call(f32[320,128]{1,0:T(8,128)S(1)} %get-tuple-element.32.own_ref, f32[32,128]{1,0:T(8,128)S(1)} %get-tuple-element.35.blow_rows), custom_call_target="tpu_custom_call" | custom-call | tf_op jit(solution)/shard_map/pallas_call | solution.py:727
  7.6 0.5 %collective-permute-done.far_ref = f32[120,128]{1,0:T(8,128)S(1)} collective-permute-done((f32[120,128]{1,0:T(8,128)S(1)}, f32[120,128]{1,0:T(8,128)S(1)}, u32[]{:S(2)}, u32[]{:S(2)}) %collective-permute-start) | collective-permute-done | bytes 61472 | tf_op jit(solution)/shard_map/ppermute | solution.py:740
  8.2 0.0 collective-permute-done.1.near_ref
  8.2 0.2 shard_map.62
  8.4 2.3 %collective-permute-start.2 = (f32[24,128]{1,0:T(8,128)S(1)}, f32[24,128]{1,0:T(8,128)S(1)}, u32[]{:S(2)}, u32[]{:S(2)}) collective-permute-start(f32[24,128]{1,0:T(8,128)S(1)} %get-tuple-element.44), channel_id=1, source_target_pairs={{0,8},{8,16},{16,24},{24,0},{1,9},{9,17},{17,25},{25,1},{2,10},{10... | collective-permute-start | bytes 36872 | tf_op jit(solution)/shard_map/ppermute | solution.py:745
  10.7 1.0 %collective-permute-start.3 = (f32[24,128]{1,0:T(8,128)S(1)}, f32[24,128]{1,0:T(8,128)S(1)}, u32[]{:S(2)}, u32[]{:S(2)}) collective-permute-start(f32[24,128]{1,0:T(8,128)S(1)} %get-tuple-element.45), channel_id=1, source_target_pairs={{0,24},{8,0},{16,8},{24,16},{1,25},{9,1},{17,9},{25,17},{2,26},{10... | collective-permute-start | bytes 36872 | tf_op jit(solution)/shard_map/ppermute | solution.py:745
  11.7 2.0 %shard_map.63 = (f32[3,8,128]{2,1,0:T(8,128)S(1)}, f32[10,8,128]{2,1,0:T(8,128)S(1)}, f32[6,45,8,128]{3,2,1,0:T(8,128)S(1)}, f32[8,20,8,128]{3,2,1,0:T(8,128)S(1)}, f32[10,10,8,128]{3,2,1,0:T(8,128)S(1)}) custom-call(f32[320,128]{1,0:T(8,128)S(1)} %get-tuple-element.32.own_ref, f32[120,128]{1,0:T(8,128)S(1)} %collective-permute-done.far_ref, ...), custom_call_target="tpu_custom_call" | custom-call | tf_op jit(solution)/shard_map/pallas_call | solution.py:727
  13.7 0.0 collective-permute-done.2.got_left_ref
  13.7 0.7 %collective-permute-done.3.got_right_ref = f32[24,128]{1,0:T(8,128)S(1)} collective-permute-done((f32[24,128]{1,0:T(8,128)S(1)}, f32[24,128]{1,0:T(8,128)S(1)}, u32[]{:S(2)}, u32[]{:S(2)}) %collective-permute-start.3) | collective-permute-done | bytes 12320 | tf_op jit(solution)/shard_map/ppermute | solution.py:745
  14.4 0.7 %shard_map.64 = (f32[32,128]{1,0:T(8,128)S(1)}, f32[10,8,128]{2,1,0:T(8,128)S(1)}, f32[45,8,128]{2,1,0:T(8,128)S(1)}, f32[3,8,128]{2,1,0:T(8,128)S(1)}) custom-call(f32[10,8,128]{2,1,0:T(8,128)S(1)} %get-tuple-element.43.clamped_ref, f32[24,128]{1,0:T(8,128)S(1)} %collective-permute-done.2.got_left_ref, f32[24,128]{1,0:T(8,128)S(1)} %collective-permute-done.3.got_right_ref, ...), custom_call_target="tpu_custom_call" | custom-call | tf_op jit(solution)/shard_map/pallas_call | solution.py:727
  15.1 0.1 collective-permute-start.4
  15.2 1.2 %collective-permute-done.4 = f32[32,128]{1,0:T(8,128)S(1)} collective-permute-done((f32[32,128]{1,0:T(8,128)S(1)}, f32[32,128]{1,0:T(8,128)S(1)}, u32[]{:S(2)}, u32[]{:S(2)}) %collective-permute-start.4) | collective-permute-done | bytes 16416 | tf_op jit(solution)/shard_map/ppermute | solution.py:821
  16.3 0.4 %collective-permute-start.5 = (f32[32,128]{1,0:T(8,128)S(1)}, f32[32,128]{1,0:T(8,128)S(1)}, u32[]{:S(2)}, u32[]{:S(2)}) collective-permute-start(f32[32,128]{1,0:T(8,128)S(1)} %add.3.refs_0_), channel_id=1, source_target_pairs={{0,4},{1,5},{2,6},{3,7},{4,0},{5,1},{6,2},{7,3},{8,12},{9,13},{10,... | collective-permute-start | bytes 49160 | tf_op jit(solution)/shard_map/ppermute | solution.py:821
  16.8 1.5 %collective-permute-start.6 = (f32[32,128]{1,0:T(8,128)S(1)}, f32[32,128]{1,0:T(8,128)S(1)}, u32[]{:S(2)}, u32[]{:S(2)}) collective-permute-start(f32[32,128]{1,0:T(8,128)S(1)} %add.3.refs_0_), channel_id=1, source_target_pairs={{0,6},{1,7},{2,4},{3,5},{4,2},{5,3},{6,0},{7,1},{8,14},{9,15},{10,... | collective-permute-start | bytes 49160 | tf_op jit(solution)/shard_map/ppermute | solution.py:821
  18.3 1.6 %collective-permute-start.7 = (f32[32,128]{1,0:T(8,128)S(1)}, f32[32,128]{1,0:T(8,128)S(1)}, u32[]{:S(2)}, u32[]{:S(2)}) collective-permute-start(f32[32,128]{1,0:T(8,128)S(1)} %add.3.refs_0_), channel_id=1, source_target_pairs={{0,2},{1,3},{2,0},{3,1},{4,6},{5,7},{6,4},{7,5},{8,10},{9,11},{10,... | collective-permute-start | bytes 49160 | tf_op jit(solution)/shard_map/ppermute | solution.py:821
  19.8 0.5 %shard_map.65.part_ref = f32[320,128]{1,0:T(8,128)S(1)} custom-call(f32[10,8,128]{2,1,0:T(8,128)S(1)} %get-tuple-element.53.corner_ref, f32[320,128]{1,0:T(8,128)S(1)} %get-tuple-element.54.face_ref, f32[320,128]{1,0:T(8,128)S(1)} %get-tuple-element.55.part_ref), custom_call_target="tpu_custom_call" | custom-call | tf_op jit(solution)/shard_map/pallas_call | solution.py:727
  20.3 0.9 %shard_map.66.refs_4_ = f32[320,128]{1,0:T(8,128)S(1)} custom-call(f32[10,10,8,128]{3,2,1,0:T(8,128)S(1)} %get-tuple-element.52.raw_ref, f32[320,128]{1,0:T(8,128)S(1)} %shard_map.65.part_ref), custom_call_target="tpu_custom_call" | custom-call | tf_op jit(solution)/shard_map/pallas_call | solution.py:727
  21.3 0.5 %shard_map.67.refs_5_ = f32[4,12,5,8,128]{4,3,2,1,0:T(8,128)S(1)} custom-call(f32[6,45,8,128]{3,2,1,0:T(8,128)S(1)} %get-tuple-element.56.tile_ref, f32[8,20,8,128]{3,2,1,0:T(8,128)S(1)} %get-tuple-element.57.state_ref, f32[45,8,128]{2,1,0:T(8,128)S(1)} %get-tuple-element.58.corner_ref, f32[3,8,128]{2,1,0:T(8,128)S(1)} %get-tuple-element.59.corner_speed_ref), custom_call_target="tpu_custom_call" | custom-call | tf_op jit(solution)/shard_map/pallas_call | solution.py:727
  21.8 0.0 collective-permute-done.5.refs_1_
  21.8 0.6 %collective-permute-done.6.refs_2_ = f32[32,128]{1,0:T(8,128)S(1)} collective-permute-done((f32[32,128]{1,0:T(8,128)S(1)}, f32[32,128]{1,0:T(8,128)S(1)}, u32[]{:S(2)}, u32[]{:S(2)}) %collective-permute-start.6) | collective-permute-done | bytes 16416 | tf_op jit(solution)/shard_map/ppermute | solution.py:821
  22.4 0.0 collective-permute-done.7.refs_3_
  22.4 0.9 %shard_map.68 = (f32[320,128]{1,0:T(8,128)}, f32[3,4,128]{2,1,0:T(4,128)}) custom-call(f32[32,128]{1,0:T(8,128)S(1)} %add.3.refs_0_, f32[32,128]{1,0:T(8,128)S(1)} %collective-permute-done.5.refs_1_, f32[32,128]{1,0:T(8,128)S(1)} %collective-permute-done.6.refs_2_, f32[32,128]{1,0:T(8,128)S(1)} %collective-permute-done.7.refs_3_, ...), custom_call_target="tpu_custom_call" | custom-call | tf_op jit(solution)/shard_map/pallas_call | solution.py:837
  (1 shorter events, 0.0 us)
Async XLA Ops:
  1.6 6.6 %collective-permute-start = (f32[120,128]{1,0:T(8,128)S(1)}, f32[120,128]{1,0:T(8,128)S(1)}, u32[]{:S(2)}, u32[]{:S(2)}) collective-permute-start(f32[120,128]{1,0:T(8,128)S(1)} %get-tuple-element.33), channel_id=1, source_target_pairs={{0,7},{1,2},{2,1},{3,4},{4,3},{5,6},{6,5},{7,0},{8,15},{9,10},{10,... | collective-permute-start | bytes 184328 | tf_op jit(solution)/shard_map/ppermute | solution.py:740
  6.1 2.0 %collective-permute-start.1 = (f32[120,128]{1,0:T(8,128)S(1)}, f32[120,128]{1,0:T(8,128)S(1)}, u32[]{:S(2)}, u32[]{:S(2)}) collective-permute-start(f32[120,128]{1,0:T(8,128)S(1)} %get-tuple-element.34), channel_id=1, source_target_pairs={{0,1},{1,0},{2,3},{3,2},{4,5},{5,4},{6,7},{7,6},{8,9},{9,8},{10,11... | collective-permute-start | bytes 184328 | tf_op jit(solution)/shard_map/ppermute | solution.py:740
  8.4 5.3 %collective-permute-start.2 = (f32[24,128]{1,0:T(8,128)S(1)}, f32[24,128]{1,0:T(8,128)S(1)}, u32[]{:S(2)}, u32[]{:S(2)}) collective-permute-start(f32[24,128]{1,0:T(8,128)S(1)} %get-tuple-element.44), channel_id=1, source_target_pairs={{0,8},{8,16},{16,24},{24,0},{1,9},{9,17},{17,25},{25,1},{2,10},{10... | collective-permute-start | bytes 36872 | tf_op jit(solution)/shard_map/ppermute | solution.py:745
  10.7 3.7 %collective-permute-start.3 = (f32[24,128]{1,0:T(8,128)S(1)}, f32[24,128]{1,0:T(8,128)S(1)}, u32[]{:S(2)}, u32[]{:S(2)}) collective-permute-start(f32[24,128]{1,0:T(8,128)S(1)} %get-tuple-element.45), channel_id=1, source_target_pairs={{0,24},{8,0},{16,8},{24,16},{1,25},{9,1},{17,9},{25,17},{2,26},{10... | collective-permute-start | bytes 36872 | tf_op jit(solution)/shard_map/ppermute | solution.py:745
  15.1 1.2 %collective-permute-start.4 = (f32[32,128]{1,0:T(8,128)S(1)}, f32[32,128]{1,0:T(8,128)S(1)}, u32[]{:S(2)}, u32[]{:S(2)}) collective-permute-start(f32[32,128]{1,0:T(8,128)S(1)} %get-tuple-element.51), channel_id=1, source_target_pairs={{0,1},{1,0},{2,3},{3,2},{4,5},{5,4},{6,7},{7,6},{8,9},{9,8},{10,11... | collective-permute-start | bytes 49160 | tf_op jit(solution)/shard_map/ppermute | solution.py:821
  16.3 5.4 %collective-permute-start.5 = (f32[32,128]{1,0:T(8,128)S(1)}, f32[32,128]{1,0:T(8,128)S(1)}, u32[]{:S(2)}, u32[]{:S(2)}) collective-permute-start(f32[32,128]{1,0:T(8,128)S(1)} %add.3.refs_0_), channel_id=1, source_target_pairs={{0,4},{1,5},{2,6},{3,7},{4,0},{5,1},{6,2},{7,3},{8,12},{9,13},{10,... | collective-permute-start | bytes 49160 | tf_op jit(solution)/shard_map/ppermute | solution.py:821
  16.8 5.7 %collective-permute-start.6 = (f32[32,128]{1,0:T(8,128)S(1)}, f32[32,128]{1,0:T(8,128)S(1)}, u32[]{:S(2)}, u32[]{:S(2)}) collective-permute-start(f32[32,128]{1,0:T(8,128)S(1)} %add.3.refs_0_), channel_id=1, source_target_pairs={{0,6},{1,7},{2,4},{3,5},{4,2},{5,3},{6,0},{7,1},{8,14},{9,15},{10,... | collective-permute-start | bytes 49160 | tf_op jit(solution)/shard_map/ppermute | solution.py:821
  18.3 4.1 %collective-permute-start.7 = (f32[32,128]{1,0:T(8,128)S(1)}, f32[32,128]{1,0:T(8,128)S(1)}, u32[]{:S(2)}, u32[]{:S(2)}) collective-permute-start(f32[32,128]{1,0:T(8,128)S(1)} %add.3.refs_0_), channel_id=1, source_target_pairs={{0,2},{1,3},{2,0},{3,1},{4,6},{5,7},{6,4},{7,5},{8,10},{9,11},{10,... | collective-permute-start | bytes 49160 | tf_op jit(solution)/shard_map/ppermute | solution.py:821

commit v8 on v7

--- a/solution.py
+++ b/solution.py
@@ -92,12 +92,13 @@
     copies.append(pltpu.make_async_copy(blow_hbm, blow_ref, arrived.at[3]))
     for copy in copies:
         copy.start()
-    for copy in copies:
-        copy.wait()
+    first_fields = (0, NSP, NSP + 3)
     even = is_even()
     first_core = is_first_of_pair("gz")
     tiles = {}
     for field in range(NF):
+        if field in first_fields:
+            copies[first_fields.index(field)].wait()
         for zz in range(ROWS):
             tile = given_ref[pl.ds(field * 32 + zz, TILE, stride=4), :]
             tiles[field, zz] = tile
@@ -109,6 +110,7 @@
                 slot = slot_of(field // 2 * HALO + k)
                 far_ref[slot, :] = jnp.where(first_core, down, up)
                 near_ref[slot, :] = jnp.where(first_core, up, down)
+    copies[3].wait()
     for level in range(4):
         blow_rows[pl.ds(level * TILE, TILE), :] = blow_ref[...].astype(F32)
 

time: 23.4 us -> 23.4 us (level)
  no operation moved by 1% of the time
where the time goes in v8:
time: 23.4 us; the launch traced here: 23.3 us
  starting transfers between devices  11.5 us (49%)
  Pallas kernels  8.06 us (34%)
  waiting for transfers between devices  3.02 us (13%)
  between operations  0.72 us (3%)
    pallas_call x8, Pallas kernels, call(): return lambda *args: run(*in_vmem(args))  6.26 us
    ppermute x2, starting transfers between devices, swap(): lax.ppermute(value, 'gz', [(i, (i + step[i % 2]) % count_z) for i in rang...  4.56 us
    ppermute x4, starting transfers between devices, crossed(): return lax.ppermute(value, 'gz', [(i, i ^ mask) for i in range(count_z)])  3.56 us
    ppermute x2, starting transfers between devices, ring(): lax.ppermute(value, 'gx', [(i, (i + step) % count_x) for i in range(count...  3.34 us
    ppermute x4, waiting for transfers between devices, crossed(): return lax.ppermute(value, 'gz', [(i, i ^ mask) for i in range(count_z)])  1.79 us
    pallas_call x1, Pallas kernels, body(): pl.pallas_call(pack_kernel, out_shape=[pltpu.VMEM(shape, F32) for shape i...  0.95 us
    pallas_call x1, Pallas kernels, body(): pl.pallas_call(final, out_shape=[jax.ShapeDtypeStruct(shape, F32) for sha...  0.85 us
    ppermute x2, waiting for transfers between devices, ring(): lax.ppermute(value, 'gx', [(i, (i + step) % count_x) for i in range(count...  0.7 us
  transfers between devices with their start and end apart: 8, of which 4 were waited for; matrix products, arithmetic and copies ran while one was open for 0% of the time, Pallas kernels for 23%

profile of v8, /device:TPU:0, one launch (start us, length us, event | category | flops | bytes accessed | tf_op | source)
XLA Modules:
  0.0 23.3 jit_solution(2608767379919612400)
XLA Ops:
  0.6 1.0 %shard_map.59 = (f32[320,128]{1,0:T(8,128)S(1)}, f32[120,128]{1,0:T(8,128)S(1)}, f32[120,128]{1,0:T(8,128)S(1)}, f32[32,128]{1,0:T(8,128)S(1)}) custom-call(f32[160,128]{1,0:T(8,128)} %bitcast.4, f32[96,128]{1,0:T(8,128)} %bitcast.5, f32[64,128]{1,0:T(8,128)} %bitcast.6, s32[8,128]{1,0:T(8,128)} %blow_hbm.1), custom_call_target="tpu_custom_call" | custom-call | tf_op jit(solution)/shard_map/pallas_call | solution.py:757
  1.6 4.6 %collective-permute-start = (f32[120,128]{1,0:T(8,128)S(1)}, f32[120,128]{1,0:T(8,128)S(1)}, u32[]{:S(2)}, u32[]{:S(2)}) collective-permute-start(f32[120,128]{1,0:T(8,128)S(1)} %get-tuple-element.33), channel_id=1, source_target_pairs={{0,7},{1,2},{2,1},{3,4},{4,3},{5,6},{6,5},{7,0},{8,15},{9,10},{10,... | collective-permute-start | bytes 184328 | tf_op jit(solution)/shard_map/ppermute | solution.py:742
  6.1 0.0 collective-permute-start.1
  6.1 0.2 %shard_map.61 = (f32[10,8,128]{2,1,0:T(8,128)S(1)}, f32[128,128]{1,0:T(8,128)S(1)}) custom-call(f32[320,128]{1,0:T(8,128)S(1)} %get-tuple-element.32.own_ref), custom_call_target="tpu_custom_call" | custom-call | tf_op jit(solution)/shard_map/pallas_call | solution.py:729
  6.4 1.2 %shard_map.60 = (f32[320,128]{1,0:T(8,128)S(1)}, f32[320,128]{1,0:T(8,128)S(1)}) custom-call(f32[320,128]{1,0:T(8,128)S(1)} %get-tuple-element.32.own_ref, f32[32,128]{1,0:T(8,128)S(1)} %get-tuple-element.35.blow_rows), custom_call_target="tpu_custom_call" | custom-call | tf_op jit(solution)/shard_map/pallas_call | solution.py:729
  7.6 0.5 %collective-permute-done.far_ref = f32[120,128]{1,0:T(8,128)S(1)} collective-permute-done((f32[120,128]{1,0:T(8,128)S(1)}, f32[120,128]{1,0:T(8,128)S(1)}, u32[]{:S(2)}, u32[]{:S(2)}) %collective-permute-start) | collective-permute-done | bytes 61472 | tf_op jit(solution)/shard_map/ppermute | solution.py:742
  8.2 0.0 collective-permute-done.1.near_ref
  8.2 0.2 shard_map.62
  8.4 2.3 %collective-permute-start.2 = (f32[24,128]{1,0:T(8,128)S(1)}, f32[24,128]{1,0:T(8,128)S(1)}, u32[]{:S(2)}, u32[]{:S(2)}) collective-permute-start(f32[24,128]{1,0:T(8,128)S(1)} %get-tuple-element.44), channel_id=1, source_target_pairs={{0,8},{8,16},{16,24},{24,0},{1,9},{9,17},{17,25},{25,1},{2,10},{10... | collective-permute-start | bytes 36872 | tf_op jit(solution)/shard_map/ppermute | solution.py:747
  10.7 1.0 %collective-permute-start.3 = (f32[24,128]{1,0:T(8,128)S(1)}, f32[24,128]{1,0:T(8,128)S(1)}, u32[]{:S(2)}, u32[]{:S(2)}) collective-permute-start(f32[24,128]{1,0:T(8,128)S(1)} %get-tuple-element.45), channel_id=1, source_target_pairs={{0,24},{8,0},{16,8},{24,16},{1,25},{9,1},{17,9},{25,17},{2,26},{10... | collective-permute-start | bytes 36872 | tf_op jit(solution)/shard_map/ppermute | solution.py:747
  11.7 2.0 %shard_map.63 = (f32[3,8,128]{2,1,0:T(8,128)S(1)}, f32[10,8,128]{2,1,0:T(8,128)S(1)}, f32[6,45,8,128]{3,2,1,0:T(8,128)S(1)}, f32[8,20,8,128]{3,2,1,0:T(8,128)S(1)}, f32[10,10,8,128]{3,2,1,0:T(8,128)S(1)}) custom-call(f32[320,128]{1,0:T(8,128)S(1)} %get-tuple-element.32.own_ref, f32[120,128]{1,0:T(8,128)S(1)} %collective-permute-done.far_ref, ...), custom_call_target="tpu_custom_call" | custom-call | tf_op jit(solution)/shard_map/pallas_call | solution.py:729
  13.7 0.0 collective-permute-done.2.got_left_ref
  13.7 0.7 %collective-permute-done.3.got_right_ref = f32[24,128]{1,0:T(8,128)S(1)} collective-permute-done((f32[24,128]{1,0:T(8,128)S(1)}, f32[24,128]{1,0:T(8,128)S(1)}, u32[]{:S(2)}, u32[]{:S(2)}) %collective-permute-start.3) | collective-permute-done | bytes 12320 | tf_op jit(solution)/shard_map/ppermute | solution.py:747
  14.4 0.7 %shard_map.64 = (f32[32,128]{1,0:T(8,128)S(1)}, f32[10,8,128]{2,1,0:T(8,128)S(1)}, f32[45,8,128]{2,1,0:T(8,128)S(1)}, f32[3,8,128]{2,1,0:T(8,128)S(1)}) custom-call(f32[10,8,128]{2,1,0:T(8,128)S(1)} %get-tuple-element.43.clamped_ref, f32[24,128]{1,0:T(8,128)S(1)} %collective-permute-done.2.got_left_ref, f32[24,128]{1,0:T(8,128)S(1)} %collective-permute-done.3.got_right_ref, ...), custom_call_target="tpu_custom_call" | custom-call | tf_op jit(solution)/shard_map/pallas_call | solution.py:729
  15.1 0.1 collective-permute-start.4
  15.2 1.2 %collective-permute-done.4 = f32[32,128]{1,0:T(8,128)S(1)} collective-permute-done((f32[32,128]{1,0:T(8,128)S(1)}, f32[32,128]{1,0:T(8,128)S(1)}, u32[]{:S(2)}, u32[]{:S(2)}) %collective-permute-start.4) | collective-permute-done | bytes 16416 | tf_op jit(solution)/shard_map/ppermute | solution.py:823
  16.3 0.4 %collective-permute-start.5 = (f32[32,128]{1,0:T(8,128)S(1)}, f32[32,128]{1,0:T(8,128)S(1)}, u32[]{:S(2)}, u32[]{:S(2)}) collective-permute-start(f32[32,128]{1,0:T(8,128)S(1)} %add.3.refs_0_), channel_id=1, source_target_pairs={{0,4},{1,5},{2,6},{3,7},{4,0},{5,1},{6,2},{7,3},{8,12},{9,13},{10,... | collective-permute-start | bytes 49160 | tf_op jit(solution)/shard_map/ppermute | solution.py:823
  16.8 1.5 %collective-permute-start.6 = (f32[32,128]{1,0:T(8,128)S(1)}, f32[32,128]{1,0:T(8,128)S(1)}, u32[]{:S(2)}, u32[]{:S(2)}) collective-permute-start(f32[32,128]{1,0:T(8,128)S(1)} %add.3.refs_0_), channel_id=1, source_target_pairs={{0,6},{1,7},{2,4},{3,5},{4,2},{5,3},{6,0},{7,1},{8,14},{9,15},{10,... | collective-permute-start | bytes 49160 | tf_op jit(solution)/shard_map/ppermute | solution.py:823
  18.3 1.6 %collective-permute-start.7 = (f32[32,128]{1,0:T(8,128)S(1)}, f32[32,128]{1,0:T(8,128)S(1)}, u32[]{:S(2)}, u32[]{:S(2)}) collective-permute-start(f32[32,128]{1,0:T(8,128)S(1)} %add.3.refs_0_), channel_id=1, source_target_pairs={{0,2},{1,3},{2,0},{3,1},{4,6},{5,7},{6,4},{7,5},{8,10},{9,11},{10,... | collective-permute-start | bytes 49160 | tf_op jit(solution)/shard_map/ppermute | solution.py:823
  19.8 0.5 %shard_map.65.part_ref = f32[320,128]{1,0:T(8,128)S(1)} custom-call(f32[10,8,128]{2,1,0:T(8,128)S(1)} %get-tuple-element.53.corner_ref, f32[320,128]{1,0:T(8,128)S(1)} %get-tuple-element.54.face_ref, f32[320,128]{1,0:T(8,128)S(1)} %get-tuple-element.55.part_ref), custom_call_target="tpu_custom_call" | custom-call | tf_op jit(solution)/shard_map/pallas_call | solution.py:729
  20.3 0.9 %shard_map.66.refs_4_ = f32[320,128]{1,0:T(8,128)S(1)} custom-call(f32[10,10,8,128]{3,2,1,0:T(8,128)S(1)} %get-tuple-element.52.raw_ref, f32[320,128]{1,0:T(8,128)S(1)} %shard_map.65.part_ref), custom_call_target="tpu_custom_call" | custom-call | tf_op jit(solution)/shard_map/pallas_call | solution.py:729
  21.3 0.5 %shard_map.67.refs_5_ = f32[4,12,5,8,128]{4,3,2,1,0:T(8,128)S(1)} custom-call(f32[6,45,8,128]{3,2,1,0:T(8,128)S(1)} %get-tuple-element.56.tile_ref, f32[8,20,8,128]{3,2,1,0:T(8,128)S(1)} %get-tuple-element.57.state_ref, f32[45,8,128]{2,1,0:T(8,128)S(1)} %get-tuple-element.58.corner_ref, f32[3,8,128]{2,1,0:T(8,128)S(1)} %get-tuple-element.59.corner_speed_ref), custom_call_target="tpu_custom_call" | custom-call | tf_op jit(solution)/shard_map/pallas_call | solution.py:729
  21.8 0.0 collective-permute-done.5.refs_1_
  21.8 0.6 %collective-permute-done.6.refs_2_ = f32[32,128]{1,0:T(8,128)S(1)} collective-permute-done((f32[32,128]{1,0:T(8,128)S(1)}, f32[32,128]{1,0:T(8,128)S(1)}, u32[]{:S(2)}, u32[]{:S(2)}) %collective-permute-start.6) | collective-permute-done | bytes 16416 | tf_op jit(solution)/shard_map/ppermute | solution.py:823
  22.4 0.0 collective-permute-done.7.refs_3_
  22.4 0.9 %shard_map.68 = (f32[320,128]{1,0:T(8,128)}, f32[3,4,128]{2,1,0:T(4,128)}) custom-call(f32[32,128]{1,0:T(8,128)S(1)} %add.3.refs_0_, f32[32,128]{1,0:T(8,128)S(1)} %collective-permute-done.5.refs_1_, f32[32,128]{1,0:T(8,128)S(1)} %collective-permute-done.6.refs_2_, f32[32,128]{1,0:T(8,128)S(1)} %collective-permute-done.7.refs_3_, ...), custom_call_target="tpu_custom_call" | custom-call | tf_op jit(solution)/shard_map/pallas_call | solution.py:839
  (1 shorter events, 0.0 us)
Async XLA Ops:
  1.6 6.6 %collective-permute-start = (f32[120,128]{1,0:T(8,128)S(1)}, f32[120,128]{1,0:T(8,128)S(1)}, u32[]{:S(2)}, u32[]{:S(2)}) collective-permute-start(f32[120,128]{1,0:T(8,128)S(1)} %get-tuple-element.33), channel_id=1, source_target_pairs={{0,7},{1,2},{2,1},{3,4},{4,3},{5,6},{6,5},{7,0},{8,15},{9,10},{10,... | collective-permute-start | bytes 184328 | tf_op jit(solution)/shard_map/ppermute | solution.py:742
  6.1 2.0 %collective-permute-start.1 = (f32[120,128]{1,0:T(8,128)S(1)}, f32[120,128]{1,0:T(8,128)S(1)}, u32[]{:S(2)}, u32[]{:S(2)}) collective-permute-start(f32[120,128]{1,0:T(8,128)S(1)} %get-tuple-element.34), channel_id=1, source_target_pairs={{0,1},{1,0},{2,3},{3,2},{4,5},{5,4},{6,7},{7,6},{8,9},{9,8},{10,11... | collective-permute-start | bytes 184328 | tf_op jit(solution)/shard_map/ppermute | solution.py:742
  8.4 5.3 %collective-permute-start.2 = (f32[24,128]{1,0:T(8,128)S(1)}, f32[24,128]{1,0:T(8,128)S(1)}, u32[]{:S(2)}, u32[]{:S(2)}) collective-permute-start(f32[24,128]{1,0:T(8,128)S(1)} %get-tuple-element.44), channel_id=1, source_target_pairs={{0,8},{8,16},{16,24},{24,0},{1,9},{9,17},{17,25},{25,1},{2,10},{10... | collective-permute-start | bytes 36872 | tf_op jit(solution)/shard_map/ppermute | solution.py:747
  10.7 3.7 %collective-permute-start.3 = (f32[24,128]{1,0:T(8,128)S(1)}, f32[24,128]{1,0:T(8,128)S(1)}, u32[]{:S(2)}, u32[]{:S(2)}) collective-permute-start(f32[24,128]{1,0:T(8,128)S(1)} %get-tuple-element.45), channel_id=1, source_target_pairs={{0,24},{8,0},{16,8},{24,16},{1,25},{9,1},{17,9},{25,17},{2,26},{10... | collective-permute-start | bytes 36872 | tf_op jit(solution)/shard_map/ppermute | solution.py:747
  15.1 1.2 %collective-permute-start.4 = (f32[32,128]{1,0:T(8,128)S(1)}, f32[32,128]{1,0:T(8,128)S(1)}, u32[]{:S(2)}, u32[]{:S(2)}) collective-permute-start(f32[32,128]{1,0:T(8,128)S(1)} %get-tuple-element.51), channel_id=1, source_target_pairs={{0,1},{1,0},{2,3},{3,2},{4,5},{5,4},{6,7},{7,6},{8,9},{9,8},{10,11... | collective-permute-start | bytes 49160 | tf_op jit(solution)/shard_map/ppermute | solution.py:823
  16.3 5.4 %collective-permute-start.5 = (f32[32,128]{1,0:T(8,128)S(1)}, f32[32,128]{1,0:T(8,128)S(1)}, u32[]{:S(2)}, u32[]{:S(2)}) collective-permute-start(f32[32,128]{1,0:T(8,128)S(1)} %add.3.refs_0_), channel_id=1, source_target_pairs={{0,4},{1,5},{2,6},{3,7},{4,0},{5,1},{6,2},{7,3},{8,12},{9,13},{10,... | collective-permute-start | bytes 49160 | tf_op jit(solution)/shard_map/ppermute | solution.py:823
  16.8 5.7 %collective-permute-start.6 = (f32[32,128]{1,0:T(8,128)S(1)}, f32[32,128]{1,0:T(8,128)S(1)}, u32[]{:S(2)}, u32[]{:S(2)}) collective-permute-start(f32[32,128]{1,0:T(8,128)S(1)} %add.3.refs_0_), channel_id=1, source_target_pairs={{0,6},{1,7},{2,4},{3,5},{4,2},{5,3},{6,0},{7,1},{8,14},{9,15},{10,... | collective-permute-start | bytes 49160 | tf_op jit(solution)/shard_map/ppermute | solution.py:823
  18.3 4.1 %collective-permute-start.7 = (f32[32,128]{1,0:T(8,128)S(1)}, f32[32,128]{1,0:T(8,128)S(1)}, u32[]{:S(2)}, u32[]{:S(2)}) collective-permute-start(f32[32,128]{1,0:T(8,128)S(1)} %add.3.refs_0_), channel_id=1, source_target_pairs={{0,2},{1,3},{2,0},{3,1},{4,6},{5,7},{6,4},{7,5},{8,10},{9,11},{10,... | collective-permute-start | bytes 49160 | tf_op jit(solution)/shard_map/ppermute | solution.py:823
